TPU v7x, 32 devices: a whole 2x2x4 slice. The times are simulated.
32 devices in a mesh: dp: 8 (over z, x), sub: 4 (over y, core).
Axes of the slice: x: 2, y: 2, z: 4, core: 2. Of those that a mesh axis runs over, the one named last changes fastest.
Arguments:
- big_maps: bfloat16 [256, 2, 7, 7, 2048], P(('dp', 'sub')), may hold values from -6 to 6
- small_maps: bfloat16 [256, 6, 3, 3, 2048], P(('dp', 'sub')), may hold values from -6 to 6
- live_counts: int32 [32], P(('dp', 'sub')), may hold values from 1 to 8, as said below
- queue: bfloat16 [2, 30720, 128], P(None, ('dp', 'sub')), may hold values from -0.5 to 0.5
- bottleneck_outer: float32 [2, 2048, 512], P(None, 'dp'), may hold values from -6 to 6
- bottleneck_inner: float32 [9, 512, 512], P(None, 'dp'), may hold values from -6 to 6
- proj_hidden: float32 [2048, 2048], P('dp'), may hold values from -6 to 6
- proj_out: float32 [2048, 128], P('dp'), may hold values from -6 to 6
- prototypes: float32 [3000, 128], replicated, may hold values from -6 to 6
- norm_params: float32 [2, 5120], replicated, may hold values from 0.1 to 1.9
- mom_outer: float32 [2, 2048, 512], P(None, 'dp'), may hold values from -6 to 6
- mom_inner: float32 [9, 512, 512], P(None, 'dp'), may hold values from -6 to 6
- mom_hidden: float32 [2048, 2048], P('dp'), may hold values from -6 to 6
- mom_out: float32 [2048, 128], P('dp'), may hold values from -6 to 6
- mom_protos: float32 [3000, 128], replicated, may hold values from -6 to 6
- mom_norms: float32 [2, 5120], replicated, may hold values from -6 to 6
- avg_outer: float32 [2, 2048, 512], P(None, 'dp'), may hold values from -6 to 6
- avg_inner: float32 [9, 512, 512], P(None, 'dp'), may hold values from -6 to 6
- avg_hidden: float32 [2048, 2048], P('dp'), may hold values from -6 to 6
- avg_out: float32 [2048, 128], P('dp'), may hold values from -6 to 6
- avg_protos: float32 [3000, 128], replicated, may hold values from -6 to 6
- avg_norms: float32 [2, 5120], replicated, may hold values from 0.1 to 1.9
Outputs:
- loss_sum: float32 [], replicated
- live_total: float32 [], replicated
- new_outer: float32 [2, 2048, 512], P(None, 'dp')
- new_inner: float32 [9, 512, 512], P(None, 'dp')
- new_hidden: float32 [2048, 2048], P('dp')
- new_out: float32 [2048, 128], P('dp')
- new_protos: float32 [3000, 128], replicated
- new_norms: float32 [2, 5120], replicated
- next_mom_outer: float32 [2, 2048, 512], P(None, 'dp')
- next_mom_inner: float32 [9, 512, 512], P(None, 'dp')
- next_mom_hidden: float32 [2048, 2048], P('dp')
- next_mom_out: float32 [2048, 128], P('dp')
- next_mom_protos: float32 [3000, 128], replicated
- next_mom_norms: float32 [2, 5120], replicated
- next_avg_outer: float32 [2, 2048, 512], P(None, 'dp')
- next_avg_inner: float32 [9, 512, 512], P(None, 'dp')
- next_avg_hidden: float32 [2048, 2048], P('dp')
- next_avg_out: float32 [2048, 128], P('dp')
- next_avg_protos: float32 [3000, 128], replicated
- next_avg_norms: float32 [2, 5120], replicated
- copy_outer: bfloat16 [2, 2048, 512], P(None, 'dp')
- copy_inner: bfloat16 [9, 512, 512], P(None, 'dp')
- copy_hidden: bfloat16 [2048, 2048], P('dp')
- copy_out: bfloat16 [2048, 128], P('dp')
Inputs may be any that keep to these rules, and one draw needn't show every extreme that they name: live_counts[d] is the number of live images on device d, which are its first slots; the last device has exactly 8.
All inputs are finite; a program needn't handle non-finite values.
Results may differ from a plain program's by a relative error of at most 0.02.
Values may be sent and summed in bfloat16 or wider, within the bound.
A program may use at most 448 MiB of HBM per device.

v0:
```python
import jax
import jax.numpy as jnp
from jax import lax
from jax.sharding import PartitionSpec as P

NBIG = 2
NSMALL = 6
BIG = 7
SMALL = 3
TAPS = 9
ITERS = 3


sink_temp = 0.05
softmax_temp = 0.1
norm_eps = 1e-05
unit_eps = 1e-12
trust_rate = 0.5
learn_rate = 1.0
momentum_rate = 0.5
average_rate = 0.5


def patches(active, crop_count, extent):
    spatial = active.reshape(crop_count, extent, extent, active.shape[-1])
    padded = jnp.pad(spatial, ((0, 0), (1, 1), (1, 1), (0, 0)))
    pieces = [
        padded[:, row_off : row_off + extent, col_off : col_off + extent, :]
        for row_off in range(3)
        for col_off in range(3)
    ]
    return jnp.concatenate(pieces, axis=-1).reshape(crop_count * extent * extent, -1)


def silu_slope(values):
    sigma = jax.nn.sigmoid(values)
    return sigma * (1.0 + values * (1.0 - sigma))


def cross_rows(left, right):
    return lax.dot_general(
        left, right, (((0,), (0,)), ((), ())), preferred_element_type=jnp.float32
    )


def against(left, right):
    return lax.dot_general(
        left, right, (((1,), (1,)), ((), ())), preferred_element_type=jnp.float32
    )


def forward_dot(left, right):
    return jnp.dot(left, right, preferred_element_type=jnp.float32)


def unit_rows(values):
    return values * lax.rsqrt(jnp.sum(values * values, 1, keepdims=True) + unit_eps)


def moments(values, row_mask, live_here, per_image):
    col_total, col_square, live_group = lax.psum(
        (
            jnp.sum(values * row_mask[:, None], 0),
            jnp.sum(values * values * row_mask[:, None], 0),
            live_here,
        ),
        "sub",
    )
    count_all = live_group * per_image
    row_mean = col_total / count_all
    inv_std = lax.rsqrt(col_square / count_all - row_mean * row_mean + norm_eps)
    return (row_mean, inv_std, count_all)


def norm_apply(values, row_mask, live_here, per_image, gain_vec, bias_vec, kept):
    if kept is None:
        kept = moments(values, row_mask, live_here, per_image)
    row_mean, inv_std, count_all = kept
    normal = (values - row_mean) * inv_std
    return (normal, gain_vec * normal + bias_vec, kept)


def norm_back(grad_out, normal, kept, gain_vec, row_mask):
    row_mean, inv_std, count_all = kept
    bias_local = jnp.sum(grad_out, 0)
    gain_local = jnp.sum(grad_out * normal, 0)
    bias_group, gain_group = lax.psum((bias_local, gain_local), "sub")
    grad_in = (
        gain_vec
        * inv_std
        * (grad_out - row_mask[:, None] * (bias_group + normal * gain_group) / count_all)
    )
    return (grad_in, gain_local, bias_local)


def trunk_pass(
    inputs, row_mask, live_here, images, first_w, middle_w, last_w, gains, biases, stored
):
    big_rows = images * NBIG * BIG * BIG
    per_image = NBIG * BIG * BIG + NSMALL * SMALL * SMALL
    hidden_one = forward_dot(inputs, first_w)
    normal_one, pre_one, stat_one = norm_apply(
        hidden_one, row_mask, live_here, per_image, gains[0], biases[0], stored[0]
    )
    act_one = jax.nn.silu(pre_one).astype(jnp.bfloat16)
    columns = jnp.concatenate(
        [
            patches(act_one[:big_rows], images * NBIG, BIG),
            patches(act_one[big_rows:], images * NSMALL, SMALL),
        ],
        0,
    )
    hidden_two = forward_dot(columns, middle_w)
    normal_two, pre_two, stat_two = norm_apply(
        hidden_two, row_mask, live_here, per_image, gains[1], biases[1], stored[1]
    )
    act_two = jax.nn.silu(pre_two).astype(jnp.bfloat16)
    hidden_three = against(act_two, last_w)
    normal_three, pre_three, stat_three = norm_apply(
        hidden_three, row_mask, live_here, per_image, gains[2], biases[2], stored[2]
    )
    summed = pre_three + inputs.astype(jnp.float32)
    return (
        (normal_one, pre_one, columns, normal_two, pre_two, act_two, normal_three, summed),
        (stat_one, stat_two, stat_three),
    )


def pool_crops(output, images):
    big_rows = images * NBIG * BIG * BIG
    channels = output.shape[-1]
    big_part = jnp.mean(output[:big_rows].reshape(images, NBIG, BIG * BIG, channels), 2)
    small_part = jnp.mean(output[big_rows:].reshape(images, NSMALL, SMALL * SMALL, channels), 2)
    return jnp.concatenate([big_part, small_part], 1).reshape(images * (NBIG + NSMALL), channels)


def advance(weight, gradient, moment, average, trust):
    step_now = trust * gradient
    moment_new = momentum_rate * moment + step_now
    weight_new = weight - learn_rate * (step_now + momentum_rate * moment_new)
    average_new = average_rate * average + (1.0 - average_rate) * weight_new
    return (weight_new, moment_new, average_new)


def per_device(
    big_maps,
    small_maps,
    live_counts,
    queue,
    bottleneck_outer,
    bottleneck_inner,
    proj_hidden,
    proj_out,
    prototypes,
    norm_params,
    mom_outer,
    mom_inner,
    mom_hidden,
    mom_out,
    mom_protos,
    mom_norms,
    avg_outer,
    avg_inner,
    avg_hidden,
    avg_out,
    avg_protos,
    avg_norms,
):
    images = big_maps.shape[0]
    channels = big_maps.shape[-1]
    middle = bottleneck_inner.shape[-1]
    hidden_width = proj_hidden.shape[1]
    proto_count = prototypes.shape[0]
    outer_low, inner_low, hidden_low, out_low = (
        lax.all_gather(bottleneck_outer.astype(jnp.bfloat16), "dp", axis=1, tiled=True),
        lax.all_gather(bottleneck_inner.astype(jnp.bfloat16), "dp", axis=1, tiled=True),
        lax.all_gather(proj_hidden.astype(jnp.bfloat16), "dp", axis=0, tiled=True),
        lax.all_gather(proj_out.astype(jnp.bfloat16), "dp", axis=0, tiled=True),
    )
    first_w = outer_low[0]
    last_w = outer_low[1]
    middle_w = inner_low.reshape(-1, middle)
    bounds = [0, middle, 2 * middle, 2 * middle + channels, 2 * middle + channels + hidden_width]
    gains = [norm_params[0, bounds[layer_idx] : bounds[layer_idx + 1]] for layer_idx in range(4)]
    biases = [norm_params[1, bounds[layer_idx] : bounds[layer_idx + 1]] for layer_idx in range(4)]
    live_here = live_counts[0]
    live_float = live_here.astype(jnp.float32)
    image_mask = (jnp.arange(images) < live_here).astype(jnp.float32)
    big_rows = images * NBIG * BIG * BIG
    small_rows = images * NSMALL * SMALL * SMALL
    inputs = jnp.concatenate([big_maps.reshape(-1, channels), small_maps.reshape(-1, channels)], 0)
    row_image = jnp.concatenate(
        [
            jnp.arange(big_rows) // (NBIG * BIG * BIG),
            jnp.arange(small_rows) // (NSMALL * SMALL * SMALL),
        ]
    )
    row_mask = (row_image < live_here).astype(jnp.float32)
    crop_mask = jnp.repeat(image_mask, NBIG + NSMALL)
    kept_acts, stats = trunk_pass(
        inputs,
        row_mask,
        live_float,
        images,
        first_w,
        middle_w,
        last_w,
        gains,
        biases,
        [None, None, None],
    )
    pooled_low = pool_crops(jax.nn.silu(kept_acts[7]), images).astype(jnp.bfloat16)
    proj_pre = forward_dot(pooled_low, hidden_low)
    normal_four, pre_four, stat_four = norm_apply(
        proj_pre, crop_mask, live_float, NBIG + NSMALL, gains[3], biases[3], None
    )
    act_four_low = jax.nn.silu(pre_four).astype(jnp.bfloat16)
    embedding = forward_dot(act_four_low, out_low)
    unit_embed, embed_back = jax.vjp(unit_rows, embedding)
    unit_low = unit_embed.astype(jnp.bfloat16)
    centers, center_back = jax.vjp(unit_rows, prototypes)
    centers_low = centers.astype(jnp.bfloat16)
    scores = against(unit_low, centers_low).reshape(images, NBIG + NSMALL, proto_count)
    queue_scores = against(queue.reshape(-1, queue.shape[-1]), centers_low).reshape(
        NBIG, -1, proto_count
    )
    shares = (
        jnp.exp(jnp.transpose(scores[:, :NBIG], (1, 0, 2)) / sink_temp) * image_mask[None, :, None]
    )
    others = jnp.exp(queue_scores / sink_temp)
    for iteration in range(ITERS):
        totals = lax.psum(jnp.sum(shares, 1) + jnp.sum(others, 1), "sub")
        shares = shares / totals[:, None, :]
        others = others / totals[:, None, :]
        shares = shares / (jnp.sum(shares, 2, keepdims=True) + (1.0 - image_mask)[None, :, None])
        others = others / jnp.sum(others, 2, keepdims=True)
    code_rows = jnp.transpose(shares, (1, 0, 2))
    log_probs = jax.nn.log_softmax(scores / softmax_temp, axis=-1)
    every_crop = jnp.sum(log_probs, 1)
    pair_count = NBIG * (NBIG + NSMALL - 1)
    loss_numer = -jnp.sum(code_rows * (every_crop[:, None, :] - log_probs[:, :NBIG])) / pair_count
    numer_all, live_all = lax.psum((loss_numer, live_float), ("dp", "sub"))
    crop_weight = jnp.concatenate(
        [jnp.full((NBIG,), NBIG - 1.0, jnp.float32), jnp.full((NSMALL,), float(NBIG), jnp.float32)]
    )
    own_codes = jnp.concatenate(
        [code_rows, jnp.zeros((images, NSMALL, proto_count), jnp.float32)], 1
    )
    code_total = jnp.sum(code_rows, 1)
    grad_scores = (
        crop_weight[None, :, None] * image_mask[:, None, None] * jnp.exp(log_probs)
        - code_total[:, None, :]
        + own_codes
    ) / (pair_count * softmax_temp)
    grad_low = grad_scores.reshape(-1, proto_count).astype(jnp.bfloat16)
    (grad_embed,) = embed_back(forward_dot(grad_low, centers_low))
    (grad_protos,) = center_back(cross_rows(grad_low, unit_low))
    embed_low = grad_embed.astype(jnp.bfloat16)
    d_out = cross_rows(act_four_low, embed_low)
    grad_act_four = against(embed_low, out_low) * silu_slope(pre_four)
    grad_proj, gain_four, bias_four = norm_back(
        grad_act_four, normal_four, stat_four, gains[3], crop_mask
    )
    proj_low = grad_proj.astype(jnp.bfloat16)
    d_hidden = cross_rows(pooled_low, proj_low)
    grad_pooled = against(proj_low, hidden_low).reshape(images, NBIG + NSMALL, channels)
    grad_big = jnp.broadcast_to(
        grad_pooled[:, :NBIG, None, :] / (BIG * BIG), (images, NBIG, BIG * BIG, channels)
    ).reshape(-1, channels)
    grad_small = jnp.broadcast_to(
        grad_pooled[:, NBIG:, None, :] / (SMALL * SMALL), (images, NSMALL, SMALL * SMALL, channels)
    ).reshape(-1, channels)
    again, unused = trunk_pass(
        inputs, row_mask, live_float, images, first_w, middle_w, last_w, gains, biases, stats
    )
    normal_one, pre_one, columns, normal_two, pre_two, act_two, normal_three, summed = again
    grad_summed = jnp.concatenate([grad_big, grad_small], 0) * silu_slope(summed)
    grad_three, gain_three, bias_three = norm_back(
        grad_summed, normal_three, stats[2], gains[2], row_mask
    )
    three_low = grad_three.astype(jnp.bfloat16)
    d_last = cross_rows(three_low, act_two)
    grad_act_two = forward_dot(three_low, last_w) * silu_slope(pre_two)
    grad_two, gain_two, bias_two = norm_back(grad_act_two, normal_two, stats[1], gains[1], row_mask)
    two_low = grad_two.astype(jnp.bfloat16)
    d_middle = cross_rows(columns, two_low)
    grad_columns = against(two_low, middle_w)

    def patch_big(active):
        return patches(active, images * NBIG, BIG)

    def patch_small(active):
        return patches(active, images * NSMALL, SMALL)

    unused_big, fold_big = jax.vjp(patch_big, jnp.zeros((big_rows, middle), jnp.float32))
    unused_small, fold_small = jax.vjp(patch_small, jnp.zeros((small_rows, middle), jnp.float32))
    (grad_act_big,) = fold_big(grad_columns[:big_rows])
    (grad_act_small,) = fold_small(grad_columns[big_rows:])
    grad_act_one = jnp.concatenate([grad_act_big, grad_act_small], 0) * silu_slope(pre_one)
    grad_one, gain_one, bias_one = norm_back(grad_act_one, normal_one, stats[0], gains[0], row_mask)
    one_low = grad_one.astype(jnp.bfloat16)
    d_first = cross_rows(inputs, one_low)
    grad_norms = jnp.stack(
        [
            jnp.concatenate([gain_one, gain_two, gain_three, gain_four]),
            jnp.concatenate([bias_one, bias_two, bias_three, bias_four]),
        ]
    )
    grad_outer = jnp.stack([d_first, d_last])
    grad_inner = d_middle.reshape(TAPS, middle, middle)
    proto_sum, norm_sum = lax.psum((grad_protos, grad_norms), ("dp", "sub"))
    data_summed = (
        lax.psum_scatter(grad_outer, "dp", scatter_dimension=1, tiled=True),
        lax.psum_scatter(grad_inner, "dp", scatter_dimension=1, tiled=True),
        lax.psum_scatter(d_hidden, "dp", scatter_dimension=0, tiled=True),
        lax.psum_scatter(d_out, "dp", scatter_dimension=0, tiled=True),
    )
    shard_outer, shard_inner, shard_hidden, shard_out = (
        lax.psum(data_summed[0].astype(jnp.bfloat16), "sub").astype(jnp.float32),
        lax.psum(data_summed[1].astype(jnp.bfloat16), "sub").astype(jnp.float32),
        lax.psum(data_summed[2].astype(jnp.bfloat16), "sub").astype(jnp.float32),
        lax.psum(data_summed[3].astype(jnp.bfloat16), "sub").astype(jnp.float32),
    )
    weight_sq = jnp.concatenate(
        [
            jnp.sum(bottleneck_outer * bottleneck_outer, (1, 2)),
            jnp.sum(bottleneck_inner * bottleneck_inner)[None],
            jnp.sum(proj_hidden * proj_hidden)[None],
            jnp.sum(proj_out * proj_out)[None],
        ]
    )
    grad_sq = jnp.concatenate(
        [
            jnp.sum(shard_outer * shard_outer, (1, 2)),
            jnp.sum(shard_inner * shard_inner)[None],
            jnp.sum(shard_hidden * shard_hidden)[None],
            jnp.sum(shard_out * shard_out)[None],
        ]
    )
    weight_all, grad_all = lax.psum((weight_sq, grad_sq), "dp")
    trusts = trust_rate * jnp.sqrt(weight_all) / (jnp.sqrt(grad_all) + 1e-12)
    proto_trust = (
        trust_rate
        * jnp.sqrt(jnp.sum(prototypes * prototypes))
        / (jnp.sqrt(jnp.sum(proto_sum * proto_sum)) + 1e-12)
    )
    norm_trust = (
        trust_rate
        * jnp.sqrt(jnp.sum(norm_params * norm_params, 1, keepdims=True))
        / (jnp.sqrt(jnp.sum(norm_sum * norm_sum, 1, keepdims=True)) + 1e-12)
    )
    outer_new = advance(
        bottleneck_outer, shard_outer, mom_outer, avg_outer, trusts[:2][:, None, None]
    )
    inner_new = advance(bottleneck_inner, shard_inner, mom_inner, avg_inner, trusts[2])
    hidden_new = advance(proj_hidden, shard_hidden, mom_hidden, avg_hidden, trusts[3])
    out_new = advance(proj_out, shard_out, mom_out, avg_out, trusts[4])
    protos_new = advance(prototypes, proto_sum, mom_protos, avg_protos, proto_trust)
    norms_new = advance(norm_params, norm_sum, mom_norms, avg_norms, norm_trust)
    return (
        numer_all,
        live_all,
        outer_new[0],
        inner_new[0],
        hidden_new[0],
        out_new[0],
        protos_new[0],
        norms_new[0],
        outer_new[1],
        inner_new[1],
        hidden_new[1],
        out_new[1],
        protos_new[1],
        norms_new[1],
        outer_new[2],
        inner_new[2],
        hidden_new[2],
        out_new[2],
        protos_new[2],
        norms_new[2],
        outer_new[0].astype(jnp.bfloat16),
        inner_new[0].astype(jnp.bfloat16),
        hidden_new[0].astype(jnp.bfloat16),
        out_new[0].astype(jnp.bfloat16),
    )


def solution(mesh):
    in_specs = (
        P(("dp", "sub"), None, None, None, None),
        P(("dp", "sub"), None, None, None, None),
        P(("dp", "sub")),
        P(None, ("dp", "sub"), None),
        P(None, "dp", None),
        P(None, "dp", None),
        P("dp", None),
        P("dp", None),
        P(),
        P(),
        P(None, "dp", None),
        P(None, "dp", None),
        P("dp", None),
        P("dp", None),
        P(),
        P(),
        P(None, "dp", None),
        P(None, "dp", None),
        P("dp", None),
        P("dp", None),
        P(),
        P(),
    )
    out_specs = (
        P(),
        P(),
        P(None, "dp", None),
        P(None, "dp", None),
        P("dp", None),
        P("dp", None),
        P(),
        P(),
        P(None, "dp", None),
        P(None, "dp", None),
        P("dp", None),
        P("dp", None),
        P(),
        P(),
        P(None, "dp", None),
        P(None, "dp", None),
        P("dp", None),
        P("dp", None),
        P(),
        P(),
        P(None, "dp", None),
        P(None, "dp", None),
        P("dp", None),
        P("dp", None),
    )
    return jax.shard_map(
        per_device, mesh=mesh, in_specs=in_specs, out_specs=out_specs, check_vma=False
    )
```

profile of v0, /device:TPU:0, one launch (start us, length us, event | category | flops | bytes accessed | tf_op | source)
XLA Modules:
  0.0 1563.6 jit_solution(8400943018732832622)
XLA Ops:
  47.3 24.3 %copy.52 = f32[1920,3000]{1,0:T(8,128)} copy(f32[1920,3000]{0,1:T(8,128)} %exponential_bitcast_fusion) | data formatting | bytes 46080000 | tf_op jit(solution)/shard_map/exp | solution.py:230
  82.2 36.2 %all_gather.15 = bf16[2048,128]{1,0:T(8,128)(2,1)} all-gather(bf16[256,128]{1,0:T(8,128)(2,1)S(1)} %get-tuple-element.144), channel_id=1, replica_groups=mesh['dp'=8,'sub'=4] {'dp'}, dimensions={0}, use_global_device_ids=true | all-gather | bytes 589824 | tf_op jit(solution)/shard_map/all_gather | solution.py:178
  202.1 13.4 multiply_reduce_fusion.6
  232.3 11.2 all-reduce.28
  275.8 20.5 %all-gather.8.cloned.1.call-done = bf16[2048,2048]{1,0:T(8,128)(2,1)} async-done(((bf16[256,2048]{1,0:T(8,128)(2,1)}), bf16[2048,2048]{1,0:T(8,128)(2,1)}) %all-gather.8.cloned.1.call-update) | async-done | bytes 8388624 | tf_op jit(solution)/shard_map/all_gather | solution.py:177
  334.4 24.2 %copy.53 = f32[1920,3000]{0,1:T(8,128)} copy(f32[1920,3000]{1,0:T(8,128)} %bitcast.118) | data formatting | bytes 46080000 | tf_op jit(solution)/shard_map/div | solution.py:234
  358.6 15.1 divide_reduce_fusion
  384.6 11.1 psum.229
  407.4 24.1 %copy.55 = f32[1920,3000]{0,1:T(8,128)} copy(f32[1920,3000]{1,0:T(8,128)} %bitcast.119) | data formatting | bytes 46080000 | tf_op jit(solution)/shard_map/div | solution.py:234
  431.5 21.9 %fusion.4 = f32[1920]{0:T(1024)S(1)} fusion(f32[1920,3000]{0,1:T(8,128)} %exponential_bitcast_fusion, f32[1920,3000]{0,1:T(8,128)} %copy.55, f32[1920,3000]{0,1:T(8,128)} %copy.53, f32[1920]{0:T(1024)S(1)} %divide_reduce_fusion), kind=kLoop, calls=%fused_computation.9 | loop fusion | flops 23038080 | bytes 69135360 | tf_op jit(solution)/shard_map/reduce_sum | solution.py:236
  453.5 11.0 fusion.3
  513.4 13.9 fusion.66
  561.4 12.9 fusion.92
  574.3 11.1 slice.194
  593.8 15.8 %reshape.350 = f32[16,7,7,4608]{3,2,1,0:T(8,128)} reshape(f32[784,4608]{1,0:T(8,128)} %slice.194) | data formatting | bytes 28901376 | tf_op jit(solution)/shard_map/transpose(jvp())/reshape | solution.py:32
  620.5 11.4 reshape.352
  671.7 11.4 fusion.6
  700.1 41.5 %all-reduce.21 = (f32[]{:T(128)}, f32[]{:T(128)}, f32[2,5120]{1,0:T(2,128)S(1)}) all-reduce(f32[]{:T(128)S(6)} %div.336, f32[]{:T(128)S(6)} %convert_element_type.126, f32[2,5120]{1,0:T(2,128)S(1)} %pad_maximum_fusion.4), channel_id=1, replica_groups=mesh['dp'=8,'sub'=4] {'dp','sub'}, use_global_device_ids=true, to_apply=%region_39.40 | all-reduce | flops 10242 | bytes 81936 | tf_op jit(solution)/shard_map/psum | solution.py:242
  744.0 113.3 %reduce-scatter.5.cloned.1.call-done = f32[2,256,512]{2,1,0:T(8,128)} async-done(((f32[2,2048,512]{2,1,0:T(8,128)}), f32[2,256,512]{2,1,0:T(8,128)}) %reduce-scatter.5.cloned.1.call-update) | async-done | bytes 1048592 | tf_op jit(solution)/shard_map/reduce_scatter | solution.py:313
  859.4 164.3 %reduce-scatter.7.cloned.1.call-done = f32[9,64,512]{2,1,0:T(8,128)} async-done(((f32[9,512,512]{2,1,0:T(8,128)}), f32[9,64,512]{2,1,0:T(8,128)}) %reduce-scatter.7.cloned.1.call-update) | async-done | bytes 1179664 | tf_op jit(solution)/shard_map/reduce_scatter | solution.py:314
  1025.8 282.7 %reduce-scatter.9.cloned.1.call-done = f32[256,2048]{1,0:T(8,128)} async-done(((f32[2048,2048]{1,0:T(8,128)}), f32[256,2048]{1,0:T(8,128)}) %reduce-scatter.9.cloned.1.call-update) | async-done | bytes 2097168 | tf_op jit(solution)/shard_map/reduce_scatter | solution.py:315
  1312.0 134.1 %all-reduce.35.cloned.1.call-done = f32[3000,128]{1,0:T(8,128)} async-done(((f32[3000,128]{1,0:T(8,128)}), f32[3000,128]{1,0:T(8,128)}) %all-reduce.35.cloned.1.call-update) | async-done | bytes 1536016 | tf_op jit(solution)/shard_map/psum | solution.py:311
  1449.2 54.0 %all-reduce.37.cloned.1.call-done = (bf16[2,256,512]{2,1,0:T(8,128)(2,1)}, bf16[256,128]{1,0:T(8,128)(2,1)}, bf16[256,2048]{1,0:T(8,128)(2,1)}, bf16[9,64,512]{2,1,0:T(8,128)(2,1)}) async-done(((bf16[2,256,512]{2,1,0:T(8,128)(2,1)}, bf16[256,128]{1,0:T(8,128)(2,1)}, bf16[256,2048]{1,0:T(8,128)(2,1)}, bf16[9,64,512]{2,1,0:T(8,128)(2,1)}), (bf16[2,256,512]{2,1,0:T(8,128)(2,1)}, bf16[256,128]{1,0:T(8,128)(2,1)}, ...) | async-done | bytes 2228240 | tf_op jit(solution)/shard_map/psum | solution.py:319
  1516.9 21.3 %all-reduce.22 = (f32[5]{0:T(128)S(1)}, f32[5]{0:T(128)S(1)}) all-reduce(f32[5]{0:T(128)S(1)} %pad_maximum_fusion.8, f32[5]{0:T(128)S(1)} %pad_maximum_fusion.7), channel_id=1, replica_groups=mesh['dp'=8,'sub'=4] {'dp'}, use_global_device_ids=true, to_apply=%region_76.77 | all-reduce | flops 10 | bytes 80 | tf_op jit(solution)/shard_map/psum | solution.py:340
  (395 shorter events, 443.4 us)
Async XLA Ops:
  7.2 11.3 copy-start
  7.2 116.7 %all-gather.4.cloned.1.call-start = ((), (), s32[]{:S(2)}) async-start(), calls=%async_computation.4 | async-start | bytes 4718592 | tf_op jit(solution)/shard_map/all_gather | solution.py:175
  10.5 191.6 %all-gather.6.cloned.1.call-start = ((), (), s32[]{:S(2)}) async-start(), calls=%async_computation.5 | async-start | bytes 5308416 | tf_op jit(solution)/shard_map/all_gather | solution.py:176
  12.3 284.0 %all-gather.8.cloned.1.call-start = ((), (), s32[]{:S(2)}) async-start(), calls=%async_computation.6 | async-start | bytes 9437184 | tf_op jit(solution)/shard_map/all_gather | solution.py:177
  16.7 725.7 %reduce-scatter.11.cloned.1.call-start = ((), (), s32[]{:S(2)}) async-start(), calls=%async_computation.10 | async-start | bytes 1179648 | tf_op jit(solution)/shard_map/reduce_scatter | solution.py:316
  81.5 58.7 %copy-start.80 = (f32[1,512]{1,0:T(1,128)}, f32[1,512]{1,0:T(1,128)S(1)}, u32[]{:S(2)}) copy-start(f32[1,512]{1,0:T(1,128)S(1)} %get-tuple-element.152) | copy-start | bytes 6148
  81.5 58.6 %copy-start.86 = (f32[1,512]{1,0:T(1,128)}, f32[1,512]{1,0:T(1,128)S(1)}, u32[]{:S(2)}) copy-start(f32[1,512]{1,0:T(1,128)S(1)} %get-tuple-element.151) | copy-start | bytes 6148
  275.7 25.6 %copy-start.57 = (bf16[8,2,2048]{2,1,0:T(2,128)(2,1)}, bf16[8,2,2048]{2,1,0:T(2,128)(2,1)S(1)}, u32[]{:S(2)}) copy-start(bf16[8,2,2048]{2,1,0:T(2,128)(2,1)S(1)} %multiply_convert_fusion.11) | copy-start | bytes 196612
  275.7 25.5 %copy-start.32 = (bf16[8,6,2048]{2,1,0:T(8,128)(2,1)}, bf16[8,6,2048]{2,1,0:T(8,128)(2,1)S(1)}, u32[]{:S(2)}) copy-start(bf16[8,6,2048]{2,1,0:T(8,128)(2,1)S(1)} %multiply_convert_fusion.10) | copy-start | bytes 589828
  275.7 36.2 %copy-start.40 = (bf16[2048,128]{1,0:T(8,128)(2,1)S(1)}, bf16[2048,128]{1,0:T(8,128)(2,1)}, u32[]{:S(2)}) copy-start(bf16[2048,128]{1,0:T(8,128)(2,1)} %all_gather.15) | copy-start | bytes 1572868
  312.3 165.2 %copy-start.55 = (f32[64,128]{1,0:T(8,128)}, f32[64,128]{1,0:T(8,128)S(1)}, u32[]{:S(2)}) copy-start(f32[64,128]{1,0:T(8,128)S(1)} %get-tuple-element.163) | copy-start | bytes 98308
  312.3 165.2 %copy-start.89 = (f32[64]{0:T(128)}, f32[64]{0:T(128)S(1)}, u32[]{:S(2)}) copy-start(f32[64]{0:T(128)S(1)} %add_rsqrt_fusion.5) | copy-start | bytes 772
  464.5 12.5 copy-start.74
  478.1 17.0 %copy-start.76 = (f32[2048]{0:T(1024)}, f32[2048]{0:T(1024)S(1)}, u32[]{:S(2)}) copy-start(f32[2048]{0:T(1024)S(1)} %get-tuple-element.40) | copy-start | bytes 24580
  478.1 17.0 %copy-start.78 = (f32[2048]{0:T(1024)}, f32[2048]{0:T(1024)S(1)}, u32[]{:S(2)}) copy-start(f32[2048]{0:T(1024)S(1)} %get-tuple-element.41) | copy-start | bytes 24580
  546.8 11.2 copy-start.88
  643.0 214.3 %reduce-scatter.5.cloned.1.call-start = ((), (), s32[]{:S(2)}) async-start(), calls=%async_computation.7 | async-start | bytes 9437184 | tf_op jit(solution)/shard_map/reduce_scatter | solution.py:313
  670.4 353.2 %reduce-scatter.7.cloned.1.call-start = ((), (), s32[]{:S(2)}) async-start(), calls=%async_computation.8 | async-start | bytes 10616832 | tf_op jit(solution)/shard_map/reduce_scatter | solution.py:314
  683.1 625.4 %reduce-scatter.9.cloned.1.call-start = ((), (), s32[]{:S(2)}) async-start(), calls=%async_computation.9 | async-start | bytes 18874368 | tf_op jit(solution)/shard_map/reduce_scatter | solution.py:315
  692.3 753.8 %all-reduce.35.cloned.1.call-start = ((), (), s32[]{:S(2)}) async-start(), calls=%async_computation.11 | async-start | bytes 3072000 | tf_op jit(solution)/shard_map/psum | solution.py:311
  698.0 805.2 %all-reduce.37.cloned.1.call-start = ((), (), s32[]{:S(2)}) async-start(), calls=%async_computation.12 | async-start | bytes 4456448 | tf_op jit(solution)/shard_map/psum | solution.py:319
  1025.8 285.4 %copy-start.72 = (f32[2,5120]{1,0:T(2,128)S(1)}, f32[2,5120]{1,0:T(2,128)}, u32[]{:S(2)}) copy-start(f32[2,5120]{1,0:T(2,128)} %param.43) | copy-start | bytes 122884
  1025.8 285.4 %copy-start.73 = (f32[2,5120]{1,0:T(2,128)S(1)}, f32[2,5120]{1,0:T(2,128)}, u32[]{:S(2)}) copy-start(f32[2,5120]{1,0:T(2,128)} %param.37) | copy-start | bytes 122884
  1512.5 26.4 %copy-start.18 = (bf16[256,2048]{1,0:T(8,128)(2,1)S(1)}, bf16[256,2048]{1,0:T(8,128)(2,1)}, u32[]{:S(2)}) copy-start(bf16[256,2048]{1,0:T(8,128)(2,1)} %get-tuple-element.68) | copy-start | bytes 3145732
  (81 other events, 290.2 us)
Sparse Core Ops, SparseCore 0:
  10.8 76.0 all-gather.3
  89.7 80.6 all-gather.5
  173.1 123.0 all-gather.7
  643.1 61.3 reduce-scatter.10
  708.4 148.8 reduce-scatter.4
  860.8 162.8 reduce-scatter.6
  1027.4 280.9 reduce-scatter.8
  1315.2 130.8 all-reduce.34
  1450.0 53.1 all-reduce.36
where the time goes:
time: 1580 us; the launch traced here: 1560 us
  waiting for transfers between devices  769 us (49%)
  local copies, waits for them, and re-layouts  280 us (18%)
  blocking collectives  199 us (13%)
  other arithmetic  189 us (12%)
  matrix products  106 us (7%)
  between operations  19.6 us (1%)
    reduce_scatter x1, waiting for transfers between devices, per_device(): lax.psum_scatter(d_hidden, 'dp', scatter_dimension=0, tiled=True)  283 us
    reduce_scatter x1, waiting for transfers between devices, per_device(): lax.psum_scatter(grad_inner, 'dp', scatter_dimension=1, tiled=True)  164 us
    psum x1, waiting for transfers between devices, per_device(): proto_sum, norm_sum = lax.psum((grad_protos, grad_norms), ('dp', 'sub'))  134 us
    reduce_scatter x1, waiting for transfers between devices, per_device(): lax.psum_scatter(grad_outer, 'dp', scatter_dimension=1, tiled=True)  113 us
    div x4, local copies, waits for them, and re-layouts, per_device(): others = others / totals[:, None, :]  69.9 us
    psum x1, waiting for transfers between devices, per_device(): lax.psum(data_summed[0].astype(jnp.bfloat16), 'sub').astype(jnp.float32)  54 us
    psum x1, blocking collectives, per_device(): numer_all, live_all = lax.psum((loss_numer, live_float), ('dp', 'sub'))  41.5 us
    dot_general x6, matrix products, against(): lax.dot_general(left, right, (((1,), (1,)), ((), ())), preferred_element_...  39.7 us
  transfers between devices with their start and end apart: 9, of which 6 were waited for; matrix products, arithmetic and copies ran while one was open for 17% of the time, Pallas kernels for 0%

commit v1 on v0

v1 whole, which is shorter than its diff:
```python
import functools
import math

import jax
import jax.numpy as jnp
from jax import lax
from jax.experimental import pallas as pl
from jax.experimental.pallas import tpu as pltpu
from jax.sharding import PartitionSpec as P

NBIG = 2
NSMALL = 6
CROPS = NBIG + NSMALL
BIG = 7
SMALL = 3
TAPS = 9
ITERS = 3
LANES = 128

sink_temp = 0.05
softmax_temp = 0.1
norm_eps = 1e-05
unit_eps = 1e-12
trust_rate = 0.5
learn_rate = 1.0
momentum_rate = 0.5
average_rate = 0.5

MESH = pl.DeviceIdType.MESH
MIB = 1 << 20
LOG2E = math.log2(math.e)
SINK2 = LOG2E / sink_temp
SOFT2 = LOG2E / softmax_temp
PAIRS = NBIG * (CROPS - 1)


def silu_slope(values):
    sigma = jax.nn.sigmoid(values)
    return sigma * (1.0 + values * (1.0 - sigma))


def cross_rows(left, right):
    return lax.dot_general(
        left, right, (((0,), (0,)), ((), ())), preferred_element_type=jnp.float32
    )


def against(left, right):
    return lax.dot_general(
        left, right, (((1,), (1,)), ((), ())), preferred_element_type=jnp.float32
    )


def forward_dot(left, right):
    return jnp.dot(left, right, preferred_element_type=jnp.float32)


def unit_rows(values):
    return values * lax.rsqrt(jnp.sum(values * values, 1, keepdims=True) + unit_eps)


def greet(axis, count):
    me = lax.axis_index(axis)
    barrier = pltpu.get_barrier_semaphore()
    for hop in range(1, count):
        pl.semaphore_signal(
            barrier, inc=1, device_id={axis: lax.rem(me + hop, count)}, device_id_type=MESH
        )
    pl.semaphore_wait(barrier, count - 1)


def exchange_kernel(axis, count, scatter, x_ref, o_ref, send_sem, recv_sem, own_sem):
    me = lax.axis_index(axis)
    greet(axis, count)
    copies = []
    for hop in range(1, count):
        to = lax.rem(me + hop, count)
        copy = pltpu.make_async_remote_copy(
            src_ref=x_ref.at[to] if scatter else x_ref,
            dst_ref=o_ref.at[me],
            send_sem=send_sem.at[hop],
            recv_sem=recv_sem.at[hop],
            device_id={axis: to},
            device_id_type=MESH,
        )
        copy.start()
        copies.append(copy)
    own = pltpu.make_async_copy(x_ref.at[me] if scatter else x_ref, o_ref.at[me], own_sem)
    own.start()
    own.wait()
    for copy in copies:
        copy.wait()


class Exchanger:
    def __init__(self, sizes):
        self.sizes = sizes
        self.used = 0

    def next_id(self):
        self.used += 1
        return self.used

    def __call__(self, values, axis, scatter=False, name="exchange"):
        count = self.sizes[axis]
        block = values.shape[1:] if scatter else values.shape
        return pl.pallas_call(
            functools.partial(exchange_kernel, axis, count, scatter),
            out_shape=jax.ShapeDtypeStruct((count,) + block, values.dtype),
            in_specs=[pl.BlockSpec(memory_space=pltpu.VMEM)],
            out_specs=pl.BlockSpec(memory_space=pltpu.VMEM),
            scratch_shapes=[
                pltpu.SemaphoreType.DMA((count,)),
                pltpu.SemaphoreType.DMA((count,)),
                pltpu.SemaphoreType.DMA,
            ],
            compiler_params=pltpu.CompilerParams(
                collective_id=self.next_id(), has_side_effects=True, vmem_limit_bytes=32 * MIB
            ),
            name=name,
        )(values)


def row_tile(rows):
    return next(size for size in (192, 160, 128, 96, 64, 48, 32, 24, 16, 8) if rows % size == 0)


def column_sums_kernel(queue_ref, turned_ref, o_ref, total):
    views, rows, _ = queue_ref.shape
    width = turned_ref.shape[1]
    tile = row_tile(rows)
    part = 256
    for view in range(views):
        total[...] = jnp.zeros_like(total)

        def step(index, carry):
            lines = queue_ref[view, pl.ds(index * tile, tile), :]
            for start in range(0, width, part):
                cols = pl.ds(start, part)
                scores = jnp.dot(lines, turned_ref[:, cols], preferred_element_type=jnp.float32)
                shares = jnp.exp2(scores * SINK2)
                total[:, cols] += jnp.sum(shares.reshape(tile // 8, 8, part), 0)
            return carry

        lax.fori_loop(0, rows // tile, step, 0)
        o_ref[pl.ds(view, 1), :] = jnp.sum(total[...], 0, keepdims=True)


def column_sums(queue, turned):
    width = turned.shape[1]
    return pl.pallas_call(
        column_sums_kernel,
        out_shape=jax.ShapeDtypeStruct((queue.shape[0], width), jnp.float32),
        in_specs=[pl.BlockSpec(memory_space=pltpu.VMEM)] * 2,
        out_specs=pl.BlockSpec(memory_space=pltpu.VMEM),
        scratch_shapes=[pltpu.VMEM((8, width), jnp.float32)],
        compiler_params=pltpu.CompilerParams(vmem_limit_bytes=32 * MIB),
        cost_estimate=pl.CostEstimate(
            flops=2 * queue.size * width,
            bytes_accessed=2 * queue.size,
            transcendentals=queue.size // queue.shape[2] * width,
        ),
        name="column_sums",
    )(queue, turned)


def sinkhorn_kernel(
    axis,
    count,
    protos,
    queue_ref,
    turned_ref,
    unit_ref,
    live_ref,
    first_ref,
    grad_ref,
    loss_ref,
    kept,
    scores,
    mine,
    landed,
    shift,
    total,
    send_sem,
    recv_sem,
):
    me = lax.axis_index(axis)
    views, rows, _ = queue_ref.shape
    width = turned_ref.shape[1]
    images = live_ref.shape[0]
    tile = row_tile(rows)
    part = 512
    parts = range(0, width, part)
    mask = live_ref[...]
    greet(axis, count)

    def sum_group(turn):
        copies = []
        for hop in range(1, count):
            copy = pltpu.make_async_remote_copy(
                src_ref=mine.at[turn],
                dst_ref=landed.at[turn, hop],
                send_sem=send_sem.at[turn, hop],
                recv_sem=recv_sem.at[turn, hop],
                device_id={axis: lax.rem(me + hop, count)},
                device_id_type=MESH,
            )
            copy.start()
            copies.append(copy)
        for copy in copies:
            copy.wait()
        whole = mine[turn]
        for hop in range(1, count):
            whole = whole + landed[turn, hop]
        return whole

    for start in parts:
        cols = pl.ds(start, part)
        scores[:, cols] = jnp.dot(
            unit_ref[...], turned_ref[:, cols], preferred_element_type=jnp.float32
        )
        for view in range(views):
            lines = pl.ds(view * images, images)
            shares = jnp.exp2(scores[lines, cols] * SINK2) * mask
            mine[0, pl.ds(view, 1), cols] = first_ref[pl.ds(view, 1), cols] + jnp.sum(
                shares, 0, keepdims=True
            )
    real = lax.broadcasted_iota(jnp.int32, (1, width), 1) < protos
    first = sum_group(0)
    shift[...] = jnp.where(real, jnp.log2(first), 1e30)

    for turn in range(1, ITERS):
        for view in range(views):
            lines = pl.ds(view * images, images)
            row = pl.ds(view, 1)
            if turn == 1:
                own = jnp.exp2(scores[lines, :] * SINK2 - shift[row, :]) * mask
                weight = jnp.sum(own, 1, keepdims=True)
            else:
                own = jnp.exp2(scores[lines, :] * SINK2 - first_log[row, :]) * mask
                weight = jnp.sum(own * shift[row, :], 1, keepdims=True)
            total[...] = own / (weight + (1.0 - mask))

            def step(index, carry):
                span = pl.ds(index * tile, tile)
                if turn == 1:
                    lines = queue_ref[view, span, :]
                sums = jnp.zeros((tile, LANES), jnp.float32)
                for start in parts:
                    cols = pl.ds(start, part)
                    if turn == 1:
                        raw = jnp.dot(lines, turned_ref[:, cols], preferred_element_type=jnp.float32)
                        shares = jnp.exp2(raw * SINK2 - shift[row, cols])
                        kept[view, span, cols] = shares
                    else:
                        shares = kept[view, span, cols] * shift[row, cols]
                    for lane in range(0, part, LANES):
                        sums = sums + shares[:, lane : lane + LANES]
                scale = 1.0 / jnp.sum(sums, 1, keepdims=True)
                for start in parts:
                    cols = pl.ds(start, part)
                    scaled = kept[view, span, cols] * scale
                    total[:, cols] += jnp.sum(scaled.reshape(tile // 8, 8, part), 0)
                return carry

            lax.fori_loop(0, rows // tile, step, 0)
            mine[turn, row, :] = jnp.sum(total[...], 0, keepdims=True)
        if turn == 1:
            first_log = shift[...]
        whole = sum_group(turn)
        shift[...] = jnp.where(real, 1.0 / whole, 0.0)

    codes = []
    for view in range(views):
        lines = pl.ds(view * images, images)
        own = jnp.exp2(scores[lines, :] * SINK2 - first_log[view : view + 1, :]) * mask
        own = own * shift[pl.ds(view, 1), :]
        codes.append(own / (jnp.sum(own, 1, keepdims=True) + (1.0 - mask)))
    code_total = codes[0] + codes[1]
    loss = jnp.zeros((images, 1), jnp.float32)
    for crop in range(CROPS):
        lines = pl.ds(crop * images, images)
        raw = jnp.where(real, scores[lines, :] * SOFT2, -1e30)
        raw = raw - jnp.max(raw, 1, keepdims=True)
        powers = jnp.exp2(raw)
        norm = jnp.sum(powers, 1, keepdims=True)
        others = code_total - codes[crop] if crop < NBIG else code_total
        logs = jnp.where(real, (raw - jnp.log2(norm)) / LOG2E, 0.0)
        loss = loss - jnp.sum(others * logs, 1, keepdims=True)
        weight = (NBIG - 1.0 if crop < NBIG else float(NBIG)) * mask / norm
        grad = (weight * powers - others) / (PAIRS * softmax_temp)
        grad_ref[lines, :] = grad.astype(grad_ref.dtype)
    loss_ref[...] = jnp.broadcast_to(
        jnp.sum(loss, 0, keepdims=True) / PAIRS, loss_ref.shape
    )


def sinkhorn(sizes, collective_id, protos, queue, turned, unit, live, first):
    count = sizes["sub"]
    views, rows, depth = queue.shape
    width = turned.shape[1]
    crops = unit.shape[0]
    return pl.pallas_call(
        functools.partial(sinkhorn_kernel, "sub", count, protos),
        out_shape=(
            jax.ShapeDtypeStruct((crops, width), jnp.bfloat16),
            jax.ShapeDtypeStruct((8, LANES), jnp.float32),
        ),
        in_specs=[pl.BlockSpec(memory_space=pltpu.VMEM)] * 5,
        out_specs=(pl.BlockSpec(memory_space=pltpu.VMEM),) * 2,
        scratch_shapes=[
            pltpu.VMEM((views, rows, width), jnp.float32),
            pltpu.VMEM((crops, width), jnp.float32),
            pltpu.VMEM((ITERS, views, width), jnp.float32),
            pltpu.VMEM((ITERS, count, views, width), jnp.float32),
            pltpu.VMEM((views, width), jnp.float32),
            pltpu.VMEM((8, width), jnp.float32),
            pltpu.SemaphoreType.DMA((ITERS, count)),
            pltpu.SemaphoreType.DMA((ITERS, count)),
        ],
        compiler_params=pltpu.CompilerParams(
            collective_id=collective_id, has_side_effects=True, vmem_limit_bytes=48 * MIB
        ),
        name="sinkhorn",
    )(queue, turned, unit, live, first)


def split_rows(values, images):
    big = BIG * BIG * NBIG * images
    wide = values.shape[1]
    return (
        values[:big].reshape(BIG, BIG, NBIG * images, wide),
        values[big:].reshape(SMALL, SMALL, NSMALL * images, wide),
    )


def patches(values, images, flip):
    parts = []
    for spatial in split_rows(values, images):
        extent = spatial.shape[0]
        padded = jnp.pad(spatial, ((1, 1), (1, 1), (0, 0), (0, 0)))
        pieces = [
            padded[row : row + extent, col : col + extent]
            for row in range(3)
            for col in range(3)
        ]
        if flip:
            pieces = pieces[::-1]
        parts.append(jnp.concatenate(pieces, -1).reshape(-1, TAPS * values.shape[1]))
    return jnp.concatenate(parts, 0)


def spread_crops(values, images):
    wide = values.shape[1]
    big = jnp.broadcast_to(
        values[: NBIG * images] / (BIG * BIG), (BIG * BIG, NBIG * images, wide)
    ).reshape(-1, wide)
    small = jnp.broadcast_to(
        values[NBIG * images :] / (SMALL * SMALL), (SMALL * SMALL, NSMALL * images, wide)
    ).reshape(-1, wide)
    return jnp.concatenate([big, small], 0)


def pool_crops(values, images):
    big, small = split_rows(values, images)
    return jnp.concatenate([jnp.mean(big, (0, 1)), jnp.mean(small, (0, 1))], 0)


def advance(weight, gradient, moment, average, trust):
    step_now = trust * gradient
    moment_new = momentum_rate * moment + step_now
    weight_new = weight - learn_rate * (step_now + momentum_rate * moment_new)
    average_new = average_rate * average + (1.0 - average_rate) * weight_new
    return (weight_new, moment_new, average_new)


def per_device(
    sizes,
    big_maps,
    small_maps,
    live_counts,
    queue,
    bottleneck_outer,
    bottleneck_inner,
    proj_hidden,
    proj_out,
    prototypes,
    norm_params,
    mom_outer,
    mom_inner,
    mom_hidden,
    mom_out,
    mom_protos,
    mom_norms,
    avg_outer,
    avg_inner,
    avg_hidden,
    avg_out,
    avg_protos,
    avg_norms,
):
    n_sub = sizes["sub"]
    exchange = Exchanger(sizes)
    images = big_maps.shape[0]
    channels = big_maps.shape[-1]
    middle = bottleneck_inner.shape[-1]
    hidden_width = proj_hidden.shape[1]
    out_width = proj_out.shape[1]
    proto_count = prototypes.shape[0]
    proto_width = -(-proto_count // 512) * 512
    here = lax.axis_index("sub")
    share = hidden_width // n_sub

    outer_low = lax.all_gather(bottleneck_outer.astype(jnp.bfloat16), "dp", axis=1, tiled=True)
    inner_low = lax.all_gather(bottleneck_inner.astype(jnp.bfloat16), "dp", axis=1, tiled=True)
    hidden_cols = lax.dynamic_slice_in_dim(proj_hidden, here * share, share, 1)
    hidden_low = lax.all_gather(hidden_cols.astype(jnp.bfloat16), "dp", axis=0, tiled=True)
    out_low = lax.all_gather(proj_out.astype(jnp.bfloat16), "dp", axis=0, tiled=True)
    out_low = lax.dynamic_slice_in_dim(out_low, here * share, share, 0)
    first_w = outer_low[0]
    last_w = outer_low[1]
    middle_w = inner_low.reshape(TAPS * middle, middle)
    middle_t = jnp.transpose(inner_low, (0, 2, 1)).reshape(TAPS * middle, middle)

    bounds = [0, middle, 2 * middle, 2 * middle + channels, 2 * middle + channels + hidden_width]
    gains = [norm_params[0, bounds[k] : bounds[k + 1]] for k in range(4)]
    biases = [norm_params[1, bounds[k] : bounds[k + 1]] for k in range(4)]
    gains[3] = lax.dynamic_slice_in_dim(gains[3], here * share, share, 0)
    biases[3] = lax.dynamic_slice_in_dim(biases[3], here * share, share, 0)

    proto_inv = lax.rsqrt(jnp.sum(prototypes * prototypes, 1, keepdims=True) + unit_eps)
    centers_low = (prototypes * proto_inv).astype(jnp.bfloat16)
    centers_low = jnp.pad(centers_low, ((0, proto_width - proto_count), (0, 0)))
    turned = centers_low.T
    first_sums = column_sums(queue, turned)

    live_float = live_counts[0].astype(jnp.float32)
    image_mask = (jnp.arange(images) < live_counts[0]).astype(jnp.float32)[:, None]
    per_image = NBIG * BIG * BIG + NSMALL * SMALL * SMALL
    rows = per_image * images
    row_mask = jnp.broadcast_to(image_mask, (per_image, images, 1)).reshape(rows, 1)

    inputs = jnp.concatenate(
        [
            jnp.transpose(big_maps, (2, 3, 1, 0, 4)).reshape(-1, channels),
            jnp.transpose(small_maps, (2, 3, 1, 0, 4)).reshape(-1, channels),
        ],
        0,
    )

    hidden_one = forward_dot(inputs, first_w)
    masked = hidden_one * row_mask
    sums = exchange(
        jnp.stack(
            [
                jnp.sum(masked, 0),
                jnp.sum(masked * hidden_one, 0),
                jnp.broadcast_to(live_float, (middle,)),
            ]
        ),
        "sub",
        name="sums_one",
    )
    lives = sums[:, 2, 0]
    count_all = jnp.sum(lives) * per_image

    def stats(total, squares, count):
        mean = total / count
        return mean, lax.rsqrt(squares / count - mean * mean + norm_eps)

    def group_stats(values, name):
        masked = values * row_mask
        both = exchange(
            jnp.stack([jnp.sum(masked, 0), jnp.sum(masked * values, 0)]), "sub", name=name
        )
        both = jnp.sum(both, 0)
        return stats(both[0], both[1], count_all)

    sums = jnp.sum(sums, 0)
    mean_one, inv_one = stats(sums[0], sums[1], count_all)
    normal_one = (hidden_one - mean_one) * inv_one
    pre_one = gains[0] * normal_one + biases[0]
    act_one = jax.nn.silu(pre_one).astype(jnp.bfloat16)
    columns = patches(act_one, images, False)
    hidden_two = forward_dot(columns, middle_w)
    mean_two, inv_two = group_stats(hidden_two, "sums_two")
    normal_two = (hidden_two - mean_two) * inv_two
    pre_two = gains[1] * normal_two + biases[1]
    act_two = jax.nn.silu(pre_two).astype(jnp.bfloat16)
    hidden_three = against(act_two, last_w)
    mean_three, inv_three = group_stats(hidden_three, "sums_three")
    normal_three = (hidden_three - mean_three) * inv_three
    summed = gains[2] * normal_three + biases[2] + inputs.astype(jnp.float32)
    pooled_low = pool_crops(jax.nn.silu(summed), images).astype(jnp.bfloat16)

    crops = CROPS * images
    pooled_all = exchange(pooled_low, "sub", name="pooled").reshape(n_sub * crops, channels)
    group_mask = (jnp.arange(images)[None, :] < lives[:, None]).astype(jnp.float32)
    group_mask = jnp.broadcast_to(group_mask[:, None, :], (n_sub, CROPS, images))
    group_mask = group_mask.reshape(n_sub * crops, 1)
    count_crops = jnp.sum(lives) * CROPS
    proj_pre = forward_dot(pooled_all, hidden_low)
    masked = proj_pre * group_mask
    mean_four, inv_four = stats(jnp.sum(masked, 0), jnp.sum(masked * proj_pre, 0), count_crops)
    normal_four = (proj_pre - mean_four) * inv_four
    pre_four = gains[3] * normal_four + biases[3]
    act_four = jax.nn.silu(pre_four).astype(jnp.bfloat16)
    partial = forward_dot(act_four, out_low).reshape(n_sub, crops, out_width)
    embedding = jnp.sum(exchange(partial, "sub", scatter=True, name="embedding"), 0)
    unit_embed, embed_back = jax.vjp(unit_rows, embedding)
    unit_low = unit_embed.astype(jnp.bfloat16)

    grad_low, loss_tile = sinkhorn(
        sizes, exchange.next_id(), proto_count, queue, turned, unit_low, image_mask, first_sums
    )
    (grad_embed,) = embed_back(forward_dot(grad_low, centers_low))
    grad_centers = cross_rows(grad_low, unit_low)
    embed_low = grad_embed.astype(jnp.bfloat16)
    embed_all = exchange(embed_low, "sub", name="embed_grad").reshape(n_sub * crops, out_width)

    d_out = cross_rows(act_four, embed_all)
    grad_four = against(embed_all, out_low) * silu_slope(pre_four)
    bias_four = jnp.sum(grad_four, 0)
    gain_four = jnp.sum(grad_four * normal_four, 0)
    proj_low = (
        gains[3]
        * inv_four
        * (grad_four - group_mask * (bias_four + normal_four * gain_four) / count_crops)
    ).astype(jnp.bfloat16)
    d_hidden = cross_rows(pooled_all, proj_low)
    partial = against(proj_low, hidden_low).astype(jnp.bfloat16).reshape(n_sub, crops, channels)
    grad_pooled = exchange(partial, "sub", scatter=True, name="pooled_grad")
    grad_pooled = jnp.sum(grad_pooled.astype(jnp.float32), 0)

    hidden_sum = lax.psum_scatter(d_hidden.astype(jnp.bfloat16), "dp", scatter_dimension=0, tiled=True)
    out_group = exchange(d_out.astype(jnp.bfloat16), "sub", name="out_grad")
    out_sum = lax.psum_scatter(
        out_group.reshape(hidden_width, out_width), "dp", scatter_dimension=0, tiled=True
    )
    shard_hidden = exchange(hidden_sum, "sub", name="hidden_shard")
    shard_hidden = jnp.transpose(shard_hidden, (1, 0, 2)).reshape(-1, hidden_width)
    shard_hidden = shard_hidden.astype(jnp.float32)
    shard_out = out_sum.astype(jnp.float32)

    def norm_back(grad_out, normal, inv_std, gain_vec, name):
        bias_local = jnp.sum(grad_out, 0)
        gain_local = jnp.sum(grad_out * normal, 0)
        both = jnp.sum(exchange(jnp.stack([bias_local, gain_local]), "sub", name=name), 0)
        grad_in = (
            gain_vec * inv_std * (grad_out - row_mask * (both[0] + normal * both[1]) / count_all)
        )
        return grad_in.astype(jnp.bfloat16), gain_local, bias_local

    grad_summed = spread_crops(grad_pooled, images) * silu_slope(summed)
    three_low, gain_three, bias_three = norm_back(
        grad_summed, normal_three, inv_three, gains[2], "back_three"
    )
    d_last = cross_rows(three_low, act_two)
    grad_act_two = forward_dot(three_low, last_w) * silu_slope(pre_two)
    two_low, gain_two, bias_two = norm_back(
        grad_act_two, normal_two, inv_two, gains[1], "back_two"
    )
    d_middle = cross_rows(columns, two_low)
    grad_act_one = forward_dot(patches(two_low, images, True), middle_t) * silu_slope(pre_one)
    one_low, gain_one, bias_one = norm_back(
        grad_act_one, normal_one, inv_one, gains[0], "back_one"
    )
    d_first = cross_rows(inputs, one_low)

    wide_four = jnp.zeros((2, hidden_width), jnp.float32)
    wide_four = lax.dynamic_update_slice(
        wide_four, jnp.stack([gain_four, bias_four]), (0, here * share)
    )
    grad_norms = jnp.concatenate(
        [
            jnp.stack(
                [
                    jnp.concatenate([gain_one, gain_two, gain_three]),
                    jnp.concatenate([bias_one, bias_two, bias_three]),
                ]
            ),
            wide_four,
        ],
        1,
    )
    centers_sum, norm_sum, numer_all, live_all = lax.psum(
        (grad_centers, grad_norms, loss_tile[0, 0], live_float), ("dp", "sub")
    )
    centers_sum = centers_sum[:proto_count]
    proto_unit = prototypes * proto_inv
    proto_sum = proto_inv * (
        centers_sum - proto_unit * jnp.sum(proto_unit * centers_sum, 1, keepdims=True)
    )
    grad_outer = jnp.stack([d_first, d_last]).astype(jnp.bfloat16)
    grad_inner = d_middle.reshape(TAPS, middle, middle).astype(jnp.bfloat16)
    shard_outer = lax.psum(
        lax.psum_scatter(grad_outer, "dp", scatter_dimension=1, tiled=True), "sub"
    ).astype(jnp.float32)
    shard_inner = lax.psum(
        lax.psum_scatter(grad_inner, "dp", scatter_dimension=1, tiled=True), "sub"
    ).astype(jnp.float32)

    squares = jnp.concatenate(
        [
            jnp.sum(bottleneck_outer * bottleneck_outer, (1, 2)),
            jnp.sum(bottleneck_inner * bottleneck_inner)[None],
            jnp.sum(proj_hidden * proj_hidden)[None],
            jnp.sum(proj_out * proj_out)[None],
            jnp.sum(shard_outer * shard_outer, (1, 2)),
            jnp.sum(shard_inner * shard_inner)[None],
            jnp.sum(shard_hidden * shard_hidden)[None],
            jnp.sum(shard_out * shard_out)[None],
        ]
    )
    squares = jnp.broadcast_to(jnp.pad(squares, (0, 6))[:, None], (16, LANES))
    squares = jnp.sum(exchange(squares, "dp", name="norms"), 0)[:, 0]
    weight_all, grad_all = squares[:5], squares[5:10]
    trusts = trust_rate * jnp.sqrt(weight_all) / (jnp.sqrt(grad_all) + 1e-12)
    proto_trust = (
        trust_rate
        * jnp.sqrt(jnp.sum(prototypes * prototypes))
        / (jnp.sqrt(jnp.sum(proto_sum * proto_sum)) + 1e-12)
    )
    norm_trust = (
        trust_rate
        * jnp.sqrt(jnp.sum(norm_params * norm_params, 1, keepdims=True))
        / (jnp.sqrt(jnp.sum(norm_sum * norm_sum, 1, keepdims=True)) + 1e-12)
    )
    outer_new = advance(
        bottleneck_outer, shard_outer, mom_outer, avg_outer, trusts[:2][:, None, None]
    )
    inner_new = advance(bottleneck_inner, shard_inner, mom_inner, avg_inner, trusts[2])
    hidden_new = advance(proj_hidden, shard_hidden, mom_hidden, avg_hidden, trusts[3])
    out_new = advance(proj_out, shard_out, mom_out, avg_out, trusts[4])
    protos_new = advance(prototypes, proto_sum, mom_protos, avg_protos, proto_trust)
    norms_new = advance(norm_params, norm_sum, mom_norms, avg_norms, norm_trust)
    news = (outer_new, inner_new, hidden_new, out_new, protos_new, norms_new)
    return (
        (numer_all, live_all)
        + tuple(new[0] for new in news)
        + tuple(new[1] for new in news)
        + tuple(new[2] for new in news)
        + tuple(new[0].astype(jnp.bfloat16) for new in news[:4])
    )


def solution(mesh):
    data = P(("dp", "sub"), None, None, None, None)
    trees = (P(None, "dp", None), P(None, "dp", None), P("dp", None), P("dp", None), P(), P())
    in_specs = (data, data, P(("dp", "sub")), P(None, ("dp", "sub"), None)) + trees * 3
    out_specs = (P(), P()) + trees * 3 + trees[:4]
    sizes = {axis: mesh.shape[axis] for axis in ("dp", "sub")}
    return jax.shard_map(
        functools.partial(per_device, sizes),
        mesh=mesh,
        in_specs=in_specs,
        out_specs=out_specs,
        check_vma=False,
    )
```

time: 1580 us -> 901 us (0.57)
  waiting for transfers between devices: 769 us -> 403 us
  local copies, waits for them, and re-layouts: 280 us -> 106 us
  blocking collectives: 199 us -> 77.3 us
  Pallas kernels: 0 us -> 121 us
  other arithmetic: 189 us -> 85.6 us
  matrix products: 106 us -> 82.9 us
    psum x2, waiting for transfers between devices: 188 us -> 24.4 us  [the longest x1 19.5 us: per_device(): lax.psum(lax.psum_scatter(grad_outer, 'dp', scatter_dimension=1, tiled=Tr...]
    reduce_scatter x2, waiting for transfers between devices: 283 us -> 123 us  [the longest x1 69.3 us: per_device(): lax.psum_scatter(d_hidden.astype(jnp.bfloat16), 'dp', scatter_dimension=0...]
    psum x13 -> x1, blocking collectives: 162 us -> 40.6 us  [per_device(): lax.psum((grad_centers, grad_norms, loss_tile[0, 0], live_float), ('dp',...]
    pallas_call x0 -> x15, Pallas kernels: none -> 121 us  [the longest x13 95 us: __call__(): pl.pallas_call(functools.partial(exchange_kernel, axis, count, scatter),...]
    reduce_sum x16 -> x13, other arithmetic: 79.1 us -> 8.46 us  [the longest x2 5.36 us: pool_crops(): return jnp.concatenate([jnp.mean(big, (0, 1)), jnp.mean(small, (0, 1))], 0)]
    div x6 -> x0, local copies, waits for them, and re-layouts: 70.1 us -> none  [the longest x4 69.9 us: per_device(): others = others / totals[:, None, :]]
    reshape x12 -> x0, local copies, waits for them, and re-layouts: 66.6 us -> none  [the longest x2 27.3 us: patches(): jnp.concatenate(pieces, axis=-1).reshape(crop_count * extent * extent, -1)]
    reduce_scatter x1, waiting for transfers between devices: 164 us -> 99.4 us  [per_device(): lax.psum_scatter(grad_inner, 'dp', scatter_dimension=1, tiled=True)]
  transfers between devices with their start and end apart: 9 -> 9, of which waited for: 6 -> 8; matrix products, arithmetic and copies ran while one was open for 17% -> 19% of each run, Pallas kernels for 0% -> 7%
where the time goes in v1:
time: 901 us; the launch traced here: 897 us
  waiting for transfers between devices  403 us (45%)
  Pallas kernels  121 us (13%)
  local copies, waits for them, and re-layouts  106 us (12%)
  other arithmetic  85.6 us (10%)
  matrix products  82.9 us (9%)
  blocking collectives  77.3 us (9%)
  between operations  19.3 us (2%)
    reduce_scatter x1, waiting for transfers between devices, per_device(): lax.psum_scatter(grad_inner, 'dp', scatter_dimension=1, tiled=True)  99.4 us
    pallas_call x13, Pallas kernels, __call__(): pl.pallas_call(functools.partial(exchange_kernel, axis, count, scatter),...  95 us
    reduce_scatter x1, waiting for transfers between devices, per_device(): lax.psum_scatter(grad_outer, 'dp', scatter_dimension=1, tiled=True)  86.9 us
    reduce_scatter x1, waiting for transfers between devices, per_device(): lax.psum_scatter(d_hidden.astype(jnp.bfloat16), 'dp', scatter_dimension=0...  69.3 us
    unnamed x293, local copies, waits for them, and re-layouts  67.8 us
    reduce_scatter x1, waiting for transfers between devices, per_device(): lax.psum_scatter(out_group.reshape(hidden_width, out_width), 'dp', scatte...  53.7 us
    all_gather x1, waiting for transfers between devices, per_device(): lax.all_gather(bottleneck_inner.astype(jnp.bfloat16), 'dp', axis=1, tiled...  45.2 us
    dot_general x7, matrix products, forward_dot(): return jnp.dot(left, right, preferred_element_type=jnp.float32)  43.9 us
  transfers between devices with their start and end apart: 9, of which 8 were waited for; matrix products, arithmetic and copies ran while one was open for 19% of the time, Pallas kernels for 7%

profile of v1, /device:TPU:0, one launch (start us, length us, event | category | flops | bytes accessed | tf_op | source)
XLA Modules:
  0.0 896.6 jit_solution(7501037826495010740)
XLA Ops:
  23.6 36.7 %all_gather.15 = bf16[2048,128]{1,0:T(8,128)(2,1)} all-gather(bf16[256,128]{1,0:T(8,128)(2,1)S(1)} %get-tuple-element.240), channel_id=1, replica_groups=mesh['dp'=8,'sub'=4] {'dp'}, dimensions={0}, use_global_device_ids=true | all-gather | bytes 589824 | tf_op jit(solution)/shard_map/all_gather | solution.py:418
  66.1 24.2 %all-gather.4.cloned.1.call-done = bf16[2,2048,512]{2,1,0:T(8,128)(2,1)} async-done(((bf16[2,256,512]{2,1,0:T(8,128)(2,1)}), bf16[2,2048,512]{2,1,0:T(8,128)(2,1)}) %all-gather.4.cloned.1.call-update) | async-done | bytes 4194320 | tf_op jit(solution)/shard_map/all_gather | solution.py:414
  90.4 7.5 multiply_reduce_fusion.3
  127.1 45.2 %all-gather.6.cloned.1.call-done = bf16[9,512,512]{2,1,0:T(8,128)(2,1)} async-done(((bf16[9,64,512]{2,1,0:T(8,128)(2,1)}), bf16[9,512,512]{2,1,0:T(8,128)(2,1)}) %all-gather.6.cloned.1.call-update) | async-done | bytes 4718608 | tf_op jit(solution)/shard_map/all_gather | solution.py:415
  172.3 13.1 %multiply_reduce_fusion.2 = (f32[512]{0:T(512)S(1)}, f32[512]{0:T(512)S(1)}, f32[1216,512]{1,0:T(8,128)}) fusion(f32[1216]{0:T(1024)S(1)} %broadcast_in_dim.33, bf16[4608,512]{1,0:T(8,128)(2,1)} %bitcast.178, bf16[432,4608]{1,0:T(8,128)(2,1)} %constant_dynamic-update-slice_fusion.9, bf16[784,4608]{1,0:T(8,128)(2,1)} %constant_dynamic-update-slice_fusion), kind=kOutput, calls=%fused_computation.20 | convolution fusion | flops 5762710528 | bytes 18424576 | tf_op jit(solution)/shard_map/dot_general | solution.py:55
  189.9 9.4 %multiply_reduce_fusion = (f32[2048]{0:T(1024)S(1)}, f32[2048]{0:T(1024)S(1)}, f32[1216,2048]{1,0:T(8,128)}) fusion(f32[1216]{0:T(1024)S(1)} %broadcast_in_dim.33, bf16[2,2048,512]{2,1,0:T(8,128)(2,1)} %all-gather.4.cloned.1.call-done, f32[1216,512]{1,0:T(8,128)} %get-tuple-element.261, f32[512]{0:T(512)S(1)} %bitcast.274, f32[512]{0:T(512)S(1)} %bitcast.246, ...), kind=kOutput, calls=%fused_computation.1 | convolution fusion | flops 2565697536 | bytes 14578432 | tf_op jit(solution)/shard_map/dot_general | solution.py:49
  203.9 7.2 fusion.5
  222.1 13.4 %pooled.1 = bf16[4,64,2048]{2,1,0:T(8,128)(2,1)S(1)} custom-call(bf16[64,2048]{1,0:T(8,128)(2,1)S(1)} %pad_maximum_fusion.5.x_ref), custom_call_target="tpu_custom_call" | custom-call | tf_op jit(solution)/shard_map/pooled/pallas_call | solution.py:107
  245.4 21.4 %sinkhorn.1 = (bf16[64,3072]{1,0:T(8,128)(2,1)S(1)}, f32[8,128]{1,0:T(8,128)S(1)}) custom-call(bf16[2,960,128]{2,1,0:T(8,128)(2,1)S(1)} %copy-done, bf16[128,3072]{1,0:T(8,128)(2,1)S(1)} %pad_bitcast_fusion.turned_ref, bf16[64,128]{1,0:T(8,128)(2,1)S(1)} %multiply_convert_fusion.11.unit_ref, f32[8,1]{1,0:T(8,128)S(1)} %fusion.48.live_ref, ...), custom_call_target="tpu_custom_call" | custom-call | tf_op jit(solution)/shard_map/sinkhorn/pallas_call | solution.py:303
  274.5 13.4 %pooled_grad.1 = bf16[4,64,2048]{2,1,0:T(8,128)(2,1)S(1)} custom-call(bf16[4,64,2048]{2,1,0:T(8,128)(2,1)S(1)} %bitcast.158), custom_call_target="tpu_custom_call" | custom-call | tf_op jit(solution)/shard_map/pooled_grad/pallas_call | solution.py:107
  292.1 7.5 fusion.55
  304.1 9.3 %multiply_convert_fusion = bf16[1216,2048]{1,0:T(8,128)(2,1)S(1)} fusion(f32[1216,2048]{1,0:T(8,128)} %get-tuple-element.198, f32[1216,2048]{1,0:T(8,128)} %get-tuple-element.262, f32[]{:T(128)S(6)} %mul.587, f32[2048]{0:T(1024)S(1)} %bitcast.234, f32[2048]{0:T(1024)S(1)} %bitcast.233, f32[2048]{0:T(1024)S(1)} %bitcast.235, f32[2048]{0:T(1024)S(1)} %bitcast.220, ...), kind=kLoop, calls=%fused_computation.9 | loop fusion | flops 22413312 | bytes 24949508 | tf_op jit(solution)/shard_map/convert_element_type | solution.py:552
  354.2 13.1 %fusion.56 = (f32[512]{0:T(512)S(1)}, f32[512]{0:T(512)S(1)}, f32[1216,512]{1,0:T(8,128)}) fusion(f32[512]{0:T(512)S(1)} %bitcast.237, f32[1216,512]{1,0:T(8,128)S(1)} %copy-done.27, f32[512]{0:T(512)S(1)} %bitcast.240, f32[512]{0:T(512)S(1)} %bitcast.245, f32[512]{0:T(512)S(1)} %bitcast.243, bf16[4608,512]{1,0:T(8,128)(2,1)S(1)} %bitcast.181, ...), kind=kOutput, calls=%fused_computation.251 | convolution fusion | flops 5769559040 | bytes 20918272 | tf_op jit(solution)/shard_map/dot_general | solution.py:55
  371.1 6.9 fusion.10
  387.8 10.6 %convolution_convert_fusion = bf16[4608,512]{1,0:T(8,128)(2,1)} fusion(bf16[1216,512]{1,0:T(8,128)(2,1)S(1)} %copy-done.10, bf16[432,4608]{1,0:T(8,128)(2,1)} %constant_dynamic-update-slice_fusion.9, bf16[784,4608]{1,0:T(8,128)(2,1)} %constant_dynamic-update-slice_fusion), kind=kOutput, calls=%fused_computation.15 | convolution fusion | flops 5762580480 | bytes 17170432 | tf_op jit(solution)/shard_map/dot_general | solution.py:43
  399.6 8.6 out_grad.1
  429.1 40.6 %all-reduce.6 = (f32[]{:T(128)}, f32[]{:T(128)}, f32[2,5120]{1,0:T(2,128)S(1)}) all-reduce(f32[]{:T(128)} %bitcast.51, f32[]{:T(128)} %convert_element_type.136, f32[2,5120]{1,0:T(2,128)S(1)} %pad_maximum_fusion.6), channel_id=1, replica_groups=mesh['dp'=8,'sub'=4] {'dp','sub'}, use_global_device_ids=true, to_apply=%region_17.18 | all-reduce | flops 10242 | bytes 81936 | tf_op jit(solution)/shard_map/psum | solution.py:586
  479.2 86.9 %reduce-scatter.5.cloned.1.call-done = bf16[2,256,512]{2,1,0:T(8,128)(2,1)} async-done(((bf16[2,2048,512]{2,1,0:T(8,128)(2,1)}), bf16[2,256,512]{2,1,0:T(8,128)(2,1)}) %reduce-scatter.5.cloned.1.call-update) | async-done | bytes 524304 | tf_op jit(solution)/shard_map/reduce_scatter | solution.py:597
  566.1 99.4 %reduce-scatter.7.cloned.1.call-done = bf16[9,64,512]{2,1,0:T(8,128)(2,1)} async-done(((bf16[9,512,512]{2,1,0:T(8,128)(2,1)}), bf16[9,64,512]{2,1,0:T(8,128)(2,1)}) %reduce-scatter.7.cloned.1.call-update) | async-done | bytes 589840 | tf_op jit(solution)/shard_map/reduce_scatter | solution.py:600
  677.2 53.7 %reduce-scatter.11.cloned.1.call-done = bf16[256,128]{1,0:T(8,128)(2,1)} async-done(((bf16[2048,128]{1,0:T(8,128)(2,1)}), bf16[256,128]{1,0:T(8,128)(2,1)}) %reduce-scatter.11.cloned.1.call-update) | async-done | bytes 65552 | tf_op jit(solution)/shard_map/reduce_scatter | solution.py:537
  732.4 69.3 %reduce-scatter.9.cloned.1.call-done.x_ref = bf16[256,512]{1,0:T(8,128)(2,1)} async-done(((bf16[2048,512]{1,0:T(8,128)(2,1)}), bf16[256,512]{1,0:T(8,128)(2,1)}) %reduce-scatter.9.cloned.1.call-update) | async-done | bytes 262160 | tf_op jit(solution)/shard_map/reduce_scatter | solution.py:535
  802.6 21.1 %hidden_shard.1 = bf16[4,256,512]{2,1,0:T(8,128)(2,1)S(1)} custom-call(bf16[256,512]{1,0:T(8,128)(2,1)S(1)} %copy-done.1), custom_call_target="tpu_custom_call" | custom-call | tf_op jit(solution)/shard_map/hidden_shard/pallas_call | solution.py:107
  824.9 19.5 %all-reduce.13.cloned.1.call-done = (bf16[2,256,512]{2,1,0:T(8,128)(2,1)}, bf16[9,64,512]{2,1,0:T(8,128)(2,1)}) async-done(((bf16[2,256,512]{2,1,0:T(8,128)(2,1)}, bf16[9,64,512]{2,1,0:T(8,128)(2,1)}), (bf16[2,256,512]{2,1,0:T(8,128)(2,1)}, bf16[9,64,512]{2,1,0:T(8,128)(2,1)})) %all-reduce.13.cloned.1.call-update) | async-done | bytes 1114128 | tf_op jit(solution)/shard_map/psum | solution.py:596
  851.6 6.9 norms.1
  (446 shorter events, 232.3 us)
Async XLA Ops:
  7.2 83.2 %all-gather.4.cloned.1.call-start = ((), (), s32[]{:S(2)}) async-start(), calls=%async_computation.4 | async-start | bytes 4718592 | tf_op jit(solution)/shard_map/all_gather | solution.py:414
  10.5 161.8 %all-gather.6.cloned.1.call-start = ((), (), s32[]{:S(2)}) async-start(), calls=%async_computation.5 | async-start | bytes 5308416 | tf_op jit(solution)/shard_map/all_gather | solution.py:415
  12.2 223.3 %all-gather.8.cloned.1.call-start = ((), (), s32[]{:S(2)}) async-start(), calls=%async_computation.6 | async-start | bytes 2359296 | tf_op jit(solution)/shard_map/all_gather | solution.py:417
  14.1 461.4 %all-reduce.11.cloned.1.call-start = ((), (), s32[]{:S(2)}) async-start(), calls=%async_computation.11 | async-start | bytes 3145728 | tf_op jit(solution)/shard_map/psum | solution.py:586
  15.6 44.7 %copy-start.2 = (f32[3000,128]{0,1:T(8,128)}, f32[3000,128]{0,1:T(8,128)S(1)}, u32[]{:S(2)}) copy-start(f32[3000,128]{0,1:T(8,128)S(1)} %copy.113) | copy-start | bytes 4608004
  16.4 173.4 %copy-start.69 = (f32[1216]{0:T(1024)}, f32[1216]{0:T(1024)S(1)}, u32[]{:S(2)}) copy-start(f32[1216]{0:T(1024)S(1)} %broadcast_in_dim.33) | copy-start | bytes 14596
  22.9 38.5 %copy-start = (bf16[2,960,128]{2,1,0:T(8,128)(2,1)S(1)}, bf16[2,960,128]{2,1,0:T(8,128)(2,1)}, u32[]{:S(2)}) copy-start(bf16[2,960,128]{2,1,0:T(8,128)(2,1)} %queue_ref.3) | copy-start | bytes 1474564
  116.8 118.8 %copy-start.110 = (f32[256]{0:T(256)}, f32[256]{0:T(256)S(1)}, u32[]{:S(2)}) copy-start(f32[256]{0:T(256)S(1)} %mul.611) | copy-start | bytes 3076
  237.9 28.8 %copy-start.14 = (bf16[3000,128]{0,1:T(8,128)(2,1)S(1)}, bf16[3000,128]{0,1:T(8,128)(2,1)}, u32[]{:S(2)}) copy-start(bf16[3000,128]{0,1:T(8,128)(2,1)} %copy-done.13) | copy-start | bytes 2304004
  244.7 27.4 %copy-start.37 = (f32[256,512]{1,0:T(8,128)S(1)}, f32[256,512]{1,0:T(8,128)}, u32[]{:S(2)}) copy-start(f32[256,512]{1,0:T(8,128)} %copy-done.36) | copy-start | bytes 1572868
  244.7 27.4 %copy-start.105 = (f32[1,512]{1,0:T(1,128)S(1)}, f32[1,512]{1,0:T(1,128)}, u32[]{:S(2)}) copy-start(f32[1,512]{1,0:T(1,128)} %copy-done.104) | copy-start | bytes 6148
  245.4 26.7 %copy-start.79 = (f32[512]{0:T(512)S(1)}, f32[512]{0:T(512)}, u32[]{:S(2)}) copy-start(f32[512]{0:T(512)} %copy-done.78) | copy-start | bytes 6148
  245.4 26.7 %copy-start.82 = (f32[512]{0:T(512)S(1)}, f32[512]{0:T(512)}, u32[]{:S(2)}) copy-start(f32[512]{0:T(512)} %copy-done.81) | copy-start | bytes 6148
  245.4 26.7 %copy-start.103 = (f32[1,512]{1,0:T(1,128)S(1)}, f32[1,512]{1,0:T(1,128)}, u32[]{:S(2)}) copy-start(f32[1,512]{1,0:T(1,128)} %copy-done.102) | copy-start | bytes 6148
  345.1 220.9 %reduce-scatter.5.cloned.1.call-start = ((), (), s32[]{:S(2)}) async-start(), calls=%async_computation.7 | async-start | bytes 4718592 | tf_op jit(solution)/shard_map/reduce_scatter | solution.py:597
  386.5 279.0 %reduce-scatter.7.cloned.1.call-start = ((), (), s32[]{:S(2)}) async-start(), calls=%async_computation.8 | async-start | bytes 5308416 | tf_op jit(solution)/shard_map/reduce_scatter | solution.py:600
  398.5 332.5 %reduce-scatter.11.cloned.1.call-start = ((), (), s32[]{:S(2)}) async-start(), calls=%async_computation.10 | async-start | bytes 589824 | tf_op jit(solution)/shard_map/reduce_scatter | solution.py:537
  408.2 393.4 %reduce-scatter.9.cloned.1.call-start = ((), (), s32[]{:S(2)}) async-start(), calls=%async_computation.9 | async-start | bytes 2359296 | tf_op jit(solution)/shard_map/reduce_scatter | solution.py:535
  410.4 434.0 %all-reduce.13.cloned.1.call-start = ((), (), s32[]{:S(2)}) async-start(), calls=%async_computation.12 | async-start | bytes 2228224 | tf_op jit(solution)/shard_map/psum | solution.py:596
  422.5 47.4 %copy-start.76 = (f32[2,5120]{1,0:T(2,128)S(1)}, f32[2,5120]{1,0:T(2,128)}, u32[]{:S(2)}) copy-start(f32[2,5120]{1,0:T(2,128)} %param.43) | copy-start | bytes 122884
  422.5 47.4 %copy-start.77 = (f32[2,5120]{1,0:T(2,128)S(1)}, f32[2,5120]{1,0:T(2,128)}, u32[]{:S(2)}) copy-start(f32[2,5120]{1,0:T(2,128)} %param.37) | copy-start | bytes 122884
  422.6 53.0 %copy-start.3 = (f32[3000,128]{0,1:T(8,128)S(1)}, f32[3000,128]{0,1:T(8,128)}, u32[]{:S(2)}) copy-start(f32[3000,128]{0,1:T(8,128)} %copy-done.2) | copy-start | bytes 4608004
  422.6 52.9 %copy-start.60 = (f32[3000]{0:T(1024)S(1)}, f32[3000]{0:T(1024)}, u32[]{:S(2)}) copy-start(f32[3000]{0:T(1024)} %copy-done.59) | copy-start | bytes 36004
  677.2 170.5 %copy-start.112 = (f32[2]{0:T(128)S(1)}, f32[2]{0:T(128)}, u32[]{:S(2)}) copy-start(f32[2]{0:T(128)} %get-tuple-element.205) | copy-start | bytes 28
  (111 other events, 619.2 us)
Sparse Core Ops, SparseCore 0:
  10.8 79.5 all-gather.3
  93.1 79.1 all-gather.5
  175.1 47.4 all-gather.7
  345.3 130.1 all-reduce.10
  479.0 87.0 reduce-scatter.4
  570.0 95.3 reduce-scatter.6
  669.2 61.6 reduce-scatter.10
  735.0 66.6 reduce-scatter.8
  804.2 40.1 all-reduce.12

commit v2 on v1

--- a/solution.py
+++ b/solution.py
@@ -119,6 +119,423 @@
             ),
             name=name,
         )(values)
+
+
+class Links:
+    def __init__(self, send_sem, recv_sem):
+        self.send_sem = send_sem
+        self.recv_sem = recv_sem
+        self.used = 0
+
+    def __call__(self, source, target, device):
+        copy = pltpu.make_async_remote_copy(
+            src_ref=source,
+            dst_ref=target,
+            send_sem=self.send_sem.at[self.used],
+            recv_sem=self.recv_sem.at[self.used],
+            device_id=device,
+            device_id_type=MESH,
+        )
+        self.used += 1
+        copy.start()
+        return copy
+
+
+def wait_all(copies):
+    for copy in copies:
+        copy.wait()
+
+
+def lanes_of(index, width=LANES):
+    return pl.ds(pl.multiple_of(index * width, LANES), width)
+
+
+class Place:
+    def __init__(self, n_dp):
+        self.n_dp = n_dp
+        self.span = n_dp // 2
+        dp, self.sub = lax.axis_index("dp"), lax.axis_index("sub")
+        self.dp = dp
+        self.near, self.far = dp // 2, dp % 2
+        row, core = self.sub // 2, self.sub % 2
+        self.row, self.core = row, core
+        self.row_sub = 2 * (1 - row) + core
+        self.core_sub = 2 * row + (1 - core)
+        self.far_peer = {"dp": self.near * 2 + (1 - self.far)}
+        self.row_peer = {"sub": self.row_sub}
+        self.core_peer = {"sub": self.core_sub}
+
+    def near_index(self, hop):
+        return (self.near + hop) % self.span
+
+    def near_peer(self, hop):
+        return {"dp": self.near_index(hop) * 2 + self.far}
+
+    def dp_peers(self):
+        return [{"dp": (self.dp + hop) % self.n_dp} for hop in range(1, self.n_dp)]
+
+    def sub_peers(self):
+        return [{"sub": (self.sub + hop) % 4} for hop in range(1, 4)]
+
+    def greet(self, peers):
+        barrier = pltpu.get_barrier_semaphore()
+        for peer in peers:
+            pl.semaphore_signal(barrier, inc=1, device_id=peer, device_id_type=MESH)
+        pl.semaphore_wait(barrier, len(peers))
+
+
+ALL = slice(None)
+
+
+def gather_kernel(n_dp, *refs):
+    w_first, w_mid, w_last, w_hid, w_out = refs[:5]
+    o_first, o_mid, o_last, o_hid, o_out = refs[5:10]
+    send_sem, recv_sem, own_sem = refs[10:]
+    at = Place(n_dp)
+    links = Links(send_sem, recv_sem)
+    at.greet(
+        [at.near_peer(hop) for hop in range(1, at.span)]
+        + [at.far_peer, at.row_peer, at.core_peer]
+    )
+    mine, beside = lanes_of(at.sub), lanes_of(at.row_sub)
+
+    def flat(source, target, split):
+        return (
+            lambda cols: source.at[:, cols],
+            lambda near, far, cols: target.at[near, far, :, cols],
+            split,
+        )
+
+    def taps(start):
+        some = pl.ds(start, 3)
+        return (
+            lambda cols: w_mid.at[some, :, cols],
+            lambda near, far, cols: o_mid.at[some, near, far, :, cols],
+            True,
+        )
+
+    pieces = [
+        flat(w_first, o_first, True),
+        taps(0),
+        taps(3),
+        taps(6),
+        flat(w_last, o_last, True),
+        flat(w_hid, o_hid, False),
+        flat(w_out, o_out, False),
+    ]
+    count = len(pieces)
+    own, first, second, third, fourth = [], [], [], [], []
+    for index, (source, target, split) in enumerate(pieces):
+        cols = mine if split else ALL
+        copy = pltpu.make_async_copy(source(cols), target(at.near, at.far, cols), own_sem.at[index])
+        copy.start()
+        own.append(copy)
+    for source, target, split in pieces:
+        cols = mine if split else ALL
+        first.append(
+            [
+                links(source(cols), target(at.near, at.far, cols), at.near_peer(hop))
+                for hop in range(1, at.span)
+            ]
+        )
+    for tick in range(count + 2):
+        if tick < count:
+            source, target, split = pieces[tick]
+            cols = mine if split else ALL
+            own[tick].wait()
+            wait_all(first[tick])
+            slab = target(ALL, at.far, cols)
+            second.append(links(slab, slab, at.far_peer))
+        if 1 <= tick < count + 1:
+            source, target, split = pieces[tick - 1]
+            second[tick - 1].wait()
+            if split:
+                slab = target(ALL, ALL, mine)
+                third.append(links(slab, slab, at.row_peer))
+            else:
+                third.append(None)
+        if tick >= 2:
+            source, target, split = pieces[tick - 2]
+            if split:
+                third[tick - 2].wait()
+                for cols in (mine, beside):
+                    slab = target(ALL, ALL, cols)
+                    fourth.append(links(slab, slab, at.core_peer))
+    wait_all(fourth)
+
+
+def gather_weights(n_dp, collective_id, first, mid, last, hid, out):
+    span = n_dp // 2
+    rows, middle = first.shape
+    some = jax.ShapeDtypeStruct
+    low = jnp.bfloat16
+    copies = 7 * (span + 4)
+    return pl.pallas_call(
+        functools.partial(gather_kernel, n_dp),
+        out_shape=(
+            some((span, 2, rows, middle), low),
+            some((TAPS, span, 2, mid.shape[1], middle), low),
+            some((span, 2, rows, middle), low),
+            some((span, 2, rows, hid.shape[1]), low),
+            some((span, 2, rows, out.shape[1]), low),
+        ),
+        in_specs=[pl.BlockSpec(memory_space=pltpu.VMEM)] * 5,
+        out_specs=(pl.BlockSpec(memory_space=pl.ANY),) * 5,
+        scratch_shapes=[
+            pltpu.SemaphoreType.DMA((copies,)),
+            pltpu.SemaphoreType.DMA((copies,)),
+            pltpu.SemaphoreType.DMA((7,)),
+        ],
+        compiler_params=pltpu.CompilerParams(
+            collective_id=collective_id, has_side_effects=True, vmem_limit_bytes=48 * MIB
+        ),
+        name="gather_weights",
+    )(first, mid, last, hid, out)
+
+
+def plus(left, right):
+    return left.astype(jnp.float32) + right.astype(jnp.float32)
+
+
+def reduce_kernel(n_dp, *refs):
+    g_first, g_mid, g_last, g_hid, g_out, g_vec = refs[:6]
+    o_first, o_mid, o_last, o_hid, o_out, o_vec = refs[6:12]
+    bufs = refs[12:-9]
+    hid_in, hid_sum, hid_land, out_in, out_sum, out_land, vec_land, send_sem, recv_sem = refs[-9:]
+    at = Place(n_dp)
+    links = Links(send_sem, recv_sem)
+    span = at.span
+    at.greet(at.dp_peers() + at.sub_peers())
+    low = jnp.bfloat16
+    wide = g_vec.shape[1] // 4
+    vec_cols = lanes_of(at.sub, wide)
+    vec_copies = [
+        links(g_vec.at[:, vec_cols], vec_land.at[hop], peer)
+        for hop, peer in enumerate(at.dp_peers())
+    ]
+    pieces = [(g_last, o_last, 0, 1), (g_mid, o_mid, 0, 3), (g_mid, o_mid, 3, 3), (g_mid, o_mid, 6, 3), (g_first, o_first, 0, 1)]
+    count = len(pieces)
+    mine, beside = lanes_of(at.sub), lanes_of(at.row_sub)
+
+    pair = []
+    for index, (source, target, start, taps) in enumerate(pieces):
+        land = bufs[4 * index]
+        sent = []
+        for row in range(2):
+            cols = lanes_of(2 * row + (1 - at.core))
+            sent.append(
+                links(source.at[pl.ds(start, taps), :, :, :, cols], land.at[row], at.core_peer)
+            )
+        pair.append(sent)
+
+    wholes = [(g_hid, hid_in, hid_sum, hid_land), (g_out, out_in, out_sum, out_land)]
+    far_copies = [
+        links(source.at[:, 1 - at.far], landed, at.far_peer)
+        for source, landed, total, land in wholes
+    ]
+
+    def whole_far(which):
+        source, landed, total, land = wholes[which]
+        far_copies[which].wait()
+        for near in range(span):
+            total[near] = plus(source[near, at.far], landed[near]).astype(low)
+        return [
+            links(total.at[at.near_index(hop)], land.at[hop - 1], at.near_peer(hop))
+            for hop in range(1, span)
+        ]
+
+    def whole_near(which, copies):
+        source, landed, total, land = wholes[which]
+        wait_all(copies)
+        value = total[at.near].astype(jnp.float32)
+        for hop in range(1, span):
+            value = value + land[hop - 1].astype(jnp.float32)
+        return value.astype(low)
+
+    def blocks(taps, body):
+        def step(index, carry):
+            rest = index // 2
+            body(rest // span, rest % span, index % 2)
+            return carry
+
+        lax.fori_loop(0, taps * span * 2, step, 0)
+
+    def lines(taps, body):
+        def step(index, carry):
+            body(index // span, index % span)
+            return carry
+
+        lax.fori_loop(0, taps * span, step, 0)
+
+    def stage_pair(index):
+        source, target, start, taps = pieces[index]
+        land = bufs[4 * index]
+        wait_all(pair[index])
+        for row in range(2):
+            cols = lanes_of(2 * row + at.core)
+
+            def body(tap, near, far):
+                land[row, tap, near, far] = plus(
+                    source[start + tap, near, far, :, cols], land[row, tap, near, far]
+                ).astype(low)
+
+            blocks(taps, body)
+        if index % 2 == 0:
+            return links(land.at[1 - at.row], bufs[4 * index + 1], at.row_peer)
+        return links(land.at[:, :, :, 1 - at.far], bufs[4 * index + 1], at.far_peer)
+
+    def stage_second(index, copy):
+        source, target, start, taps = pieces[index]
+        held, land, total = bufs[4 * index], bufs[4 * index + 1], bufs[4 * index + 2]
+        copy.wait()
+        if index % 2 == 0:
+
+            def body(tap, near, far):
+                land[tap, near, far] = plus(
+                    held[at.row, tap, near, far], land[tap, near, far]
+                ).astype(low)
+
+            blocks(taps, body)
+            return links(land.at[:, :, 1 - at.far], total, at.far_peer)
+        for row in range(2):
+
+            def body(tap, near):
+                land[row, tap, near] = plus(
+                    held[row, tap, near, at.far], land[row, tap, near]
+                ).astype(low)
+
+            lines(taps, body)
+        return links(land.at[1 - at.row], total, at.row_peer)
+
+    def stage_third(index, copy):
+        source, target, start, taps = pieces[index]
+        held, total, land = bufs[4 * index + 1], bufs[4 * index + 2], bufs[4 * index + 3]
+        copy.wait()
+
+        def body(tap, near):
+            part = held[tap, near, at.far] if index % 2 == 0 else held[at.row, tap, near]
+            total[tap, near] = plus(part, total[tap, near]).astype(low)
+
+        lines(taps, body)
+        return [
+            links(total.at[:, at.near_index(hop)], land.at[hop - 1], at.near_peer(hop))
+            for hop in range(1, span)
+        ]
+
+    def stage_near(index, copies):
+        source, target, start, taps = pieces[index]
+        total, land = bufs[4 * index + 2], bufs[4 * index + 3]
+        wait_all(copies)
+        for tap in range(taps):
+            value = total[tap, at.near].astype(jnp.float32)
+            for hop in range(1, span):
+                value = value + land[hop - 1, tap].astype(jnp.float32)
+            target[start + tap, :, mine] = value.astype(low)
+        slab = target.at[pl.ds(start, taps), :, mine]
+        return links(slab, slab, at.row_peer)
+
+    def stage_row(index, copy):
+        source, target, start, taps = pieces[index]
+        copy.wait()
+        sent = []
+        for cols in (mine, beside):
+            slab = target.at[pl.ds(start, taps), :, cols]
+            sent.append(links(slab, slab, at.core_peer))
+        return sent
+
+    hold = {}
+    final = []
+    for tick in range(count + 4):
+        if tick < count:
+            hold[0, tick] = stage_pair(tick)
+        if tick == 0:
+            near_hid = whole_far(0)
+            near_out = whole_far(1)
+        if 0 <= tick - 1 < count:
+            hold[1, tick - 1] = stage_second(tick - 1, hold[0, tick - 1])
+        if 0 <= tick - 2 < count:
+            hold[2, tick - 2] = stage_third(tick - 2, hold[1, tick - 2])
+        if tick == 2:
+            o_hid[at.sub] = whole_near(0, near_hid)
+            hid_row = links(o_hid.at[at.sub], o_hid.at[at.sub], at.row_peer)
+            o_out[...] = whole_near(1, near_out)
+            wait_all(vec_copies)
+            value = g_vec[:, vec_cols]
+            for hop in range(n_dp - 1):
+                value = value + vec_land[hop]
+            o_vec[:, vec_cols] = value
+            vec_final = [
+                links(o_vec.at[:, vec_cols], o_vec.at[:, vec_cols], peer)
+                for peer in at.sub_peers()
+            ]
+        if 0 <= tick - 3 < count:
+            hold[3, tick - 3] = stage_near(tick - 3, hold[2, tick - 3])
+        if tick == 3:
+            hid_row.wait()
+            for which in (at.sub, at.row_sub):
+                final.append(links(o_hid.at[which], o_hid.at[which], at.core_peer))
+        if 0 <= tick - 4 < count:
+            final += stage_row(tick - 4, hold[3, tick - 4])
+    wait_all(final)
+    wait_all(vec_final)
+
+
+def reduce_gradients(n_dp, collective_id, first, mid, last, hid, out, vec):
+    span = n_dp // 2
+    low = jnp.bfloat16
+    rows = first.shape[0] // n_dp
+    mid_rows = mid.shape[1] // n_dp
+    wide, narrow = first.shape[1], out.shape[1]
+    some = jax.ShapeDtypeStruct
+    bufs = []
+    for index in range(5):
+        taps, height = (3, mid_rows) if 1 <= index <= 3 else (1, rows)
+        block = (height, LANES)
+        bufs.append(pltpu.VMEM((2, taps, span, 2) + block, low))
+        if index % 2 == 0:
+            bufs.append(pltpu.VMEM((taps, span, 2) + block, low))
+        else:
+            bufs.append(pltpu.VMEM((2, taps, span) + block, low))
+        bufs.append(pltpu.VMEM((taps, span) + block, low))
+        bufs.append(pltpu.VMEM((span - 1, taps) + block, low))
+    copies = 5 * (span + 8) + 2 * (span + 2) + n_dp + 8
+    results = pl.pallas_call(
+        functools.partial(reduce_kernel, n_dp),
+        out_shape=(
+            some((1, rows, wide), low),
+            some((TAPS, mid_rows, wide), low),
+            some((1, rows, wide), low),
+            some((4, rows, hid.shape[1]), low),
+            some((rows, narrow), low),
+            some(vec.shape, vec.dtype),
+        ),
+        in_specs=[pl.BlockSpec(memory_space=pltpu.VMEM)] * 6,
+        out_specs=(pl.BlockSpec(memory_space=pltpu.VMEM),) * 6,
+        scratch_shapes=bufs
+        + [
+            pltpu.VMEM((span, rows, hid.shape[1]), low),
+            pltpu.VMEM((span, rows, hid.shape[1]), low),
+            pltpu.VMEM((span - 1, rows, hid.shape[1]), low),
+            pltpu.VMEM((span, rows, narrow), low),
+            pltpu.VMEM((span, rows, narrow), low),
+            pltpu.VMEM((span - 1, rows, narrow), low),
+            pltpu.VMEM((n_dp - 1, vec.shape[0], vec.shape[1] // 4), jnp.float32),
+            pltpu.SemaphoreType.DMA((copies,)),
+            pltpu.SemaphoreType.DMA((copies,)),
+        ],
+        compiler_params=pltpu.CompilerParams(
+            collective_id=collective_id, has_side_effects=True, vmem_limit_bytes=56 * MIB
+        ),
+        name="reduce_gradients",
+    )(
+        first.reshape(1, span, 2, rows, wide),
+        mid.reshape(TAPS, span, 2, mid_rows, wide),
+        last.reshape(1, span, 2, rows, wide),
+        hid.reshape(span, 2, rows, hid.shape[1]),
+        out.reshape(span, 2, rows, narrow),
+        vec,
+    )
+    return results
 
 
 def row_tile(rows):
@@ -399,7 +816,7 @@
     avg_protos,
     avg_norms,
 ):
-    n_sub = sizes["sub"]
+    n_dp, n_sub = sizes["dp"], sizes["sub"]
     exchange = Exchanger(sizes)
     images = big_maps.shape[0]
     channels = big_maps.shape[-1]
@@ -411,14 +828,22 @@
     here = lax.axis_index("sub")
     share = hidden_width // n_sub
 
-    outer_low = lax.all_gather(bottleneck_outer.astype(jnp.bfloat16), "dp", axis=1, tiled=True)
-    inner_low = lax.all_gather(bottleneck_inner.astype(jnp.bfloat16), "dp", axis=1, tiled=True)
+    low = jnp.bfloat16
     hidden_cols = lax.dynamic_slice_in_dim(proj_hidden, here * share, share, 1)
-    hidden_low = lax.all_gather(hidden_cols.astype(jnp.bfloat16), "dp", axis=0, tiled=True)
-    out_low = lax.all_gather(proj_out.astype(jnp.bfloat16), "dp", axis=0, tiled=True)
-    out_low = lax.dynamic_slice_in_dim(out_low, here * share, share, 0)
-    first_w = outer_low[0]
-    last_w = outer_low[1]
+    first_w, inner_low, last_w, hidden_low, out_low = gather_weights(
+        n_dp,
+        exchange.next_id(),
+        bottleneck_outer[0].astype(low),
+        bottleneck_inner.astype(low),
+        bottleneck_outer[1].astype(low),
+        hidden_cols.astype(low),
+        proj_out.astype(low),
+    )
+    first_w = first_w.reshape(channels, middle)
+    last_w = last_w.reshape(channels, middle)
+    hidden_low = hidden_low.reshape(channels, share)
+    out_low = lax.dynamic_slice_in_dim(out_low.reshape(hidden_width, out_width), here * share, share, 0)
+    inner_low = inner_low.reshape(TAPS, middle, middle)
     middle_w = inner_low.reshape(TAPS * middle, middle)
     middle_t = jnp.transpose(inner_low, (0, 2, 1)).reshape(TAPS * middle, middle)
 
@@ -532,24 +957,23 @@
     grad_pooled = exchange(partial, "sub", scatter=True, name="pooled_grad")
     grad_pooled = jnp.sum(grad_pooled.astype(jnp.float32), 0)
 
-    hidden_sum = lax.psum_scatter(d_hidden.astype(jnp.bfloat16), "dp", scatter_dimension=0, tiled=True)
-    out_group = exchange(d_out.astype(jnp.bfloat16), "sub", name="out_grad")
-    out_sum = lax.psum_scatter(
-        out_group.reshape(hidden_width, out_width), "dp", scatter_dimension=0, tiled=True
-    )
-    shard_hidden = exchange(hidden_sum, "sub", name="hidden_shard")
-    shard_hidden = jnp.transpose(shard_hidden, (1, 0, 2)).reshape(-1, hidden_width)
-    shard_hidden = shard_hidden.astype(jnp.float32)
-    shard_out = out_sum.astype(jnp.float32)
+    out_group = exchange(d_out.astype(low), "sub", name="out_grad").reshape(hidden_width, out_width)
+    four = exchange(
+        jnp.stack([gain_four, bias_four, jnp.broadcast_to(loss_tile[0, 0], (share,))]),
+        "sub",
+        name="sums_four",
+    )
+    gain_four, bias_four = four[:, 0].reshape(-1), four[:, 1].reshape(-1)
+    loss_group = jnp.sum(four[:, 2, 0])
+    centers_sum = lax.psum(grad_centers, ("dp", "sub"))[:proto_count]
 
     def norm_back(grad_out, normal, inv_std, gain_vec, name):
-        bias_local = jnp.sum(grad_out, 0)
-        gain_local = jnp.sum(grad_out * normal, 0)
-        both = jnp.sum(exchange(jnp.stack([bias_local, gain_local]), "sub", name=name), 0)
+        both = jnp.stack([jnp.sum(grad_out, 0), jnp.sum(grad_out * normal, 0)])
+        both = jnp.sum(exchange(both, "sub", name=name), 0)
         grad_in = (
             gain_vec * inv_std * (grad_out - row_mask * (both[0] + normal * both[1]) / count_all)
         )
-        return grad_in.astype(jnp.bfloat16), gain_local, bias_local
+        return grad_in.astype(jnp.bfloat16), both[1], both[0]
 
     grad_summed = spread_crops(grad_pooled, images) * silu_slope(summed)
     three_low, gain_three, bias_three = norm_back(
@@ -567,54 +991,59 @@
     )
     d_first = cross_rows(inputs, one_low)
 
-    wide_four = jnp.zeros((2, hidden_width), jnp.float32)
-    wide_four = lax.dynamic_update_slice(
-        wide_four, jnp.stack([gain_four, bias_four]), (0, here * share)
-    )
-    grad_norms = jnp.concatenate(
+    vector = jnp.concatenate(
         [
+            gain_one, gain_two, gain_three, gain_four, bias_one, bias_two, bias_three, bias_four,
             jnp.stack(
                 [
-                    jnp.concatenate([gain_one, gain_two, gain_three]),
-                    jnp.concatenate([bias_one, bias_two, bias_three]),
+                    loss_group,
+                    jnp.sum(lives),
+                    jnp.sum(bottleneck_outer[0] * bottleneck_outer[0]),
+                    jnp.sum(bottleneck_outer[1] * bottleneck_outer[1]),
+                    jnp.sum(bottleneck_inner * bottleneck_inner),
+                    jnp.sum(proj_hidden * proj_hidden),
+                    jnp.sum(proj_out * proj_out),
                 ]
             ),
-            wide_four,
-        ],
-        1,
-    )
-    centers_sum, norm_sum, numer_all, live_all = lax.psum(
-        (grad_centers, grad_norms, loss_tile[0, 0], live_float), ("dp", "sub")
-    )
-    centers_sum = centers_sum[:proto_count]
+        ]
+    )
+    vec_width = -(-vector.shape[0] // 4096) * 512
+    vector = jnp.pad(vector, (0, 8 * vec_width - vector.shape[0])).reshape(8, vec_width)
+    shard_first, shard_inner, shard_last, shard_hidden, shard_out, vector = reduce_gradients(
+        n_dp,
+        exchange.next_id(),
+        d_first.astype(low),
+        d_middle.astype(low).reshape(TAPS, middle, middle),
+        d_last.astype(low),
+        d_hidden.astype(low),
+        out_group,
+        vector,
+    )
+    shard_outer = jnp.concatenate([shard_first, shard_last], 0).astype(jnp.float32)
+    shard_inner = shard_inner.astype(jnp.float32)
+    shard_hidden = jnp.transpose(shard_hidden, (1, 0, 2)).reshape(-1, hidden_width)
+    shard_hidden = shard_hidden.astype(jnp.float32)
+    shard_out = shard_out.astype(jnp.float32)
+    vector = vector.reshape(-1)
+    norms = norm_params.shape[1]
+    norm_sum = vector[: 2 * norms].reshape(2, norms)
+    numer_all, live_all = vector[2 * norms], vector[2 * norms + 1]
+    weight_all = vector[2 * norms + 2 : 2 * norms + 7]
     proto_unit = prototypes * proto_inv
     proto_sum = proto_inv * (
         centers_sum - proto_unit * jnp.sum(proto_unit * centers_sum, 1, keepdims=True)
     )
-    grad_outer = jnp.stack([d_first, d_last]).astype(jnp.bfloat16)
-    grad_inner = d_middle.reshape(TAPS, middle, middle).astype(jnp.bfloat16)
-    shard_outer = lax.psum(
-        lax.psum_scatter(grad_outer, "dp", scatter_dimension=1, tiled=True), "sub"
-    ).astype(jnp.float32)
-    shard_inner = lax.psum(
-        lax.psum_scatter(grad_inner, "dp", scatter_dimension=1, tiled=True), "sub"
-    ).astype(jnp.float32)
 
     squares = jnp.concatenate(
         [
-            jnp.sum(bottleneck_outer * bottleneck_outer, (1, 2)),
-            jnp.sum(bottleneck_inner * bottleneck_inner)[None],
-            jnp.sum(proj_hidden * proj_hidden)[None],
-            jnp.sum(proj_out * proj_out)[None],
             jnp.sum(shard_outer * shard_outer, (1, 2)),
             jnp.sum(shard_inner * shard_inner)[None],
             jnp.sum(shard_hidden * shard_hidden)[None],
             jnp.sum(shard_out * shard_out)[None],
         ]
     )
-    squares = jnp.broadcast_to(jnp.pad(squares, (0, 6))[:, None], (16, LANES))
-    squares = jnp.sum(exchange(squares, "dp", name="norms"), 0)[:, 0]
-    weight_all, grad_all = squares[:5], squares[5:10]
+    squares = jnp.broadcast_to(jnp.pad(squares, (0, 3))[:, None], (8, LANES))
+    grad_all = jnp.sum(exchange(squares, "dp", name="norms"), 0)[:5, 0]
     trusts = trust_rate * jnp.sqrt(weight_all) / (jnp.sqrt(grad_all) + 1e-12)
     proto_trust = (
         trust_rate

time: 901 us -> 577 us (0.64)
  waiting for transfers between devices: 403 us -> 0.02 us
  Pallas kernels: 121 us -> 296 us
  blocking collectives: 77.3 us -> 0 us
  local copies, waits for them, and re-layouts: 106 us -> 85.6 us
    reduce_scatter x4 -> x0, waiting for transfers between devices: 309 us -> none  [the longest x1 99.4 us: per_device(): lax.psum_scatter(grad_inner, 'dp', scatter_dimension=1, tiled=True)]
    pallas_call x0 -> x2, Pallas kernels: none -> 189 us  [the longest x1 107 us: reduce_gradients(): pl.pallas_call(functools.partial(reduce_kernel, n_dp), out_shape=(some((1...]
    all_gather x3 -> x0, waiting for transfers between devices: 69.5 us -> none  [the longest x1 45.2 us: per_device(): lax.all_gather(bottleneck_inner.astype(jnp.bfloat16), 'dp', axis=1, tiled...]
    psum x1 -> x0, blocking collectives: 40.6 us -> none  [per_device(): lax.psum((grad_centers, grad_norms, loss_tile[0, 0], live_float), ('dp',...]
    all_gather x1 -> x0, blocking collectives: 36.7 us -> none  [per_device(): lax.all_gather(proj_out.astype(jnp.bfloat16), 'dp', axis=0, tiled=True)]
    psum x2 -> x1, waiting for transfers between devices: 24.4 us -> 0.01 us  [per_device(): centers_sum = lax.psum(grad_centers, ('dp', 'sub'))[:proto_count]]
    unnamed x293 -> x255, local copies, waits for them, and re-layouts: 67.8 us -> 50.5 us
    pallas_call x13, Pallas kernels: 95 us -> 80.8 us  [__call__(): pl.pallas_call(functools.partial(exchange_kernel, axis, count, scatter),...]
  transfers between devices with their start and end apart: 9 -> 1, of which waited for: 8 -> 0; matrix products, arithmetic and copies ran while one was open for 19% -> 26% of each run, Pallas kernels for 7% -> 28%
where the time goes in v2:
time: 577 us; the launch traced here: 568 us
  Pallas kernels  296 us (51%)
  other arithmetic  87.8 us (15%)
  local copies, waits for them, and re-layouts  85.6 us (15%)
  matrix products  78.9 us (14%)
  between operations  19.6 us (3%)
    pallas_call x1, Pallas kernels, reduce_gradients(): pl.pallas_call(functools.partial(reduce_kernel, n_dp), out_shape=(some((1...  107 us
    pallas_call x1, Pallas kernels, gather_weights(): pl.pallas_call(functools.partial(gather_kernel, n_dp), out_shape=(some((s...  81.4 us
    pallas_call x13, Pallas kernels, __call__(): pl.pallas_call(functools.partial(exchange_kernel, axis, count, scatter),...  80.8 us
    unnamed x255, local copies, waits for them, and re-layouts  50.5 us
    dot_general x7, matrix products, forward_dot(): return jnp.dot(left, right, preferred_element_type=jnp.float32)  40.8 us
    dot_general x6, matrix products, cross_rows(): lax.dot_general(left, right, (((0,), (0,)), ((), ())), preferred_element_...  27 us
    pallas_call x1, Pallas kernels, sinkhorn(): pl.pallas_call(functools.partial(sinkhorn_kernel, 'sub', count, protos),...  21.8 us
    add x6, other arithmetic, advance(): average_new = average_rate * average + (1.0 - average_rate) * weight_new  14.3 us
  transfers between devices with their start and end apart: 1, of which 0 were waited for; matrix products, arithmetic and copies ran while one was open for 26% of the time, Pallas kernels for 28%

profile of v2, /device:TPU:0, one launch (start us, length us, event | category | flops | bytes accessed | tf_op | source)
XLA Modules:
  0.0 568.1 jit_solution(10812805793814231376)
XLA Ops:
  18.8 81.4 %gather_weights.1 = (bf16[4,2,256,512]{3,2,1,0:T(8,128)(2,1)S(1)}, bf16[9,4,2,64,512]{4,3,2,1,0:T(8,128)(2,1)}, bf16[4,2,256,512]{3,2,1,0:T(8,128)(2,1)S(1)}, bf...) custom-call(bf16[256,512]{1,0:T(8,128)(2,1)S(1)} %get-tuple-element.201.refs_0_, ...), custom_call_target="tpu_custom_call" | custom-call | tf_op jit(solution)/shard_map/gather_weights/pallas_call | solution.py:273
  100.3 7.0 %multiply_reduce_fusion.3 = (f32[512]{0:T(512)S(1)}, f32[512]{0:T(512)S(1)}, f32[1216,512]{1,0:T(8,128)}) fusion(f32[1216]{0:T(1024)S(1)} %broadcast_in_dim.25, bf16[2048,512]{1,0:T(8,128)(2,1)S(1)} %bitcast.175, bf16[432,2048]{1,0:T(8,128)(2,1)S(1)} %bitcast.185, bf16[784,2048]{1,0:T(8,128)(2,1)} %bitcast.178), kind=kOutput, calls=%fused_computation.21 | convolution fusion | flops 2562587648 | bytes 9577216 | tf_op jit(solution)/shard_map/dot_general | solution.py:55
  122.6 12.1 %multiply_reduce_fusion.2 = (f32[512]{0:T(512)S(1)}, f32[512]{0:T(512)S(1)}, f32[1216,512]{1,0:T(8,128)}) fusion(f32[1216]{0:T(1024)S(1)} %broadcast_in_dim.25, bf16[4608,512]{1,0:T(8,128)(2,1)S(1)} %bitcast.198, bf16[432,4608]{1,0:T(8,128)(2,1)} %copy-done.58, bf16[784,4608]{1,0:T(8,128)(2,1)} %copy-done.48), kind=kOutput, calls=%fused_computation.19 | convolution fusion | flops 5762710528 | bytes 18424576 | tf_op jit(solution)/shard_map/dot_general | solution.py:55
  139.1 8.7 %multiply_reduce_fusion = (f32[2048]{0:T(1024)S(1)}, f32[2048]{0:T(1024)S(1)}, f32[1216,2048]{1,0:T(8,128)}) fusion(f32[1216]{0:T(1024)S(1)} %broadcast_in_dim.25, bf16[2048,512]{1,0:T(8,128)(2,1)S(1)} %bitcast.173, f32[1216,512]{1,0:T(8,128)} %get-tuple-element.260, f32[512]{0:T(512)S(1)} %bitcast.304, f32[512]{0:T(512)S(1)} %bitcast.277, ...), kind=kOutput, calls=%fused_computation.1 | convolution fusion | flops 2565697536 | bytes 14578432 | tf_op jit(solution)/shard_map/dot_general | solution.py:49
  152.5 7.2 %fusion.5 = f32[1216,2048]{1,0:T(8,128)S(1)} fusion(f32[2048]{0:T(1024)S(1)} %bitcast.251, f32[2048]{0:T(1024)S(1)} %bitcast.243, f32[1216,2048]{1,0:T(8,128)} %get-tuple-element.261, f32[2048]{0:T(1024)S(1)} %bitcast.246, f32[2048]{0:T(1024)S(1)} %bitcast.249, bf16[432,2048]{1,0:T(8,128)(2,1)} %bitcast.186, bf16[784,2048]{1,0:T(8,128)(2,1)} %bitcast.179), kind=kLoop, calls=%fused_computation.12 | loop fusion | flops 32374784 | bytes 24936448 | tf_op jit(solution)/shard_map/jit(silu)/mul | solution.py:919
  173.6 13.2 %pooled.1 = bf16[4,64,2048]{2,1,0:T(8,128)(2,1)S(1)} custom-call(bf16[64,2048]{1,0:T(8,128)(2,1)S(1)} %pad_maximum_fusion.5.x_ref), custom_call_target="tpu_custom_call" | custom-call | tf_op jit(solution)/shard_map/pooled/pallas_call | solution.py:107
  191.0 4.7 embedding.1
  198.1 4.7 column_sums.1.first_ref
  202.7 21.8 %sinkhorn.1 = (bf16[64,3072]{1,0:T(8,128)(2,1)S(1)}, f32[8,128]{1,0:T(8,128)S(1)}) custom-call(bf16[2,960,128]{2,1,0:T(8,128)(2,1)S(1)} %copy-done.1, bf16[128,3072]{1,0:T(8,128)(2,1)S(1)} %pad_bitcast_fusion.turned_ref, bf16[64,128]{1,0:T(8,128)(2,1)S(1)} %multiply_convert_fusion.11.unit_ref, f32[8,1]{1,0:T(8,128)S(1)} %fusion.43.live_ref, ...), custom_call_target="tpu_custom_call" | custom-call | tf_op jit(solution)/shard_map/sinkhorn/pallas_call | solution.py:720
  233.3 16.4 %pooled_grad.1 = bf16[4,64,2048]{2,1,0:T(8,128)(2,1)S(1)} custom-call(bf16[4,64,2048]{2,1,0:T(8,128)(2,1)S(1)} %bitcast.166), custom_call_target="tpu_custom_call" | custom-call | tf_op jit(solution)/shard_map/pooled_grad/pallas_call | solution.py:107
  253.8 7.5 %fusion.54 = (f32[2048]{0:T(1024)S(1)}, f32[2048]{0:T(1024)S(1)}, f32[1216,2048]{1,0:T(8,128)}) fusion(f32[2048]{0:T(1024)S(1)} %bitcast.244, f32[1216,2048]{1,0:T(8,128)S(1)} %bitcast.177, f32[2048]{0:T(1024)S(1)} %bitcast.247, bf16[432,2048]{1,0:T(8,128)(2,1)S(1)} %bitcast.188, bf16[784,2048]{1,0:T(8,128)(2,1)S(1)} %bitcast.180, f32[2048]{0:T(1024)S(1)} %bitcast.252, ...), kind=kLoop, calls=%fused_computation.251 | loop fusion | flops 52293632 | bytes 34914304 | tf_op jit(solution)/shard_map/reduce_sum | solution.py:971
  261.3 4.8 back_three.1
  266.3 9.4 %multiply_convert_fusion = bf16[1216,2048]{1,0:T(8,128)(2,1)S(1)} fusion(f32[1216,2048]{1,0:T(8,128)} %get-tuple-element.193, f32[1216,2048]{1,0:T(8,128)} %get-tuple-element.261, f32[]{:T(128)S(6)} %mul.579, f32[2048]{0:T(1024)S(1)} %bitcast.255, f32[2048]{0:T(1024)S(1)} %bitcast.253, f32[2048]{0:T(1024)S(1)} %bitcast.245, f32[2048]{0:T(1024)S(1)} %bitcast.248, ...), kind=kLoop, calls=%fused_computation.9 | loop fusion | flops 22413312 | bytes 24949508 | tf_op jit(solution)/shard_map/convert_element_type | solution.py:976
  275.8 5.4 fusion.56
  289.1 10.9 %convolution_convert_fusion = bf16[4608,512]{1,0:T(8,128)(2,1)} fusion(bf16[1216,512]{1,0:T(8,128)(2,1)S(1)} %multiply_convert_fusion.2, bf16[432,4608]{1,0:T(8,128)(2,1)S(1)} %copy-done.59, bf16[784,4608]{1,0:T(8,128)(2,1)} %copy-done.48), kind=kOutput, calls=%fused_computation.15 | convolution fusion | flops 5762580480 | bytes 17170432 | tf_op jit(solution)/shard_map/dot_general | solution.py:43
  300.0 4.7 convolution_convert_fusion.2
  317.5 6.8 %copy.97 = bf16[9,512,512]{1,2,0:T(8,128)(2,1)} copy(bf16[9,512,512]{2,1,0:T(8,128)(2,1)} %bitcast.195) | data formatting | bytes 9437184 | tf_op jit(solution)/shard_map/reshape | solution.py:846
  334.9 13.3 %fusion.55 = (f32[512]{0:T(512)S(1)}, f32[512]{0:T(512)S(1)}, f32[1216,512]{1,0:T(8,128)}) fusion(f32[512]{0:T(512)S(1)} %bitcast.268, f32[1216,512]{1,0:T(8,128)S(1)} %copy-done.25, f32[512]{0:T(512)S(1)} %bitcast.271, f32[512]{0:T(512)S(1)} %bitcast.276, f32[512]{0:T(512)S(1)} %bitcast.274, bf16[4608,512]{1,0:T(8,128)(2,1)S(1)} %bitcast.202, ...), kind=kOutput, calls=%fused_computation.252 | convolution fusion | flops 5769559040 | bytes 20918272 | tf_op jit(solution)/shard_map/dot_general | solution.py:55
  352.0 7.9 %out_grad.1 = bf16[4,512,128]{2,1,0:T(8,128)(2,1)S(1)} custom-call(bf16[512,128]{1,0:T(8,128)(2,1)S(1)} %convolution_convert_fusion.5.x_ref), custom_call_target="tpu_custom_call" | custom-call | tf_op jit(solution)/shard_map/out_grad/pallas_call | solution.py:107
  360.7 4.6 concatenate.146
  365.9 7.5 %convolution_convert_fusion.3 = bf16[2048,512]{1,0:T(8,128)(2,1)} fusion(f32[1216,512]{1,0:T(8,128)} %get-tuple-element.267, f32[1216,512]{1,0:T(8,128)} %get-tuple-element.259, f32[512]{0:T(512)S(1)} %bitcast.296, f32[512]{0:T(512)S(1)} %bitcast.294, f32[]{:T(128)S(6)} %mul.579, f32[512]{0:T(512)S(1)} %bitcast.269, f32[512]{0:T(512)S(1)} %bitcast.272, ...), kind=kOutput, calls=%fused_computation.26 | convolution fusion | flops 2566750208 | bytes 12073732 | tf_op jit(solution)/shard_map/dot_general | solution.py:43
  373.5 107.4 %reduce_gradients.1 = (bf16[1,256,512]{2,1,0:T(8,128)(2,1)}, bf16[9,64,512]{2,1,0:T(8,128)(2,1)}, bf16[1,256,512]{2,1,0:T(8,128)(2,1)}, bf16[4,256,512]{2,1,0:T(...) custom-call(bf16[1,4,2,256,512]{4,3,2,1,0:T(8,128)(2,1)} %bitcast.224, bf16[9,4,2,64,512]{4,3,2,1,0:T(8,128)(2,1)} %bitcast.199, ...), custom_call_target="tpu_custom_call" | custom-call | tf_op jit(solution)/shard_map/reduce_gradients/pallas_call | solution.py:502
  492.2 6.9 %norms.1 = f32[8,8,128]{2,1,0:T(8,128)S(1)} custom-call(f32[8,128]{1,0:T(8,128)S(1)} %broadcast_in_dim.35.x_ref), custom_call_target="tpu_custom_call" | custom-call | tf_op jit(solution)/shard_map/norms/pallas_call | solution.py:107
  505.8 4.6 fusion.61
  (393 shorter events, 169.5 us)
Async XLA Ops:
  7.2 539.0 %all-reduce.9.cloned.1.call-start = ((), (), s32[]{:S(2)}) async-start(), calls=%async_computation | async-start | bytes 3145728 | tf_op jit(solution)/shard_map/psum | solution.py:968
  8.1 131.0 %copy-start.50 = (f32[1216]{0:T(1024)}, f32[1216]{0:T(1024)S(1)}, u32[]{:S(2)}) copy-start(f32[1216]{0:T(1024)S(1)} %broadcast_in_dim.25) | copy-start | bytes 14596
  14.5 85.8 %copy-start.8 = (bf16[3,3,6,8,2048]{4,3,2,1,0:T(8,128)(2,1)}, bf16[3,3,6,8,2048]{4,3,2,1,0:T(8,128)(2,1)S(1)}, u32[]{:S(2)}) copy-start(bf16[3,3,6,8,2048]{4,3,2,1,0:T(8,128)(2,1)S(1)} %copy.95) | copy-start | bytes 5308420
  100.2 12.1 %copy-start.38 = (f32[2,5120]{1,0:T(2,128)S(1)}, f32[2,5120]{1,0:T(2,128)}, u32[]{:S(2)}) copy-start(f32[2,5120]{1,0:T(2,128)} %param.31) | copy-start | bytes 122884
  113.0 26.1 %copy-start.87 = (f32[1,512]{1,0:T(1,128)}, f32[1,512]{1,0:T(1,128)S(1)}, u32[]{:S(2)}) copy-start(f32[1,512]{1,0:T(1,128)S(1)} %get-tuple-element.242) | copy-start | bytes 6148
  122.6 16.5 %copy-start.3 = (bf16[4,2,256,512]{3,2,1,0:T(8,128)(2,1)S(1)}, bf16[4,2,256,512]{3,2,1,0:T(8,128)(2,1)}, u32[]{:S(2)}) copy-start(bf16[4,2,256,512]{3,2,1,0:T(8,128)(2,1)} %copy-done.2) | copy-start | bytes 6291460
  168.1 19.3 %copy-start.84 = (f32[256]{0:T(256)}, f32[256]{0:T(256)S(1)}, u32[]{:S(2)}) copy-start(f32[256]{0:T(256)S(1)} %mul.618) | copy-start | bytes 3076
  232.3 18.9 %slice-start = ((s8[9961472]{0:T(1024)(128)(4,1)}), s8[1572864]{0:T(1024)(128)(4,1)S(1)}, s32[]{:S(2)}) async-start(s8[9961472]{0:T(1024)(128)(4,1)} %bitcast.176), calls=%async_computation.1 | async-start | bytes 3145728
  233.3 17.9 %slice-start.1 = ((s8[9961472]{0:T(1024)(128)(4,1)}), s8[4194304]{0:T(1024)(128)(4,1)S(1)}, s32[]{:S(2)}) async-start(s8[9961472]{0:T(1024)(128)(4,1)} %bitcast.176), calls=%async_computation.2 | async-start | bytes 8388608
  253.7 12.4 %copy-start.51 = (f32[1216]{0:T(1024)S(1)}, f32[1216]{0:T(1024)}, u32[]{:S(2)}) copy-start(f32[1216]{0:T(1024)} %copy-done.50) | copy-start | bytes 14596
  253.8 12.4 %copy-start.65 = (f32[1,2048]{1,0:T(1,128)S(1)}, f32[1,2048]{1,0:T(1,128)}, u32[]{:S(2)}) copy-start(f32[1,2048]{1,0:T(1,128)} %get-tuple-element.190) | copy-start | bytes 24580
  266.2 9.5 %copy-start.56 = (f32[1,2048]{1,0:T(1,128)}, f32[1,2048]{1,0:T(1,128)S(1)}, u32[]{:S(2)}) copy-start(f32[1,2048]{1,0:T(1,128)S(1)} %get-tuple-element.249) | copy-start | bytes 24580
  266.2 9.5 %copy-start.4 = (bf16[4,2,256,512]{3,2,1,0:T(8,128)(2,1)S(1)}, bf16[4,2,256,512]{3,2,1,0:T(8,128)(2,1)}, u32[]{:S(2)}) copy-start(bf16[4,2,256,512]{3,2,1,0:T(8,128)(2,1)} %copy-done.2) | copy-start | bytes 6291460
  275.7 9.7 %copy-start.80 = (f32[1,512]{1,0:T(1,128)S(1)}, f32[1,512]{1,0:T(1,128)}, u32[]{:S(2)}) copy-start(f32[1,512]{1,0:T(1,128)} %get-tuple-element.187) | copy-start | bytes 6148
  288.8 11.2 %copy-start.11 = (bf16[1216,512]{1,0:T(8,128)(2,1)}, bf16[1216,512]{1,0:T(8,128)(2,1)S(1)}, u32[]{:S(2)}) copy-start(bf16[1216,512]{1,0:T(8,128)(2,1)S(1)} %multiply_convert_fusion.2) | copy-start | bytes 3735556
  288.8 11.2 %slice-start.5 = ((s8[4980736]{0:T(1024)(128)(4,1)}), s8[4194304]{0:T(1024)(128)(4,1)S(1)}, s32[]{:S(2)}) async-start(s8[4980736]{0:T(1024)(128)(4,1)} %bitcast.193), calls=%async_computation.6 | async-start | bytes 8388608
  289.1 10.9 %slice-start.6 = ((s8[4980736]{0:T(1024)(128)(4,1)}), s8[786432]{0:T(1024)(128)(4,1)S(1)}, s32[]{:S(2)}) async-start(s8[4980736]{0:T(1024)(128)(4,1)} %bitcast.193), calls=%async_computation.7 | async-start | bytes 1572864
  289.1 10.9 %copy-start.27 = (f32[1216,512]{1,0:T(8,128)S(1)}, f32[1216,512]{1,0:T(8,128)}, u32[]{:S(2)}) copy-start(f32[1216,512]{1,0:T(8,128)} %get-tuple-element.260) | copy-start | bytes 7471108
  334.9 25.8 %copy-start.57 = (f32[1,2048]{1,0:T(1,128)S(1)}, f32[1,2048]{1,0:T(1,128)}, u32[]{:S(2)}) copy-start(f32[1,2048]{1,0:T(1,128)} %copy-done.56) | copy-start | bytes 24580
  334.9 31.1 %copy-start.7 = (bf16[7,7,2,8,2048]{4,3,2,1,0:T(8,128)(2,1)S(1)}, bf16[7,7,2,8,2048]{4,3,2,1,0:T(8,128)(2,1)}, u32[]{:S(2)}) copy-start(bf16[7,7,2,8,2048]{4,3,2,1,0:T(8,128)(2,1)} %copy.94) | copy-start | bytes 9633796
  334.9 31.1 %copy-start.86 = (f32[1,512]{1,0:T(1,128)S(1)}, f32[1,512]{1,0:T(1,128)}, u32[]{:S(2)}) copy-start(f32[1,512]{1,0:T(1,128)} %get-tuple-element.184) | copy-start | bytes 6148
  373.5 108.8 %copy-start.39 = (f32[2,5120]{1,0:T(2,128)S(1)}, f32[2,5120]{1,0:T(2,128)}, u32[]{:S(2)}) copy-start(f32[2,5120]{1,0:T(2,128)} %param.31) | copy-start | bytes 122884
  481.7 21.4 %copy-start.41 = (f32[12288]{0:T(1024)}, f32[12288]{0:T(1024)S(1)}, u32[]{:S(2)}) copy-start(f32[12288]{0:T(1024)S(1)} %reshape.333) | copy-start | bytes 147460
  488.8 14.3 %copy-start.23 = (bf16[4,256,512]{2,1,0:T(8,128)(2,1)S(1)}, bf16[4,256,512]{2,1,0:T(8,128)(2,1)}, u32[]{:S(2)}) copy-start(bf16[4,256,512]{2,1,0:T(8,128)(2,1)} %get-tuple-element.48) | copy-start | bytes 3145732
  (85 other events, 384.3 us)
Sparse Core Ops, SparseCore 0:
  226.2 135.9 all-reduce.8

commit v3 on v2

--- a/solution.py
+++ b/solution.py
@@ -90,6 +90,57 @@
     own.wait()
     for copy in copies:
         copy.wait()
+
+
+def relay_kernel(scatter, x_ref, o_ref, *rest):
+    sub = lax.axis_index("sub")
+    row, core = sub // 2, sub % 2
+    row_sub, core_sub = 2 * (1 - row) + core, 2 * row + (1 - core)
+    barrier = pltpu.get_barrier_semaphore()
+    for peer in (row_sub, core_sub):
+        pl.semaphore_signal(barrier, inc=1, device_id={"sub": peer}, device_id_type=MESH)
+    pl.semaphore_wait(barrier, 2)
+    links = Links(*rest[-2:])
+    if scatter:
+        landed, summed, arrived = rest[:3]
+        pair = [
+            links(x_ref.at[2 * line + (1 - core)], landed.at[line], {"sub": core_sub})
+            for line in (1 - row, row)
+        ]
+        pair[0].wait()
+        summed[...] = plus(x_ref[2 * (1 - row) + core], landed[1 - row]).astype(summed.dtype)
+        over = links(summed, arrived, {"sub": row_sub})
+        pair[1].wait()
+        value = plus(x_ref[sub], landed[row])
+        over.wait()
+        o_ref[...] = value + arrived[...].astype(jnp.float32)
+    else:
+        over = links(x_ref, o_ref.at[sub], {"sub": row_sub})
+        pair = links(x_ref, o_ref.at[sub], {"sub": core_sub})
+        o_ref[sub] = x_ref[...]
+        over.wait()
+        last = links(o_ref.at[row_sub], o_ref.at[row_sub], {"sub": core_sub})
+        pair.wait()
+        last.wait()
+
+
+def relay(collective_id, values, scatter, name):
+    block = values.shape[1:] if scatter else values.shape
+    held = [pltpu.VMEM((2,) + block, values.dtype)] + [pltpu.VMEM(block, values.dtype)] * 2
+    return pl.pallas_call(
+        functools.partial(relay_kernel, scatter),
+        out_shape=jax.ShapeDtypeStruct(
+            block if scatter else (4,) + block, jnp.float32 if scatter else values.dtype
+        ),
+        in_specs=[pl.BlockSpec(memory_space=pltpu.VMEM)],
+        out_specs=pl.BlockSpec(memory_space=pltpu.VMEM),
+        scratch_shapes=(held if scatter else [])
+        + [pltpu.SemaphoreType.DMA((3,)), pltpu.SemaphoreType.DMA((3,))],
+        compiler_params=pltpu.CompilerParams(
+            collective_id=collective_id, has_side_effects=True, vmem_limit_bytes=32 * MIB
+        ),
+        name=name,
+    )(values)
 
 
 class Exchanger:
@@ -298,10 +349,13 @@
 
 
 def reduce_kernel(n_dp, *refs):
-    g_first, g_mid, g_last, g_hid, g_out, g_vec = refs[:6]
-    o_first, o_mid, o_last, o_hid, o_out, o_vec = refs[6:12]
-    bufs = refs[12:-9]
-    hid_in, hid_sum, hid_land, out_in, out_sum, out_land, vec_land, send_sem, recv_sem = refs[-9:]
+    g_first, g_mid, g_last, g_hid, g_some, g_vec = refs[:6]
+    o_first, o_mid, o_last, o_hid, o_out, o_vec, o_sq = refs[6:13]
+    bufs = refs[13:-13]
+    (
+        hid_in, hid_sum, hid_land, g_out, out_in, out_sum, out_land, vec_land, sq_mine, sq_land,
+        send_sem, recv_sem, own_sem,
+    ) = refs[-13:]
     at = Place(n_dp)
     links = Links(send_sem, recv_sem)
     span = at.span
@@ -317,6 +371,12 @@
     count = len(pieces)
     mine, beside = lanes_of(at.sub), lanes_of(at.row_sub)
 
+    some = g_some.shape[0]
+    block = g_out.at[pl.ds(at.sub * some, some)]
+    own_out = pltpu.make_async_copy(g_some, block, own_sem)
+    own_out.start()
+    out_copies = [links(g_some, block, peer) for peer in at.sub_peers()]
+
     pair = []
     for index, (source, target, start, taps) in enumerate(pieces):
         land = bufs[4 * index]
@@ -329,10 +389,7 @@
         pair.append(sent)
 
     wholes = [(g_hid, hid_in, hid_sum, hid_land), (g_out, out_in, out_sum, out_land)]
-    far_copies = [
-        links(source.at[:, 1 - at.far], landed, at.far_peer)
-        for source, landed, total, land in wholes
-    ]
+    far_copies = [links(g_hid.at[:, 1 - at.far], hid_in, at.far_peer)]
 
     def whole_far(which):
         source, landed, total, land = wholes[which]
@@ -422,6 +479,14 @@
             for hop in range(1, span)
         ]
 
+    sq_mine[0] = jnp.zeros_like(sq_mine[0])
+
+    def squares_of(matrix, value):
+        value = value.astype(jnp.float32)
+        line = jnp.sum(value * value, 0, keepdims=True)
+        for lane in range(0, line.shape[1], LANES):
+            sq_mine[0, pl.ds(matrix, 1), :] += line[:, lane : lane + LANES]
+
     def stage_near(index, copies):
         source, target, start, taps = pieces[index]
         total, land = bufs[4 * index + 2], bufs[4 * index + 3]
@@ -430,7 +495,9 @@
             value = total[tap, at.near].astype(jnp.float32)
             for hop in range(1, span):
                 value = value + land[hop - 1, tap].astype(jnp.float32)
-            target[start + tap, :, mine] = value.astype(low)
+            value = value.astype(low)
+            squares_of({0: 2, count - 1: 0}.get(index, 1), value)
+            target[start + tap, :, mine] = value
         slab = target.at[pl.ds(start, taps), :, mine]
         return links(slab, slab, at.row_peer)
 
@@ -450,15 +517,26 @@
             hold[0, tick] = stage_pair(tick)
         if tick == 0:
             near_hid = whole_far(0)
+            own_out.wait()
+            wait_all(out_copies)
+            far_copies.append(links(g_out.at[:, 1 - at.far], out_in, at.far_peer))
+        if tick == 1:
             near_out = whole_far(1)
         if 0 <= tick - 1 < count:
             hold[1, tick - 1] = stage_second(tick - 1, hold[0, tick - 1])
         if 0 <= tick - 2 < count:
             hold[2, tick - 2] = stage_third(tick - 2, hold[1, tick - 2])
         if tick == 2:
-            o_hid[at.sub] = whole_near(0, near_hid)
-            hid_row = links(o_hid.at[at.sub], o_hid.at[at.sub], at.row_peer)
-            o_out[...] = whole_near(1, near_out)
+            hid_slabs = [
+                o_hid.at[:, lanes_of(which, g_hid.shape[3])] for which in (at.sub, at.row_sub)
+            ]
+            value = whole_near(0, near_hid)
+            squares_of(3, value)
+            o_hid[:, lanes_of(at.sub, g_hid.shape[3])] = value
+            hid_row = links(hid_slabs[0], hid_slabs[0], at.row_peer)
+            value = whole_near(1, near_out)
+            squares_of(4, value)
+            o_out[...] = value
             wait_all(vec_copies)
             value = g_vec[:, vec_cols]
             for hop in range(n_dp - 1):
@@ -472,10 +550,28 @@
             hold[3, tick - 3] = stage_near(tick - 3, hold[2, tick - 3])
         if tick == 3:
             hid_row.wait()
-            for which in (at.sub, at.row_sub):
-                final.append(links(o_hid.at[which], o_hid.at[which], at.core_peer))
+            for slab in hid_slabs:
+                final.append(links(slab, slab, at.core_peer))
         if 0 <= tick - 4 < count:
             final += stage_row(tick - 4, hold[3, tick - 4])
+        if tick == count + 2:
+            sq_copies = [
+                links(sq_mine.at[0], sq_land.at[hop], peer)
+                for hop, peer in enumerate(at.dp_peers())
+            ]
+    wait_all(sq_copies)
+    total = sq_mine[0]
+    for hop in range(n_dp - 1):
+        total = total + sq_land[hop]
+    sq_mine[1] = total
+    sq_copies = [
+        links(sq_mine.at[1], sq_land.at[n_dp - 1 + hop], peer)
+        for hop, peer in enumerate(at.sub_peers())
+    ]
+    wait_all(sq_copies)
+    for hop in range(3):
+        total = total + sq_land[n_dp - 1 + hop]
+    o_sq[...] = total
     wait_all(final)
     wait_all(vec_final)
 
@@ -498,30 +594,35 @@
             bufs.append(pltpu.VMEM((2, taps, span) + block, low))
         bufs.append(pltpu.VMEM((taps, span) + block, low))
         bufs.append(pltpu.VMEM((span - 1, taps) + block, low))
-    copies = 5 * (span + 8) + 2 * (span + 2) + n_dp + 8
+    copies = 5 * (span + 8) + 2 * (span + 2) + 2 * n_dp + 16
     results = pl.pallas_call(
         functools.partial(reduce_kernel, n_dp),
         out_shape=(
             some((1, rows, wide), low),
             some((TAPS, mid_rows, wide), low),
             some((1, rows, wide), low),
-            some((4, rows, hid.shape[1]), low),
+            some((rows, 4 * hid.shape[1]), low),
             some((rows, narrow), low),
             some(vec.shape, vec.dtype),
+            some((8, LANES), jnp.float32),
         ),
         in_specs=[pl.BlockSpec(memory_space=pltpu.VMEM)] * 6,
-        out_specs=(pl.BlockSpec(memory_space=pltpu.VMEM),) * 6,
+        out_specs=(pl.BlockSpec(memory_space=pltpu.VMEM),) * 7,
         scratch_shapes=bufs
         + [
             pltpu.VMEM((span, rows, hid.shape[1]), low),
             pltpu.VMEM((span, rows, hid.shape[1]), low),
             pltpu.VMEM((span - 1, rows, hid.shape[1]), low),
+            pltpu.VMEM((span, 2, rows, narrow), low),
             pltpu.VMEM((span, rows, narrow), low),
             pltpu.VMEM((span, rows, narrow), low),
             pltpu.VMEM((span - 1, rows, narrow), low),
             pltpu.VMEM((n_dp - 1, vec.shape[0], vec.shape[1] // 4), jnp.float32),
+            pltpu.VMEM((2, 8, LANES), jnp.float32),
+            pltpu.VMEM((n_dp + 2, 8, LANES), jnp.float32),
             pltpu.SemaphoreType.DMA((copies,)),
             pltpu.SemaphoreType.DMA((copies,)),
+            pltpu.SemaphoreType.DMA,
         ],
         compiler_params=pltpu.CompilerParams(
             collective_id=collective_id, has_side_effects=True, vmem_limit_bytes=56 * MIB
@@ -532,7 +633,7 @@
         mid.reshape(TAPS, span, 2, mid_rows, wide),
         last.reshape(1, span, 2, rows, wide),
         hid.reshape(span, 2, rows, hid.shape[1]),
-        out.reshape(span, 2, rows, narrow),
+        out.reshape(span // 4, 2, rows, narrow),
         vec,
     )
     return results
@@ -542,11 +643,22 @@
     return next(size for size in (192, 160, 128, 96, 64, 48, 32, 24, 16, 8) if rows % size == 0)
 
 
-def column_sums_kernel(queue_ref, turned_ref, o_ref, total):
+def column_sums_kernel(queue_ref, proto_ref, centers_ref, turned_ref, o_ref, total):
     views, rows, _ = queue_ref.shape
+    protos, depth = proto_ref.shape
     width = turned_ref.shape[1]
     tile = row_tile(rows)
     part = 256
+    for start in range(0, width, part):
+        here = max(0, min(part, protos - start))
+        values = jnp.zeros((part, depth), jnp.float32)
+        if here:
+            values = proto_ref[pl.ds(start, here), :]
+            values = values * lax.rsqrt(jnp.sum(values * values, 1, keepdims=True) + unit_eps)
+        if here < part:
+            values = jnp.concatenate([values, jnp.zeros((part - here, depth), jnp.float32)], 0)
+        centers_ref[pl.ds(start, part), :] = values.astype(jnp.bfloat16)
+        turned_ref[:, pl.ds(start, part)] = values.T.astype(jnp.bfloat16)
     for view in range(views):
         total[...] = jnp.zeros_like(total)
 
@@ -563,13 +675,17 @@
         o_ref[pl.ds(view, 1), :] = jnp.sum(total[...], 0, keepdims=True)
 
 
-def column_sums(queue, turned):
-    width = turned.shape[1]
+def column_sums(queue, prototypes, width):
+    depth = prototypes.shape[1]
     return pl.pallas_call(
         column_sums_kernel,
-        out_shape=jax.ShapeDtypeStruct((queue.shape[0], width), jnp.float32),
+        out_shape=(
+            jax.ShapeDtypeStruct((width, depth), jnp.bfloat16),
+            jax.ShapeDtypeStruct((depth, width), jnp.bfloat16),
+            jax.ShapeDtypeStruct((queue.shape[0], width), jnp.float32),
+        ),
         in_specs=[pl.BlockSpec(memory_space=pltpu.VMEM)] * 2,
-        out_specs=pl.BlockSpec(memory_space=pltpu.VMEM),
+        out_specs=(pl.BlockSpec(memory_space=pltpu.VMEM),) * 3,
         scratch_shapes=[pltpu.VMEM((8, width), jnp.float32)],
         compiler_params=pltpu.CompilerParams(vmem_limit_bytes=32 * MIB),
         cost_estimate=pl.CostEstimate(
@@ -578,7 +694,7 @@
             transcendentals=queue.size // queue.shape[2] * width,
         ),
         name="column_sums",
-    )(queue, turned)
+    )(queue, prototypes)
 
 
 def sinkhorn_kernel(
@@ -586,12 +702,16 @@
     count,
     protos,
     queue_ref,
+    centers_ref,
     turned_ref,
-    unit_ref,
+    partial_ref,
     live_ref,
     first_ref,
-    grad_ref,
+    embed_ref,
+    proto_grad_ref,
     loss_ref,
+    grad,
+    parts_land,
     kept,
     scores,
     mine,
@@ -610,6 +730,31 @@
     parts = range(0, width, part)
     mask = live_ref[...]
     greet(axis, count)
+
+    def to_group(turn, source, target):
+        copies = []
+        for hop in range(1, count):
+            to = lax.rem(me + hop, count)
+            copy = pltpu.make_async_remote_copy(
+                src_ref=source(to),
+                dst_ref=target(hop),
+                send_sem=send_sem.at[turn, hop],
+                recv_sem=recv_sem.at[turn, hop],
+                device_id={axis: to},
+                device_id_type=MESH,
+            )
+            copy.start()
+            copies.append(copy)
+        for copy in copies:
+            copy.wait()
+
+    to_group(ITERS, lambda to: partial_ref.at[to], lambda hop: parts_land.at[hop])
+    embedding = partial_ref[me]
+    for hop in range(1, count):
+        embedding = embedding + parts_land[hop]
+    inverse = lax.rsqrt(jnp.sum(embedding * embedding, 1, keepdims=True) + unit_eps)
+    unit = embedding * inverse
+    unit_low = unit.astype(jnp.bfloat16)
 
     def sum_group(turn):
         copies = []
@@ -634,7 +779,7 @@
     for start in parts:
         cols = pl.ds(start, part)
         scores[:, cols] = jnp.dot(
-            unit_ref[...], turned_ref[:, cols], preferred_element_type=jnp.float32
+            unit_low, turned_ref[:, cols], preferred_element_type=jnp.float32
         )
         for view in range(views):
             lines = pl.ds(view * images, images)
@@ -705,41 +850,56 @@
         logs = jnp.where(real, (raw - jnp.log2(norm)) / LOG2E, 0.0)
         loss = loss - jnp.sum(others * logs, 1, keepdims=True)
         weight = (NBIG - 1.0 if crop < NBIG else float(NBIG)) * mask / norm
-        grad = (weight * powers - others) / (PAIRS * softmax_temp)
-        grad_ref[lines, :] = grad.astype(grad_ref.dtype)
+        grad[lines, :] = (weight * powers - others) / (PAIRS * softmax_temp)
     loss_ref[...] = jnp.broadcast_to(
         jnp.sum(loss, 0, keepdims=True) / PAIRS, loss_ref.shape
     )
-
-
-def sinkhorn(sizes, collective_id, protos, queue, turned, unit, live, first):
+    grad_unit = jnp.zeros(unit.shape, jnp.float32)
+    for start in parts:
+        cols = pl.ds(start, part)
+        some = grad[:, cols].astype(jnp.bfloat16)
+        grad_unit = grad_unit + jnp.dot(
+            some, centers_ref[cols, :], preferred_element_type=jnp.float32
+        )
+        proto_grad_ref[cols, :] = cross_rows(some, unit_low)
+    grad_embed = inverse * (
+        grad_unit - unit * jnp.sum(unit * grad_unit, 1, keepdims=True)
+    )
+    embed_ref[me] = grad_embed.astype(jnp.bfloat16)
+    to_group(ITERS + 1, lambda to: embed_ref.at[me], lambda hop: embed_ref.at[me])
+
+
+def sinkhorn(sizes, collective_id, protos, queue, centers, turned, partial, live, first):
     count = sizes["sub"]
     views, rows, depth = queue.shape
     width = turned.shape[1]
-    crops = unit.shape[0]
+    crops = partial.shape[1]
     return pl.pallas_call(
         functools.partial(sinkhorn_kernel, "sub", count, protos),
         out_shape=(
-            jax.ShapeDtypeStruct((crops, width), jnp.bfloat16),
+            jax.ShapeDtypeStruct((count, crops, depth), jnp.bfloat16),
+            jax.ShapeDtypeStruct((width, depth), jnp.float32),
             jax.ShapeDtypeStruct((8, LANES), jnp.float32),
         ),
-        in_specs=[pl.BlockSpec(memory_space=pltpu.VMEM)] * 5,
-        out_specs=(pl.BlockSpec(memory_space=pltpu.VMEM),) * 2,
+        in_specs=[pl.BlockSpec(memory_space=pltpu.VMEM)] * 6,
+        out_specs=(pl.BlockSpec(memory_space=pltpu.VMEM),) * 3,
         scratch_shapes=[
+            pltpu.VMEM((crops, width), jnp.float32),
+            pltpu.VMEM((count, crops, depth), jnp.float32),
             pltpu.VMEM((views, rows, width), jnp.float32),
             pltpu.VMEM((crops, width), jnp.float32),
             pltpu.VMEM((ITERS, views, width), jnp.float32),
             pltpu.VMEM((ITERS, count, views, width), jnp.float32),
             pltpu.VMEM((views, width), jnp.float32),
             pltpu.VMEM((8, width), jnp.float32),
-            pltpu.SemaphoreType.DMA((ITERS, count)),
-            pltpu.SemaphoreType.DMA((ITERS, count)),
+            pltpu.SemaphoreType.DMA((ITERS + 2, count)),
+            pltpu.SemaphoreType.DMA((ITERS + 2, count)),
         ],
         compiler_params=pltpu.CompilerParams(
             collective_id=collective_id, has_side_effects=True, vmem_limit_bytes=48 * MIB
         ),
         name="sinkhorn",
-    )(queue, turned, unit, live, first)
+    )(queue, centers, turned, partial, live, first)
 
 
 def split_rows(values, images):
@@ -854,10 +1014,7 @@
     biases[3] = lax.dynamic_slice_in_dim(biases[3], here * share, share, 0)
 
     proto_inv = lax.rsqrt(jnp.sum(prototypes * prototypes, 1, keepdims=True) + unit_eps)
-    centers_low = (prototypes * proto_inv).astype(jnp.bfloat16)
-    centers_low = jnp.pad(centers_low, ((0, proto_width - proto_count), (0, 0)))
-    turned = centers_low.T
-    first_sums = column_sums(queue, turned)
+    centers_low, turned, first_sums = column_sums(queue, prototypes, proto_width)
 
     live_float = live_counts[0].astype(jnp.float32)
     image_mask = (jnp.arange(images) < live_counts[0]).astype(jnp.float32)[:, None]
@@ -919,7 +1076,7 @@
     pooled_low = pool_crops(jax.nn.silu(summed), images).astype(jnp.bfloat16)
 
     crops = CROPS * images
-    pooled_all = exchange(pooled_low, "sub", name="pooled").reshape(n_sub * crops, channels)
+    pooled_all = relay(exchange.next_id(), pooled_low, False, "pooled").reshape(n_sub * crops, channels)
     group_mask = (jnp.arange(images)[None, :] < lives[:, None]).astype(jnp.float32)
     group_mask = jnp.broadcast_to(group_mask[:, None, :], (n_sub, CROPS, images))
     group_mask = group_mask.reshape(n_sub * crops, 1)
@@ -931,17 +1088,19 @@
     pre_four = gains[3] * normal_four + biases[3]
     act_four = jax.nn.silu(pre_four).astype(jnp.bfloat16)
     partial = forward_dot(act_four, out_low).reshape(n_sub, crops, out_width)
-    embedding = jnp.sum(exchange(partial, "sub", scatter=True, name="embedding"), 0)
-    unit_embed, embed_back = jax.vjp(unit_rows, embedding)
-    unit_low = unit_embed.astype(jnp.bfloat16)
-
-    grad_low, loss_tile = sinkhorn(
-        sizes, exchange.next_id(), proto_count, queue, turned, unit_low, image_mask, first_sums
-    )
-    (grad_embed,) = embed_back(forward_dot(grad_low, centers_low))
-    grad_centers = cross_rows(grad_low, unit_low)
-    embed_low = grad_embed.astype(jnp.bfloat16)
-    embed_all = exchange(embed_low, "sub", name="embed_grad").reshape(n_sub * crops, out_width)
+
+    embed_all, grad_centers, loss_tile = sinkhorn(
+        sizes,
+        exchange.next_id(),
+        proto_count,
+        queue,
+        centers_low,
+        turned,
+        partial,
+        image_mask,
+        first_sums,
+    )
+    embed_all = embed_all.reshape(n_sub * crops, out_width)
 
     d_out = cross_rows(act_four, embed_all)
     grad_four = against(embed_all, out_low) * silu_slope(pre_four)
@@ -954,10 +1113,8 @@
     ).astype(jnp.bfloat16)
     d_hidden = cross_rows(pooled_all, proj_low)
     partial = against(proj_low, hidden_low).astype(jnp.bfloat16).reshape(n_sub, crops, channels)
-    grad_pooled = exchange(partial, "sub", scatter=True, name="pooled_grad")
-    grad_pooled = jnp.sum(grad_pooled.astype(jnp.float32), 0)
-
-    out_group = exchange(d_out.astype(low), "sub", name="out_grad").reshape(hidden_width, out_width)
+    grad_pooled = relay(exchange.next_id(), partial, True, "pooled_grad")
+
     four = exchange(
         jnp.stack([gain_four, bias_four, jnp.broadcast_to(loss_tile[0, 0], (share,))]),
         "sub",
@@ -991,59 +1148,58 @@
     )
     d_first = cross_rows(inputs, one_low)
 
+    scalars = jnp.stack(
+        [
+            loss_group,
+            jnp.sum(lives),
+            jnp.sum(bottleneck_outer[0] * bottleneck_outer[0]),
+            jnp.sum(bottleneck_outer[1] * bottleneck_outer[1]),
+            jnp.sum(bottleneck_inner * bottleneck_inner),
+            jnp.sum(proj_hidden * proj_hidden),
+            jnp.sum(proj_out * proj_out),
+        ]
+    )
+    width = 4 * middle
     vector = jnp.concatenate(
         [
-            gain_one, gain_two, gain_three, gain_four, bias_one, bias_two, bias_three, bias_four,
-            jnp.stack(
-                [
-                    loss_group,
-                    jnp.sum(lives),
-                    jnp.sum(bottleneck_outer[0] * bottleneck_outer[0]),
-                    jnp.sum(bottleneck_outer[1] * bottleneck_outer[1]),
-                    jnp.sum(bottleneck_inner * bottleneck_inner),
-                    jnp.sum(proj_hidden * proj_hidden),
-                    jnp.sum(proj_out * proj_out),
-                ]
-            ),
-        ]
-    )
-    vec_width = -(-vector.shape[0] // 4096) * 512
-    vector = jnp.pad(vector, (0, 8 * vec_width - vector.shape[0])).reshape(8, vec_width)
-    shard_first, shard_inner, shard_last, shard_hidden, shard_out, vector = reduce_gradients(
+            jnp.concatenate([gain_one, gain_two, bias_one, bias_two]).reshape(1, width),
+            gain_three.reshape(-1, width),
+            gain_four.reshape(-1, width),
+            bias_three.reshape(-1, width),
+            bias_four.reshape(-1, width),
+            jnp.pad(scalars, (0, width - 7))[None],
+            jnp.zeros((2, width), jnp.float32),
+        ],
+        0,
+    )
+    shard_first, shard_inner, shard_last, shard_hidden, shard_out, vector, grad_all = reduce_gradients(
         n_dp,
         exchange.next_id(),
         d_first.astype(low),
         d_middle.astype(low).reshape(TAPS, middle, middle),
         d_last.astype(low),
         d_hidden.astype(low),
-        out_group,
+        d_out.astype(low),
         vector,
     )
     shard_outer = jnp.concatenate([shard_first, shard_last], 0).astype(jnp.float32)
     shard_inner = shard_inner.astype(jnp.float32)
-    shard_hidden = jnp.transpose(shard_hidden, (1, 0, 2)).reshape(-1, hidden_width)
     shard_hidden = shard_hidden.astype(jnp.float32)
     shard_out = shard_out.astype(jnp.float32)
-    vector = vector.reshape(-1)
-    norms = norm_params.shape[1]
-    norm_sum = vector[: 2 * norms].reshape(2, norms)
-    numer_all, live_all = vector[2 * norms], vector[2 * norms + 1]
-    weight_all = vector[2 * norms + 2 : 2 * norms + 7]
+    norm_sum = jnp.stack(
+        [
+            jnp.concatenate([vector[0, : 2 * middle], vector[1], vector[2]]),
+            jnp.concatenate([vector[0, 2 * middle :], vector[3], vector[4]]),
+        ]
+    )
+    numer_all, live_all, weight_all = vector[5, 0], vector[5, 1], vector[5, 2:7]
     proto_unit = prototypes * proto_inv
     proto_sum = proto_inv * (
         centers_sum - proto_unit * jnp.sum(proto_unit * centers_sum, 1, keepdims=True)
     )
 
-    squares = jnp.concatenate(
-        [
-            jnp.sum(shard_outer * shard_outer, (1, 2)),
-            jnp.sum(shard_inner * shard_inner)[None],
-            jnp.sum(shard_hidden * shard_hidden)[None],
-            jnp.sum(shard_out * shard_out)[None],
-        ]
-    )
-    squares = jnp.broadcast_to(jnp.pad(squares, (0, 3))[:, None], (8, LANES))
-    grad_all = jnp.sum(exchange(squares, "dp", name="norms"), 0)[:5, 0]
+    grad_all = jnp.sum(grad_all[:5], 1) / jnp.array([1.0, 1.0, 1.0, 1.0, 4.0], jnp.float32)
+    grad_all = jnp.stack([grad_all[0], grad_all[2], grad_all[1], grad_all[3], grad_all[4]])
     trusts = trust_rate * jnp.sqrt(weight_all) / (jnp.sqrt(grad_all) + 1e-12)
     proto_trust = (
         trust_rate

time: 577 us -> 507 us (0.88); the launches traced: 568 us -> 504 us
  local copies, waits for them, and re-layouts: 85.6 us -> 55.8 us
  Pallas kernels: 296 us -> 277 us
  other arithmetic: 87.8 us -> 74.7 us
    pallas_call x13 -> x7, Pallas kernels: 80.8 us -> 26.4 us  [__call__(): pl.pallas_call(functools.partial(exchange_kernel, axis, count, scatter),...]
    unnamed x255 -> x162, local copies, waits for them, and re-layouts: 50.5 us -> 20.6 us
    pallas_call x1 -> x3, Pallas kernels: 4.68 us -> 26.3 us  [the longest x2 20.9 us: relay(): pl.pallas_call(functools.partial(relay_kernel, scatter), out_shape=jax.Sh...]
    reduce_sum x9 -> x2, other arithmetic: 8.53 us -> 1.36 us  [the longest x1 0.88 us: per_device(): jnp.sum(grad_all[:5], 1) / jnp.array([1.0, 1.0, 1.0, 1.0, 4.0], jnp.float32)]
    pallas_call x1, Pallas kernels: 21.8 us -> 28.4 us  [sinkhorn(): pl.pallas_call(functools.partial(sinkhorn_kernel, 'sub', count, protos),...]
    pallas_call x1, Pallas kernels: 107 us -> 114 us  [reduce_gradients(): pl.pallas_call(functools.partial(reduce_kernel, n_dp), out_shape=(some((1...]
    dot_general x7 -> x6, matrix products: 40.8 us -> 39.4 us  [forward_dot(): return jnp.dot(left, right, preferred_element_type=jnp.float32)]
    dot_general x6 -> x5, matrix products: 27 us -> 26.7 us  [cross_rows(): lax.dot_general(left, right, (((0,), (0,)), ((), ())), preferred_element_...]
  transfers between devices with their start and end apart: 1 -> 1, of which waited for: 0 -> 0; matrix products, arithmetic and copies ran while one was open for 26% -> 22% of each run, Pallas kernels for 28% -> 28%
where the time goes in v3:
time: 507 us; the launch traced here: 504 us
  Pallas kernels  277 us (55%)
  matrix products  77.9 us (15%)
  other arithmetic  74.7 us (15%)
  local copies, waits for them, and re-layouts  55.8 us (11%)
  between operations  18.9 us (4%)
    pallas_call x1, Pallas kernels, reduce_gradients(): pl.pallas_call(functools.partial(reduce_kernel, n_dp), out_shape=(some((1...  114 us
    pallas_call x1, Pallas kernels, gather_weights(): pl.pallas_call(functools.partial(gather_kernel, n_dp), out_shape=(some((s...  82 us
    dot_general x6, matrix products, forward_dot(): return jnp.dot(left, right, preferred_element_type=jnp.float32)  39.4 us
    pallas_call x1, Pallas kernels, sinkhorn(): pl.pallas_call(functools.partial(sinkhorn_kernel, 'sub', count, protos),...  28.4 us
    dot_general x5, matrix products, cross_rows(): lax.dot_general(left, right, (((0,), (0,)), ((), ())), preferred_element_...  26.7 us
    pallas_call x7, Pallas kernels, __call__(): pl.pallas_call(functools.partial(exchange_kernel, axis, count, scatter),...  26.4 us
    pallas_call x2, Pallas kernels, relay(): pl.pallas_call(functools.partial(relay_kernel, scatter), out_shape=jax.Sh...  20.9 us
    unnamed x162, local copies, waits for them, and re-layouts  20.6 us
  transfers between devices with their start and end apart: 1, of which 0 were waited for; matrix products, arithmetic and copies ran while one was open for 22% of the time, Pallas kernels for 28%

profile of v3, /device:TPU:0, one launch (start us, length us, event | category | flops | bytes accessed | tf_op | source)
XLA Modules:
  0.0 504.1 jit_solution(9472330736589305990)
XLA Ops:
  18.8 82.0 %gather_weights.1 = (bf16[4,2,256,512]{3,2,1,0:T(8,128)(2,1)S(1)}, bf16[9,4,2,64,512]{4,3,2,1,0:T(8,128)(2,1)}, bf16[4,2,256,512]{3,2,1,0:T(8,128)(2,1)S(1)}, bf...) custom-call(bf16[256,512]{1,0:T(8,128)(2,1)S(1)} %get-tuple-element.115.refs_0_, ...), custom_call_target="tpu_custom_call" | custom-call | tf_op jit(solution)/shard_map/gather_weights/pallas_call | solution.py:324
  100.8 7.2 %multiply_reduce_fusion.3 = (f32[512]{0:T(512)S(1)}, f32[512]{0:T(512)S(1)}, f32[1216,512]{1,0:T(8,128)}) fusion(f32[1216]{0:T(1024)S(1)} %broadcast_in_dim.19, bf16[2048,512]{1,0:T(8,128)(2,1)S(1)} %bitcast.168, bf16[432,2048]{1,0:T(8,128)(2,1)S(1)} %bitcast.178, bf16[784,2048]{1,0:T(8,128)(2,1)} %bitcast.171), kind=kOutput, calls=%fused_computation.21 | convolution fusion | flops 2562587648 | bytes 9577216 | tf_op jit(solution)/shard_map/dot_general | solution.py:55
  108.1 3.7 sums_one.1
  123.3 11.9 %multiply_reduce_fusion.2 = (f32[512]{0:T(512)S(1)}, f32[512]{0:T(512)S(1)}, f32[1216,512]{1,0:T(8,128)}) fusion(f32[1216]{0:T(1024)S(1)} %broadcast_in_dim.19, bf16[4608,512]{1,0:T(8,128)(2,1)S(1)} %bitcast.191, bf16[432,4608]{1,0:T(8,128)(2,1)} %copy-done.47, bf16[784,4608]{1,0:T(8,128)(2,1)} %copy-done.44), kind=kOutput, calls=%fused_computation.19 | convolution fusion | flops 5762710528 | bytes 18424576 | tf_op jit(solution)/shard_map/dot_general | solution.py:55
  139.0 9.4 %multiply_reduce_fusion = (f32[2048]{0:T(1024)S(1)}, f32[2048]{0:T(1024)S(1)}, f32[1216,2048]{1,0:T(8,128)}) fusion(f32[1216]{0:T(1024)S(1)} %broadcast_in_dim.19, bf16[2048,512]{1,0:T(8,128)(2,1)} %bitcast.166, f32[1216,512]{1,0:T(8,128)} %get-tuple-element.183, f32[512]{0:T(512)S(1)} %bitcast.308, f32[512]{0:T(512)S(1)} %bitcast.282, ...), kind=kOutput, calls=%fused_computation.1 | convolution fusion | flops 2565697536 | bytes 14578432 | tf_op jit(solution)/shard_map/dot_general | solution.py:49
  148.4 3.9 sums_three.1
  152.4 8.5 %fusion.5 = f32[1216,2048]{1,0:T(8,128)S(1)} fusion(f32[2048]{0:T(1024)S(1)} %bitcast.249, f32[2048]{0:T(1024)S(1)} %bitcast.241, f32[1216,2048]{1,0:T(8,128)} %get-tuple-element.184, f32[2048]{0:T(1024)S(1)} %bitcast.244, f32[2048]{0:T(1024)S(1)} %bitcast.247, bf16[432,2048]{1,0:T(8,128)(2,1)S(1)} %bitcast.179, bf16[784,2048]{1,0:T(8,128)(2,1)} %bitcast.172), kind=kLoop, calls=%fused_computation.12 | loop fusion | flops 32374784 | bytes 24936448 | tf_op jit(solution)/shard_map/jit(silu)/mul | solution.py:1076
  172.3 9.6 %pooled.1 = bf16[4,64,2048]{2,1,0:T(8,128)(2,1)S(1)} custom-call(bf16[64,2048]{1,0:T(8,128)(2,1)S(1)} %pad_maximum_fusion.5.x_ref), custom_call_target="tpu_custom_call" | custom-call | tf_op jit(solution)/shard_map/pooled/pallas_call | solution.py:130
  182.5 5.4 %column_sums.1 = (bf16[3072,128]{1,0:T(8,128)(2,1)S(1)}, bf16[128,3072]{1,0:T(8,128)(2,1)S(1)}, f32[2,3072]{1,0:T(2,128)S(1)}) custom-call(bf16[2,960,128]{2,1,0:T(8,128)(2,1)S(1)} %copy-done.2, f32[3000,128]{1,0:T(8,128)S(1)} %copy-done), custom_call_target="tpu_custom_call" | custom-call | flops 1509949440 | bytes 491520 | tf_op jit(solution)/shard_map/column_sums/pallas_call | solution.py:680
  190.6 28.4 %sinkhorn.1 = (bf16[4,64,128]{2,1,0:T(8,128)(2,1)S(1)}, f32[3072,128]{1,0:T(8,128)S(1)}, f32[8,128]{1,0:T(8,128)S(1)}) custom-call(bf16[2,960,128]{2,1,0:T(8,128)(2,1)S(1)} %copy-done.2, bf16[3072,128]{1,0:T(8,128)(2,1)S(1)} %get-tuple-element.46.centers_ref, bf16[128,3072]{1,0:T(8,128)(2,1)S(1)} %get-tuple-element.47.turned_ref, ...), custom_call_target="tpu_custom_call" | custom-call | tf_op jit(solution)/shard_map/sinkhorn/pallas_call | solution.py:877
  223.0 11.3 %pooled_grad.1 = f32[64,2048]{1,0:T(8,128)S(1)} custom-call(bf16[4,64,2048]{2,1,0:T(8,128)(2,1)S(1)} %bitcast.160), custom_call_target="tpu_custom_call" | custom-call | tf_op jit(solution)/shard_map/pooled_grad/pallas_call | solution.py:130
  238.2 7.7 %fusion.35 = (f32[2048]{0:T(1024)S(1)}, f32[2048]{0:T(1024)S(1)}, f32[1216,2048]{1,0:T(8,128)}) fusion(f32[2048]{0:T(1024)S(1)} %bitcast.242, f32[1216,2048]{1,0:T(8,128)S(1)} %bitcast.170, f32[2048]{0:T(1024)S(1)} %bitcast.245, bf16[432,2048]{1,0:T(8,128)(2,1)S(1)} %bitcast.180, bf16[784,2048]{1,0:T(8,128)(2,1)S(1)} %bitcast.174, f32[2048]{0:T(1024)S(1)} %bitcast.250, ...), kind=kLoop, calls=%fused_computation.225 | loop fusion | flops 52293632 | bytes 34914304 | tf_op jit(solution)/shard_map/reduce_sum | solution.py:1128
  245.9 3.9 back_three.1
  249.8 9.4 %multiply_convert_fusion = bf16[1216,2048]{1,0:T(8,128)(2,1)S(1)} fusion(f32[1216,2048]{1,0:T(8,128)} %get-tuple-element.109, f32[1216,2048]{1,0:T(8,128)} %get-tuple-element.184, f32[]{:T(128)S(6)} %mul.519, f32[2048]{0:T(1024)S(1)} %bitcast.252, f32[2048]{0:T(1024)S(1)} %bitcast.251, f32[2048]{0:T(1024)S(1)} %bitcast.243, f32[2048]{0:T(1024)S(1)} %bitcast.246, ...), kind=kLoop, calls=%fused_computation.9 | loop fusion | flops 22413312 | bytes 24949508 | tf_op jit(solution)/shard_map/convert_element_type | solution.py:1133
  259.3 5.4 %fusion.37 = (f32[512]{0:T(512)S(1)}, f32[512]{0:T(512)S(1)}, f32[1216,512]{1,0:T(8,128)}) fusion(f32[512]{0:T(512)S(1)} %bitcast.283, f32[1216,512]{1,0:T(8,128)S(1)} %copy-done.24, f32[512]{0:T(512)S(1)} %bitcast.287, f32[512]{0:T(512)S(1)} %bitcast.309, f32[512]{0:T(512)S(1)} %bitcast.306, bf16[1216,2048]{1,0:T(8,128)(2,1)S(1)} %multiply_convert_fusion, ...), kind=kOutput, calls=%fused_computation.227 | convolution fusion | flops 2559474688 | bytes 12070912 | tf_op jit(solution)/shard_map/dot_general | solution.py:55
  264.7 3.7 back_two.1
  272.1 10.7 %convolution_convert_fusion = bf16[4608,512]{1,0:T(8,128)(2,1)} fusion(bf16[1216,512]{1,0:T(8,128)(2,1)S(1)} %multiply_convert_fusion.2, bf16[432,4608]{1,0:T(8,128)(2,1)S(1)} %copy-done.48, bf16[784,4608]{1,0:T(8,128)(2,1)} %copy-done.44), kind=kOutput, calls=%fused_computation.15 | convolution fusion | flops 5762580480 | bytes 17170432 | tf_op jit(solution)/shard_map/dot_general | solution.py:43
  282.8 5.0 convolution_convert_fusion.2
  298.4 6.7 %copy.51 = bf16[9,512,512]{1,2,0:T(8,128)(2,1)} copy(bf16[9,512,512]{2,1,0:T(8,128)(2,1)} %bitcast.188) | data formatting | bytes 9437184 | tf_op jit(solution)/shard_map/reshape | solution.py:1006
  315.3 13.0 %fusion.36 = (f32[512]{0:T(512)S(1)}, f32[512]{0:T(512)S(1)}, f32[1216,512]{1,0:T(8,128)}) fusion(f32[512]{0:T(512)S(1)} %bitcast.273, f32[1216,512]{1,0:T(8,128)S(1)} %copy-done.23, f32[512]{0:T(512)S(1)} %bitcast.276, f32[512]{0:T(512)S(1)} %bitcast.281, f32[512]{0:T(512)S(1)} %bitcast.279, bf16[4608,512]{1,0:T(8,128)(2,1)S(1)} %bitcast.194, ...), kind=kOutput, calls=%fused_computation.226 | convolution fusion | flops 5769559040 | bytes 20918272 | tf_op jit(solution)/shard_map/dot_general | solution.py:55
  332.1 4.6 stack.122
  336.7 8.1 %convolution_convert_fusion.3 = bf16[2048,512]{1,0:T(8,128)(2,1)} fusion(f32[1216,512]{1,0:T(8,128)} %get-tuple-element.188, f32[1216,512]{1,0:T(8,128)} %get-tuple-element.182, f32[512]{0:T(512)S(1)} %bitcast.303, f32[512]{0:T(512)S(1)} %bitcast.301, f32[]{:T(128)S(6)} %mul.519, f32[512]{0:T(512)S(1)} %bitcast.274, f32[512]{0:T(512)S(1)} %bitcast.277, ...), kind=kOutput, calls=%fused_computation.26 | convolution fusion | flops 2566750208 | bytes 12073732 | tf_op jit(solution)/shard_map/dot_general | solution.py:43
  345.5 113.8 %reduce_gradients.1 = (bf16[1,256,512]{2,1,0:T(8,128)(2,1)}, bf16[9,64,512]{2,1,0:T(8,128)(2,1)}, bf16[1,256,512]{2,1,0:T(8,128)(2,1)}, bf16[256,2048]{1,0:T(8,1...) custom-call(bf16[1,4,2,256,512]{4,3,2,1,0:T(8,128)(2,1)} %bitcast.217, ...), custom_call_target="tpu_custom_call" | custom-call | tf_op jit(solution)/shard_map/reduce_gradients/pallas_call | solution.py:598
  492.3 4.8 add_multiply_fusion.1
  (281 shorter events, 107.4 us)
Async XLA Ops:
  7.2 479.1 %all-reduce.7.cloned.1.call-start = ((), (), s32[]{:S(2)}) async-start(), calls=%async_computation | async-start | bytes 3145728 | tf_op jit(solution)/shard_map/psum | solution.py:1125
  14.4 138.0 %copy-start.7 = (bf16[3,3,6,8,2048]{4,3,2,1,0:T(8,128)(2,1)}, bf16[3,3,6,8,2048]{4,3,2,1,0:T(8,128)(2,1)S(1)}, u32[]{:S(2)}) copy-start(bf16[3,3,6,8,2048]{4,3,2,1,0:T(8,128)(2,1)S(1)} %copy.50) | copy-start | bytes 5308420
  100.7 7.3 %copy-start.3 = (bf16[4,2,256,128]{3,2,1,0:T(8,128)(2,1)}, bf16[4,2,256,128]{3,2,1,0:T(8,128)(2,1)S(1)}, u32[]{:S(2)}) copy-start(bf16[4,2,256,128]{3,2,1,0:T(8,128)(2,1)S(1)} %get-tuple-element.48) | copy-start | bytes 1572868
  100.8 7.3 %copy-start.4 = (bf16[4,2,256,512]{3,2,1,0:T(8,128)(2,1)}, bf16[4,2,256,512]{3,2,1,0:T(8,128)(2,1)S(1)}, u32[]{:S(2)}) copy-start(bf16[4,2,256,512]{3,2,1,0:T(8,128)(2,1)S(1)} %get-tuple-element.44) | copy-start | bytes 6291460
  100.8 12.3 %copy-start.41 = (f32[2,5120]{1,0:T(2,128)S(1)}, f32[2,5120]{1,0:T(2,128)}, u32[]{:S(2)}) copy-start(f32[2,5120]{1,0:T(2,128)} %param.32) | copy-start | bytes 122884
  139.0 9.4 %copy-start.53 = (f32[1,512]{1,0:T(1,128)}, f32[1,512]{1,0:T(1,128)S(1)}, u32[]{:S(2)}) copy-start(f32[1,512]{1,0:T(1,128)S(1)} %get-tuple-element.163) | copy-start | bytes 6148
  168.9 13.6 %copy-start = (f32[3000,128]{1,0:T(8,128)S(1)}, f32[3000,128]{1,0:T(8,128)}, u32[]{:S(2)}) copy-start(f32[3000,128]{1,0:T(8,128)} %proto_ref.1) | copy-start | bytes 4608004
  168.9 13.6 %copy-start.2 = (bf16[2,960,128]{2,1,0:T(8,128)(2,1)S(1)}, bf16[2,960,128]{2,1,0:T(8,128)(2,1)}, u32[]{:S(2)}) copy-start(bf16[2,960,128]{2,1,0:T(8,128)(2,1)} %queue_ref.3) | copy-start | bytes 1474564
  220.3 15.3 %slice-start = ((s8[9961472]{0:T(1024)(128)(4,1)}), s8[1572864]{0:T(1024)(128)(4,1)S(1)}, s32[]{:S(2)}) async-start(s8[9961472]{0:T(1024)(128)(4,1)} %bitcast.169), calls=%async_computation.1 | async-start | bytes 3145728
  222.2 13.4 %slice-start.1 = ((s8[9961472]{0:T(1024)(128)(4,1)}), s8[4194304]{0:T(1024)(128)(4,1)S(1)}, s32[]{:S(2)}) async-start(s8[9961472]{0:T(1024)(128)(4,1)} %bitcast.169), calls=%async_computation.2 | async-start | bytes 8388608
  249.8 9.4 %copy-start.5 = (bf16[4,2,256,512]{3,2,1,0:T(8,128)(2,1)S(1)}, bf16[4,2,256,512]{3,2,1,0:T(8,128)(2,1)}, u32[]{:S(2)}) copy-start(bf16[4,2,256,512]{3,2,1,0:T(8,128)(2,1)} %copy-done.4) | copy-start | bytes 6291460
  249.8 9.4 %copy-start.24 = (f32[1216,512]{1,0:T(8,128)S(1)}, f32[1216,512]{1,0:T(8,128)}, u32[]{:S(2)}) copy-start(f32[1216,512]{1,0:T(8,128)} %get-tuple-element.183) | copy-start | bytes 7471108
  249.8 9.4 %copy-start.54 = (f32[1,512]{1,0:T(1,128)S(1)}, f32[1,512]{1,0:T(1,128)}, u32[]{:S(2)}) copy-start(f32[1,512]{1,0:T(1,128)} %copy-done.53) | copy-start | bytes 6148
  271.8 11.0 %copy-start.11 = (bf16[1216,512]{1,0:T(8,128)(2,1)}, bf16[1216,512]{1,0:T(8,128)(2,1)S(1)}, u32[]{:S(2)}) copy-start(bf16[1216,512]{1,0:T(8,128)(2,1)S(1)} %multiply_convert_fusion.2) | copy-start | bytes 3735556
  271.8 10.9 %slice-start.5 = ((s8[4980736]{0:T(1024)(128)(4,1)}), s8[4194304]{0:T(1024)(128)(4,1)S(1)}, s32[]{:S(2)}) async-start(s8[4980736]{0:T(1024)(128)(4,1)} %bitcast.186), calls=%async_computation.6 | async-start | bytes 8388608
  272.1 10.7 %slice-start.6 = ((s8[4980736]{0:T(1024)(128)(4,1)}), s8[786432]{0:T(1024)(128)(4,1)S(1)}, s32[]{:S(2)}) async-start(s8[4980736]{0:T(1024)(128)(4,1)} %bitcast.186), calls=%async_computation.7 | async-start | bytes 1572864
  272.1 10.7 %copy-start.25 = (f32[1216,512]{1,0:T(8,128)S(1)}, f32[1216,512]{1,0:T(8,128)}, u32[]{:S(2)}) copy-start(f32[1216,512]{1,0:T(8,128)} %get-tuple-element.183) | copy-start | bytes 7471108
  287.8 8.7 %copy-start.16 = (f32[2,256,512]{2,1,0:T(8,128)S(1)}, f32[2,256,512]{2,1,0:T(8,128)}, u32[]{:S(2)}) copy-start(f32[2,256,512]{2,1,0:T(8,128)} %param.27) | copy-start | bytes 3145732
  287.8 9.4 %copy-start.13 = (f32[256,2048]{1,0:T(8,128)S(1)}, f32[256,2048]{1,0:T(8,128)}, u32[]{:S(2)}) copy-start(f32[256,2048]{1,0:T(8,128)} %param.29) | copy-start | bytes 6291460
  315.3 21.4 %copy-start.9 = (bf16[3,3,6,8,2048]{4,3,2,1,0:T(8,128)(2,1)S(1)}, bf16[3,3,6,8,2048]{4,3,2,1,0:T(8,128)(2,1)}, u32[]{:S(2)}) copy-start(bf16[3,3,6,8,2048]{4,3,2,1,0:T(8,128)(2,1)} %copy-done.7) | copy-start | bytes 5308420
  315.3 21.4 %copy-start.52 = (f32[1,512]{1,0:T(1,128)S(1)}, f32[1,512]{1,0:T(1,128)}, u32[]{:S(2)}) copy-start(f32[1,512]{1,0:T(1,128)} %get-tuple-element.100) | copy-start | bytes 6148
  345.5 114.7 %copy-start.55 = (f32[5]{0:T(128)S(1)}, f32[5]{0:T(128)}, u32[]{:S(2)}) copy-start(f32[5]{0:T(128)} %constant.75) | copy-start | bytes 64
  345.5 122.6 %copy-start.35 = (f32[2,256,512]{2,1,0:T(8,128)S(1)}, f32[2,256,512]{2,1,0:T(8,128)}, u32[]{:S(2)}) copy-start(f32[2,256,512]{2,1,0:T(8,128)} %param.33) | copy-start | bytes 3145732
  459.3 8.8 %copy-start.17 = (f32[2,256,512]{2,1,0:T(8,128)S(1)}, f32[2,256,512]{2,1,0:T(8,128)}, u32[]{:S(2)}) copy-start(f32[2,256,512]{2,1,0:T(8,128)} %param.27) | copy-start | bytes 3145732
  (44 other events, 153.3 us)
Sparse Core Ops, SparseCore 0:
  220.4 135.8 all-reduce.6

commit v4 on v3

--- a/solution.py
+++ b/solution.py
@@ -238,17 +238,101 @@
 ALL = slice(None)
 
 
-def gather_kernel(n_dp, *refs):
-    w_first, w_mid, w_last, w_hid, w_out = refs[:5]
-    o_first, o_mid, o_last, o_hid, o_out = refs[5:10]
-    send_sem, recv_sem, own_sem = refs[10:]
+def sigmoid_of(values):
+    return 0.5 * jnp.tanh(0.5 * values) + 0.5
+
+
+def rows_at(start, size):
+    return pl.ds(start if isinstance(start, int) else pl.multiple_of(start, 16), size)
+
+
+def tap_blocks(images, flip):
+    moves = [[] for _ in range(TAPS)]
+    zeros = [[] for _ in range(TAPS)]
+    base = 0
+    for extent, lines in ((BIG, NBIG * images), (SMALL, NSMALL * images)):
+        for tap in range(TAPS):
+            down, right = tap // 3 - 1, tap % 3 - 1
+            if flip:
+                down, right = -down, -right
+            for row in range(extent):
+                start = base + row * extent * lines
+                if not 0 <= row + down < extent:
+                    zeros[tap].append((start, extent * lines))
+                    continue
+                left, stop = max(0, -right), min(extent, extent - right)
+                moves[tap].append(
+                    (
+                        start + left * lines,
+                        base + ((row + down) * extent + left + right) * lines,
+                        (stop - left) * lines,
+                    )
+                )
+                if left:
+                    zeros[tap].append((start, left * lines))
+                if stop < extent:
+                    zeros[tap].append((start + stop * lines, (extent - stop) * lines))
+        base += extent * extent * lines
+    return moves, zeros
+
+
+def fill_columns(columns, source, images, flip):
+    wide = source.shape[1]
+    moves, zeros = tap_blocks(images, flip)
+    for tap in range(TAPS):
+        cols = pl.ds(tap * wide, wide)
+        for target, start, size in moves[tap]:
+            columns[pl.ds(target, size), cols] = source[pl.ds(start, size), :]
+        for target, size in zeros[tap]:
+            columns[pl.ds(target, size), cols] = jnp.zeros((size, wide), columns.dtype)
+
+
+def masked_sums(values, mask, total):
+    rows, wide = values.shape
+    blocks = values.reshape(rows // 8, 8, wide)
+    masked = blocks * mask
+    total[0] += jnp.sum(masked, 0)
+    total[1] += jnp.sum(masked * blocks, 0)
+
+
+class GroupSums:
+    def __init__(self, at, links):
+        self.at, self.links = at, links
+
+    def start(self, mine, land):
+        self.mine, self.land = mine, land
+        self.copies = [
+            self.links(mine, land.at[hop], peer) for hop, peer in enumerate(self.at.sub_peers())
+        ]
+
+    def finish(self):
+        wait_all(self.copies)
+        value = self.mine[...]
+        for hop in range(3):
+            value = value + self.land[hop]
+        return value
+
+
+def forward_kernel(n_dp, images, *refs):
+    w_first, w_mid, w_last, w_hid, w_out, x_ref, norm_ref, live_ref = refs[:8]
+    (
+        o_mid, o_last, o_hid, o_out, o_columns, o_one, o_two, o_act, o_stat, o_pooled, o_live,
+    ) = refs[8:19]
+    (
+        first_w, mid_w, last_w, columns, act_one, act_two, one, two, three, total, pool,
+        sums_a, land_a, sums_b, land_b, sums_c, land_c, pooled, send_sem, recv_sem, own_sem,
+    ) = refs[19:]
     at = Place(n_dp)
     links = Links(send_sem, recv_sem)
     at.greet(
-        [at.near_peer(hop) for hop in range(1, at.span)]
-        + [at.far_peer, at.row_peer, at.core_peer]
-    )
-    mine, beside = lanes_of(at.sub), lanes_of(at.row_sub)
+        [at.near_peer(hop) for hop in range(1, at.span)] + [at.far_peer] + at.sub_peers()
+    )
+    low = jnp.bfloat16
+    middle = first_w.shape[3]
+    channels = x_ref.shape[1]
+    rows = x_ref.shape[0]
+    mask = live_ref[...][:, :1]
+    half = middle // 2
 
     def flat(source, target, split):
         return (
@@ -257,91 +341,270 @@
             split,
         )
 
-    def taps(start):
+    def taps(start, split):
         some = pl.ds(start, 3)
         return (
             lambda cols: w_mid.at[some, :, cols],
-            lambda near, far, cols: o_mid.at[some, near, far, :, cols],
-            True,
+            lambda near, far, cols: mid_w.at[some, near, far, :, cols],
+            split,
         )
 
     pieces = [
-        flat(w_first, o_first, True),
-        taps(0),
-        taps(3),
-        taps(6),
-        flat(w_last, o_last, True),
-        flat(w_hid, o_hid, False),
-        flat(w_out, o_out, False),
+        flat(w_first, first_w, 4),
+        taps(0, 4),
+        taps(3, 2),
+        taps(6, 4),
+        flat(w_last, last_w, 2),
+        flat(w_hid, o_hid, 1),
+        flat(w_out, o_out, 1),
     ]
     count = len(pieces)
+    mine = {4: lanes_of(at.sub), 2: lanes_of(at.core, half), 1: ALL}
     own, first, second, third, fourth = [], [], [], [], []
     for index, (source, target, split) in enumerate(pieces):
-        cols = mine if split else ALL
+        cols = mine[split]
         copy = pltpu.make_async_copy(source(cols), target(at.near, at.far, cols), own_sem.at[index])
         copy.start()
         own.append(copy)
     for source, target, split in pieces:
-        cols = mine if split else ALL
+        cols = mine[split]
         first.append(
             [
                 links(source(cols), target(at.near, at.far, cols), at.near_peer(hop))
                 for hop in range(1, at.span)
             ]
         )
-    for tick in range(count + 2):
-        if tick < count:
-            source, target, split = pieces[tick]
-            cols = mine if split else ALL
-            own[tick].wait()
-            wait_all(first[tick])
-            slab = target(ALL, at.far, cols)
+
+    def tick(now):
+        if now < count:
+            source, target, split = pieces[now]
+            own[now].wait()
+            wait_all(first[now])
+            slab = target(ALL, at.far, mine[split])
             second.append(links(slab, slab, at.far_peer))
-        if 1 <= tick < count + 1:
-            source, target, split = pieces[tick - 1]
-            second[tick - 1].wait()
-            if split:
-                slab = target(ALL, ALL, mine)
-                third.append(links(slab, slab, at.row_peer))
+        if 0 <= now - 1 < count:
+            source, target, split = pieces[now - 1]
+            second[now - 1].wait()
+            slab = target(ALL, ALL, mine[split])
+            third.append(links(slab, slab, at.row_peer) if split == 4 else None)
+            if split == 2:
+                fourth.append([links(slab, slab, at.core_peer)])
+            elif split == 1:
+                fourth.append([])
             else:
-                third.append(None)
-        if tick >= 2:
-            source, target, split = pieces[tick - 2]
-            if split:
-                third[tick - 2].wait()
-                for cols in (mine, beside):
-                    slab = target(ALL, ALL, cols)
-                    fourth.append(links(slab, slab, at.core_peer))
-    wait_all(fourth)
-
-
-def gather_weights(n_dp, collective_id, first, mid, last, hid, out):
+                fourth.append(None)
+        if 0 <= now - 2 < count and pieces[now - 2][2] == 4:
+            source, target, split = pieces[now - 2]
+            third[now - 2].wait()
+            slabs = [target(ALL, ALL, cols) for cols in (mine[4], lanes_of(at.row_sub))]
+            fourth[now - 2] = [links(slab, slab, at.core_peer) for slab in slabs]
+
+    def arrived(index):
+        wait_all(fourth[index])
+
+    tile = rows // 4
+    sums = GroupSums(at, links)
+
+    def pack(target, wide):
+        target[pl.ds(0, 1), :] = jnp.sum(total[0, :, :wide], 0, keepdims=True)
+        target[pl.ds(1, 1), :] = jnp.sum(total[1, :, :wide], 0, keepdims=True)
+
+    def settle(value, count_all, start, wide):
+        mean = value[0:1] / count_all
+        inverse = lax.rsqrt(value[1:2] / count_all - mean * mean + norm_eps)
+        o_stat[pl.ds(0, 1), pl.ds(start, wide)] = mean
+        o_stat[pl.ds(1, 1), pl.ds(start, wide)] = inverse
+        scale = norm_ref[pl.ds(0, 1), pl.ds(start, wide)] * inverse
+        return scale, norm_ref[pl.ds(1, 1), pl.ds(start, wide)] - scale * mean
+
+    for now in range(4):
+        tick(now)
+    arrived(0)
+    tick(4)
+
+    total[...] = jnp.zeros_like(total)
+
+    def step_one(index, carry):
+        span = rows_at(index * tile, tile)
+        value = jnp.dot(
+            x_ref[span, :],
+            first_w[...].reshape(channels, middle),
+            preferred_element_type=jnp.float32,
+        )
+        one[span, :] = value
+        masked_sums(value, mask, total.at[:, :, pl.ds(0, middle)])
+        return carry
+
+    lax.fori_loop(0, 4, step_one, 0)
+    pack(sums_a, middle)
+    live = jnp.sum(mask, 0, keepdims=True)
+    sums_a[pl.ds(2, 1), :] = jnp.broadcast_to(live, (1, middle))
+    sums.start(sums_a, land_a)
+    tick(5)
+    value = sums.finish()
+    per_image = rows // images
+    lives = value[2:3, :1]
+    count_all = lives * per_image
+    o_live[at.sub] = jnp.broadcast_to(live, o_live.shape[1:])
+    for hop in range(3):
+        o_live[(at.sub + 3 - hop) % 4] = jnp.broadcast_to(land_a[hop, 2:3, :1], o_live.shape[1:])
+    scale, shift = settle(value, count_all, 0, middle)
+
+    def step_act(source, target):
+        def step(index, carry):
+            span = rows_at(index * tile, tile)
+            pre = source[span, :] * scale + shift
+            target[span, :] = (pre * sigmoid_of(pre)).astype(low)
+            return carry
+
+        lax.fori_loop(0, 4, step, 0)
+
+    step_act(one, act_one)
+    save = [pltpu.make_async_copy(one, o_one, own_sem.at[count])]
+    save[-1].start()
+    tick(6)
+    fill_columns(columns, act_one, images, False)
+    save.append(pltpu.make_async_copy(columns, o_columns, own_sem.at[count + 1]))
+    save[-1].start()
+
+    total[...] = jnp.zeros_like(total)
+    for part in range(3):
+        arrived(1 + part)
+        if part == 0:
+            tick(7)
+
+        def step_two(index, carry):
+            span = rows_at(index * tile, tile)
+            value = jnp.dot(
+                columns[span, pl.ds(part * 3 * middle, 3 * middle)],
+                mid_w[pl.ds(part * 3, 3)].reshape(3 * middle, middle),
+                preferred_element_type=jnp.float32,
+            )
+            if part:
+                value = value + two[span, :]
+            two[span, :] = value
+            if part == 2:
+                masked_sums(value, mask, total.at[:, :, pl.ds(0, middle)])
+            return carry
+
+        lax.fori_loop(0, 4, step_two, 0)
+    save.append(pltpu.make_async_copy(mid_w, o_mid, own_sem.at[count + 2]))
+    save[-1].start()
+    pack(sums_b, middle)
+    sums.start(sums_b, land_b)
+    tick(8)
+    scale, shift = settle(sums.finish(), count_all, middle, middle)
+    step_act(two, act_two)
+    save.append(pltpu.make_async_copy(two, o_two, own_sem.at[count + 3]))
+    save[-1].start()
+    save.append(pltpu.make_async_copy(act_two, o_act, own_sem.at[count + 4]))
+    save[-1].start()
+
+    arrived(4)
+    save.append(pltpu.make_async_copy(last_w, o_last, own_sem.at[count + 5]))
+    save[-1].start()
+    total[...] = jnp.zeros_like(total)
+
+    def step_three(index, carry):
+        span = rows_at(index * tile, tile)
+        for quarter in range(4):
+            wide = channels // 4
+            cols = pl.ds(quarter * wide, wide)
+            weights = last_w[pl.ds(quarter * (at.span // 4), at.span // 4)].reshape(wide, middle)
+            value = against(act_two[span, :], weights)
+            three[span, cols] = value
+            masked_sums(value, mask, total.at[:, :, cols])
+        return carry
+
+    lax.fori_loop(0, 4, step_three, 0)
+    pack(sums_c, channels)
+    sums.start(sums_c, land_c)
+    scale, shift = settle(sums.finish(), count_all, 2 * middle, channels)
+
+    pool[...] = jnp.zeros_like(pool)
+    base = 0
+    for extent, crops in ((BIG, NBIG), (SMALL, NSMALL)):
+        lines = crops * images
+        into = pl.ds(0, lines) if extent == BIG else pl.ds(NBIG * images, lines)
+
+        def step_out(index, carry):
+            span = rows_at(base + index * extent * lines, extent * lines)
+            for start in range(0, channels, 512):
+                cols = pl.ds(start, 512)
+                pre = three[span, cols] * scale[:, start : start + 512]
+                pre = pre + shift[:, start : start + 512] + x_ref[span, cols].astype(jnp.float32)
+                value = pre * sigmoid_of(pre)
+                pool[into, cols] += jnp.sum(value.reshape(extent, lines, 512), 0)
+            return carry
+
+        lax.fori_loop(0, extent, step_out, 0)
+        pooled[into, :] = (pool[into, :] * (1.0 / (extent * extent))).astype(low)
+        base += extent * extent * lines
+
+    over = links(pooled, o_pooled.at[at.sub], at.row_peer)
+    pair = links(pooled, o_pooled.at[at.sub], at.core_peer)
+    o_pooled[at.sub] = pooled[...]
+    over.wait()
+    last = links(o_pooled.at[at.row_sub], o_pooled.at[at.row_sub], at.core_peer)
+    pair.wait()
+    last.wait()
+    for copy in save:
+        copy.wait()
+
+
+def forward_trunk(n_dp, collective_id, images, first, mid, last, hid, out, inputs, norms, live):
     span = n_dp // 2
-    rows, middle = first.shape
+    height, middle = first.shape
+    rows, channels = inputs.shape
     some = jax.ShapeDtypeStruct
-    low = jnp.bfloat16
-    copies = 7 * (span + 4)
+    low, full = jnp.bfloat16, jnp.float32
+    copies = 7 * (span + 4) + 12
+    vmem, anywhere = pl.BlockSpec(memory_space=pltpu.VMEM), pl.BlockSpec(memory_space=pl.ANY)
     return pl.pallas_call(
-        functools.partial(gather_kernel, n_dp),
+        functools.partial(forward_kernel, n_dp, images),
         out_shape=(
-            some((span, 2, rows, middle), low),
             some((TAPS, span, 2, mid.shape[1], middle), low),
-            some((span, 2, rows, middle), low),
-            some((span, 2, rows, hid.shape[1]), low),
-            some((span, 2, rows, out.shape[1]), low),
+            some((span, 2, height, middle), low),
+            some((span, 2, height, hid.shape[1]), low),
+            some((span, 2, height, out.shape[1]), low),
+            some((rows, TAPS * middle), low),
+            some((rows, middle), full),
+            some((rows, middle), full),
+            some((rows, middle), low),
+            some((2, 2 * middle + channels), full),
+            some((4, CROPS * images, channels), low),
+            some((4, 8, LANES), full),
         ),
-        in_specs=[pl.BlockSpec(memory_space=pltpu.VMEM)] * 5,
-        out_specs=(pl.BlockSpec(memory_space=pl.ANY),) * 5,
+        in_specs=[vmem] * 8,
+        out_specs=(anywhere,) * 8 + (vmem,) * 3,
         scratch_shapes=[
+            pltpu.VMEM((span, 2, height, middle), low),
+            pltpu.VMEM((TAPS, span, 2, mid.shape[1], middle), low),
+            pltpu.VMEM((span, 2, height, middle), low),
+            pltpu.VMEM((rows, TAPS * middle), low),
+            pltpu.VMEM((rows, middle), low),
+            pltpu.VMEM((rows, middle), low),
+            pltpu.VMEM((rows, middle), full),
+            pltpu.VMEM((rows, middle), full),
+            pltpu.VMEM((rows, channels), full),
+            pltpu.VMEM((2, 8, channels), full),
+            pltpu.VMEM((CROPS * images, channels), full),
+            pltpu.VMEM((3, middle), full),
+            pltpu.VMEM((3, 3, middle), full),
+            pltpu.VMEM((2, middle), full),
+            pltpu.VMEM((3, 2, middle), full),
+            pltpu.VMEM((2, channels), full),
+            pltpu.VMEM((3, 2, channels), full),
+            pltpu.VMEM((CROPS * images, channels), low),
             pltpu.SemaphoreType.DMA((copies,)),
             pltpu.SemaphoreType.DMA((copies,)),
-            pltpu.SemaphoreType.DMA((7,)),
+            pltpu.SemaphoreType.DMA((7 + 6,)),
         ],
         compiler_params=pltpu.CompilerParams(
-            collective_id=collective_id, has_side_effects=True, vmem_limit_bytes=48 * MIB
+            collective_id=collective_id, has_side_effects=True, vmem_limit_bytes=60 * MIB
         ),
-        name="gather_weights",
-    )(first, mid, last, hid, out)
+        name="forward_trunk",
+    )(first, mid, last, hid, out, inputs, norms, live)
 
 
 def plus(left, right):
@@ -990,23 +1253,6 @@
 
     low = jnp.bfloat16
     hidden_cols = lax.dynamic_slice_in_dim(proj_hidden, here * share, share, 1)
-    first_w, inner_low, last_w, hidden_low, out_low = gather_weights(
-        n_dp,
-        exchange.next_id(),
-        bottleneck_outer[0].astype(low),
-        bottleneck_inner.astype(low),
-        bottleneck_outer[1].astype(low),
-        hidden_cols.astype(low),
-        proj_out.astype(low),
-    )
-    first_w = first_w.reshape(channels, middle)
-    last_w = last_w.reshape(channels, middle)
-    hidden_low = hidden_low.reshape(channels, share)
-    out_low = lax.dynamic_slice_in_dim(out_low.reshape(hidden_width, out_width), here * share, share, 0)
-    inner_low = inner_low.reshape(TAPS, middle, middle)
-    middle_w = inner_low.reshape(TAPS * middle, middle)
-    middle_t = jnp.transpose(inner_low, (0, 2, 1)).reshape(TAPS * middle, middle)
-
     bounds = [0, middle, 2 * middle, 2 * middle + channels, 2 * middle + channels + hidden_width]
     gains = [norm_params[0, bounds[k] : bounds[k + 1]] for k in range(4)]
     biases = [norm_params[1, bounds[k] : bounds[k + 1]] for k in range(4)]
@@ -1030,53 +1276,45 @@
         0,
     )
 
-    hidden_one = forward_dot(inputs, first_w)
-    masked = hidden_one * row_mask
-    sums = exchange(
-        jnp.stack(
-            [
-                jnp.sum(masked, 0),
-                jnp.sum(masked * hidden_one, 0),
-                jnp.broadcast_to(live_float, (middle,)),
-            ]
-        ),
-        "sub",
-        name="sums_one",
-    )
-    lives = sums[:, 2, 0]
+    (
+        inner_low, last_w, hidden_low, out_low, columns, hidden_one, hidden_two, act_two,
+        trunk_stat, pooled_all, lives,
+    ) = forward_trunk(
+        n_dp,
+        exchange.next_id(),
+        images,
+        bottleneck_outer[0].astype(low),
+        bottleneck_inner.astype(low),
+        bottleneck_outer[1].astype(low),
+        hidden_cols.astype(low),
+        proj_out.astype(low),
+        inputs,
+        norm_params,
+        jnp.broadcast_to(image_mask, (images, LANES)),
+    )
+    last_w = last_w.reshape(channels, middle)
+    hidden_low = hidden_low.reshape(channels, share)
+    out_low = lax.dynamic_slice_in_dim(out_low.reshape(hidden_width, out_width), here * share, share, 0)
+    inner_low = inner_low.reshape(TAPS, middle, middle)
+    middle_t = jnp.transpose(inner_low, (0, 2, 1)).reshape(TAPS * middle, middle)
+    lives = lives[:, 0, 0]
     count_all = jnp.sum(lives) * per_image
+    mean_one, mean_two, mean_three = [trunk_stat[0, bounds[k] : bounds[k + 1]] for k in range(3)]
+    inv_one, inv_two, inv_three = [trunk_stat[1, bounds[k] : bounds[k + 1]] for k in range(3)]
+    normal_one = (hidden_one - mean_one) * inv_one
+    pre_one = gains[0] * normal_one + biases[0]
+    normal_two = (hidden_two - mean_two) * inv_two
+    pre_two = gains[1] * normal_two + biases[1]
+    hidden_three = against(act_two, last_w)
+    normal_three = (hidden_three - mean_three) * inv_three
+    summed = gains[2] * normal_three + biases[2] + inputs.astype(jnp.float32)
 
     def stats(total, squares, count):
         mean = total / count
         return mean, lax.rsqrt(squares / count - mean * mean + norm_eps)
 
-    def group_stats(values, name):
-        masked = values * row_mask
-        both = exchange(
-            jnp.stack([jnp.sum(masked, 0), jnp.sum(masked * values, 0)]), "sub", name=name
-        )
-        both = jnp.sum(both, 0)
-        return stats(both[0], both[1], count_all)
-
-    sums = jnp.sum(sums, 0)
-    mean_one, inv_one = stats(sums[0], sums[1], count_all)
-    normal_one = (hidden_one - mean_one) * inv_one
-    pre_one = gains[0] * normal_one + biases[0]
-    act_one = jax.nn.silu(pre_one).astype(jnp.bfloat16)
-    columns = patches(act_one, images, False)
-    hidden_two = forward_dot(columns, middle_w)
-    mean_two, inv_two = group_stats(hidden_two, "sums_two")
-    normal_two = (hidden_two - mean_two) * inv_two
-    pre_two = gains[1] * normal_two + biases[1]
-    act_two = jax.nn.silu(pre_two).astype(jnp.bfloat16)
-    hidden_three = against(act_two, last_w)
-    mean_three, inv_three = group_stats(hidden_three, "sums_three")
-    normal_three = (hidden_three - mean_three) * inv_three
-    summed = gains[2] * normal_three + biases[2] + inputs.astype(jnp.float32)
-    pooled_low = pool_crops(jax.nn.silu(summed), images).astype(jnp.bfloat16)
-
     crops = CROPS * images
-    pooled_all = relay(exchange.next_id(), pooled_low, False, "pooled").reshape(n_sub * crops, channels)
+    pooled_all = pooled_all.reshape(n_sub * crops, channels)
     group_mask = (jnp.arange(images)[None, :] < lives[:, None]).astype(jnp.float32)
     group_mask = jnp.broadcast_to(group_mask[:, None, :], (n_sub, CROPS, images))
     group_mask = group_mask.reshape(n_sub * crops, 1)

time: 507 us -> 499 us (0.984)
  Pallas kernels: 277 us -> 301 us
  other arithmetic: 74.7 us -> 58.9 us
  matrix products: 77.9 us -> 67.6 us
  local copies, waits for them, and re-layouts: 55.8 us -> 49.4 us
    pallas_call x1, Pallas kernels: 82 us -> 126 us  [forward_trunk(): pl.pallas_call(functools.partial(forward_kernel, n_dp, images), out_shape...]
    dot_general x6 -> x4, matrix products: 39.4 us -> 20 us  [forward_dot(): return jnp.dot(left, right, preferred_element_type=jnp.float32)]
    reduce_sum x6 -> x1, other arithmetic: 13.2 us -> 1.43 us  [per_device(): count_crops = jnp.sum(lives) * CROPS]
    pallas_call x7 -> x4, Pallas kernels: 26.4 us -> 15.1 us  [__call__(): pl.pallas_call(functools.partial(exchange_kernel, axis, count, scatter),...]
    pallas_call x2 -> x1, Pallas kernels: 20.9 us -> 11.8 us  [relay(): pl.pallas_call(functools.partial(relay_kernel, scatter), out_shape=jax.Sh...]
    mul x1 -> x0, other arithmetic: 8.48 us -> none  [per_device(): pooled_low = pool_crops(jax.nn.silu(summed), images).astype(jnp.bfloat16)]
    unnamed x162 -> x148, local copies, waits for them, and re-layouts: 20.6 us -> 12.3 us
    dot_general x3, matrix products: 11.8 us -> 19.3 us  [against(): lax.dot_general(left, right, (((1,), (1,)), ((), ())), preferred_element_...]
  transfers between devices with their start and end apart: 1 -> 1, of which waited for: 0 -> 0; matrix products, arithmetic and copies ran while one was open for 22% -> 26% of each run, Pallas kernels for 28% -> 28%
where the time goes in v4:
time: 499 us; the launch traced here: 495 us
  Pallas kernels  301 us (60%)
  matrix products  67.6 us (14%)
  other arithmetic  58.9 us (12%)
  local copies, waits for them, and re-layouts  49.4 us (10%)
  between operations  18.7 us (4%)
    pallas_call x1, Pallas kernels, forward_trunk(): pl.pallas_call(functools.partial(forward_kernel, n_dp, images), out_shape...  126 us
    pallas_call x1, Pallas kernels, reduce_gradients(): pl.pallas_call(functools.partial(reduce_kernel, n_dp), out_shape=(some((1...  113 us
    pallas_call x1, Pallas kernels, sinkhorn(): pl.pallas_call(functools.partial(sinkhorn_kernel, 'sub', count, protos),...  30.2 us
    dot_general x5, matrix products, cross_rows(): lax.dot_general(left, right, (((0,), (0,)), ((), ())), preferred_element_...  28.3 us
    dot_general x4, matrix products, forward_dot(): return jnp.dot(left, right, preferred_element_type=jnp.float32)  20 us
    dot_general x3, matrix products, against(): lax.dot_general(left, right, (((1,), (1,)), ((), ())), preferred_element_...  19.3 us
    pallas_call x4, Pallas kernels, __call__(): pl.pallas_call(functools.partial(exchange_kernel, axis, count, scatter),...  15.1 us
    convert_element_type x2, other arithmetic, norm_back(): return (grad_in.astype(jnp.bfloat16), both[1], both[0])  12.6 us
  transfers between devices with their start and end apart: 1, of which 0 were waited for; matrix products, arithmetic and copies ran while one was open for 26% of the time, Pallas kernels for 28%

profile of v4, /device:TPU:0, one launch (start us, length us, event | category | flops | bytes accessed | tf_op | source)
XLA Modules:
  0.0 495.3 jit_solution(5570395448451312773)
XLA Ops:
  15.5 5.6 %copy.49 = bf16[7,7,2,8,2048]{4,3,2,1,0:T(8,128)(2,1)} copy(bf16[7,7,2,8,2048]{4,2,1,0,3:T(2,128)(2,1)} %bitcast.159) | data formatting | bytes 6422528 | tf_op jit(solution)/shard_map/transpose | solution.py:1273
  23.6 5.1 %pad_maximum_fusion.refs_5_ = bf16[1216,2048]{1,0:T(8,128)(2,1)} fusion(bf16[432,2048]{1,0:T(8,128)(2,1)S(1)} %bitcast.139, bf16[784,2048]{1,0:T(8,128)(2,1)} %bitcast.134), kind=kLoop, calls=%fused_computation.9 | loop fusion | flops 9961472 | bytes 9961472 | tf_op jit(solution)/shard_map/concatenate | solution.py:1271
  29.3 125.6 %forward_trunk.1 = (bf16[9,4,2,64,512]{4,3,2,1,0:T(8,128)(2,1)}, bf16[4,2,256,512]{3,2,1,0:T(8,128)(2,1)}, bf16[4,2,256,512]{3,2,1,0:T(8,128)(2,1)}, bf16[4,2,25...) custom-call(bf16[256,512]{1,0:T(8,128)(2,1)} %get-tuple-element.112., ...), custom_call_target="tpu_custom_call" | custom-call | tf_op jit(solution)/shard_map/forward_trunk/pallas_call | solution.py:563
  158.0 5.4 %column_sums.1 = (bf16[3072,128]{1,0:T(8,128)(2,1)S(1)}, bf16[128,3072]{1,0:T(8,128)(2,1)S(1)}, f32[2,3072]{1,0:T(2,128)S(1)}) custom-call(bf16[2,960,128]{2,1,0:T(8,128)(2,1)S(1)} %copy-done.1, f32[3000,128]{1,0:T(8,128)S(1)} %copy-done), custom_call_target="tpu_custom_call" | custom-call | flops 1509949440 | bytes 491520 | tf_op jit(solution)/shard_map/column_sums/pallas_call | solution.py:943
  165.5 30.2 %sinkhorn.1 = (bf16[4,64,128]{2,1,0:T(8,128)(2,1)S(1)}, f32[3072,128]{1,0:T(8,128)}, f32[8,128]{1,0:T(8,128)S(1)}) custom-call(bf16[2,960,128]{2,1,0:T(8,128)(2,1)S(1)} %copy-done.1, bf16[3072,128]{1,0:T(8,128)(2,1)S(1)} %get-tuple-element.52.centers_ref, bf16[128,3072]{1,0:T(8,128)(2,1)S(1)} %get-tuple-element.53.turned_ref, f32[4,64,128]{2,1,0:T(8,128)S(1)} %bitcast.130, ...), custom_call_target="tpu_custom_call" | custom-call | tf_op jit(solution)/shard_map/sinkhorn/pallas_call | solution.py:1140
  199.6 11.8 %pooled_grad.1 = f32[64,2048]{1,0:T(8,128)S(1)} custom-call(bf16[4,64,2048]{2,1,0:T(8,128)(2,1)S(1)} %bitcast.129), custom_call_target="tpu_custom_call" | custom-call | tf_op jit(solution)/shard_map/pooled_grad/pallas_call | solution.py:130
  214.3 3.6 broadcast_in_dim.22
  217.9 17.1 %fusion.26 = (f32[2048]{0:T(1024)S(1)}, f32[2048]{0:T(1024)S(1)}, f32[1216,2048]{1,0:T(8,128)}, f32[1216,2048]{1,0:T(8,128)}) fusion(bf16[432,2048]{1,0:T(8,128)(2,1)S(1)} %bitcast.141, bf16[784,2048]{1,0:T(8,128)(2,1)} %bitcast.135, f32[2048]{0:T(1024)S(1)} %bitcast.217, f32[2048]{0:T(1024)S(1)} %bitcast.218, f32[432,2048]{1,0:T(8,128)} %bitcast.150, ...), kind=kOutput, calls=%fused_computation.152 | convolution fusion | flops 2602430464 | bytes 38256640 | tf_op jit(solution)/shard_map/dot_general | solution.py:49
  235.0 3.9 back_three.1
  239.1 9.2 %multiply_convert_fusion = bf16[1216,2048]{1,0:T(8,128)(2,1)S(1)} fusion(f32[1216,2048]{1,0:T(8,128)} %get-tuple-element.106, f32[1216,2048]{1,0:T(8,128)} %get-tuple-element.174, f32[]{:T(128)S(6)} %mul.510, f32[2048]{0:T(1024)S(1)} %bitcast.179, f32[2048]{0:T(1024)S(1)} %bitcast.178, f32[1216]{0:T(1024)S(1)} %broadcast_in_dim.25, f32[2048]{0:T(1024)S(1)} %bitcast.181), kind=kLoop, calls=%fused_computation.5 | loop fusion | flops 17432576 | bytes 24933124 | tf_op jit(solution)/shard_map/convert_element_type | solution.py:1371
  248.3 5.4 %fusion.28 = (f32[512]{0:T(512)S(1)}, f32[512]{0:T(512)S(1)}, f32[1216,512]{1,0:T(8,128)}) fusion(f32[512]{0:T(512)S(1)} %bitcast.204, f32[1216,512]{1,0:T(8,128)S(1)} %copy-done.19, f32[512]{0:T(512)S(1)} %bitcast.202, f32[512]{0:T(512)S(1)} %bitcast.228, f32[512]{0:T(512)S(1)} %bitcast.229, bf16[1216,2048]{1,0:T(8,128)(2,1)S(1)} %multiply_convert_fusion, ...), kind=kOutput, calls=%fused_computation.154 | convolution fusion | flops 2559474688 | bytes 12070912 | tf_op jit(solution)/shard_map/dot_general | solution.py:55
  253.7 3.7 back_two.1
  257.5 3.4 multiply_convert_fusion.2
  262.8 4.3 convolution_convert_fusion.2
  271.4 3.7 sums_four.1
  277.7 6.7 %copy.51 = bf16[9,512,512]{1,2,0:T(8,128)(2,1)} copy(bf16[9,512,512]{2,1,0:T(8,128)(2,1)} %bitcast.143) | data formatting | bytes 9437184 | tf_op jit(solution)/shard_map/reshape | solution.py:1298
  289.8 3.7 copy-done.35
  294.7 12.8 %fusion.27 = (f32[512]{0:T(512)S(1)}, f32[512]{0:T(512)S(1)}, f32[1216,512]{1,0:T(8,128)}) fusion(f32[512]{0:T(512)S(1)} %bitcast.224, f32[1216,512]{1,0:T(8,128)S(1)} %copy-done.59, f32[512]{0:T(512)S(1)} %bitcast.222, f32[512]{0:T(512)S(1)} %bitcast.226, f32[512]{0:T(512)S(1)} %bitcast.227, bf16[4608,512]{1,0:T(8,128)(2,1)S(1)} %bitcast.146, ...), kind=kOutput, calls=%fused_computation.153 | convolution fusion | flops 5769559040 | bytes 20918272 | tf_op jit(solution)/shard_map/dot_general | solution.py:55
  307.5 3.7 back_one.1
  311.3 12.6 %convolution_convert_fusion = bf16[4608,512]{1,0:T(8,128)(2,1)} fusion(bf16[1216,4608]{1,0:T(8,128)(2,1)} %get-tuple-element.62, bf16[1216,512]{1,0:T(8,128)(2,1)S(1)} %copy-done.4), kind=kOutput, calls=%fused_computation.8 | convolution fusion | flops 5740167168 | bytes 17170432 | tf_op jit(solution)/shard_map/dot_general | solution.py:43
  323.9 4.6 stack.86
  328.6 8.5 %convolution_convert_fusion.3 = bf16[2048,512]{1,0:T(8,128)(2,1)} fusion(f32[1216,512]{1,0:T(8,128)} %get-tuple-element.176, f32[1216,512]{1,0:T(8,128)} %get-tuple-element.61, f32[512]{0:T(512)S(1)} %bitcast.216, f32[512]{0:T(512)S(1)} %bitcast.214, f32[512]{0:T(512)S(1)} %bitcast.225, f32[512]{0:T(512)S(1)} %bitcast.223, f32[]{:T(128)S(6)} %mul.510, ...), kind=kOutput, calls=%fused_computation.14 | convolution fusion | flops 2566750208 | bytes 12073732 | tf_op jit(solution)/shard_map/dot_general | solution.py:43
  337.8 112.5 %reduce_gradients.1 = (bf16[1,256,512]{2,1,0:T(8,128)(2,1)}, bf16[9,64,512]{2,1,0:T(8,128)(2,1)}, bf16[1,256,512]{2,1,0:T(8,128)(2,1)}, bf16[256,2048]{1,0:T(8,1...) custom-call(bf16[1,4,2,256,512]{4,3,2,1,0:T(8,128)(2,1)} %bitcast.163, ...), custom_call_target="tpu_custom_call" | custom-call | tf_op jit(solution)/shard_map/reduce_gradients/pallas_call | solution.py:861
  483.4 4.8 add_multiply_fusion.1
  (236 shorter events, 68.8 us)
Async XLA Ops:
  7.2 470.2 %all-reduce.5.cloned.1.call-start = ((), (), s32[]{:S(2)}) async-start(), calls=%async_computation | async-start | bytes 3145728 | tf_op jit(solution)/shard_map/psum | solution.py:1363
  15.5 8.1 %copy-start.8 = (bf16[3,3,6,8,2048]{4,3,2,1,0:T(8,128)(2,1)}, bf16[3,3,6,8,2048]{4,3,2,1,0:T(8,128)(2,1)S(1)}, u32[]{:S(2)}) copy-start(bf16[3,3,6,8,2048]{4,3,2,1,0:T(8,128)(2,1)S(1)} %copy.50) | copy-start | bytes 5308420
  29.3 125.6 %copy-start.29 = (f32[2,5120]{1,0:T(2,128)S(1)}, f32[2,5120]{1,0:T(2,128)}, u32[]{:S(2)}) copy-start(f32[2,5120]{1,0:T(2,128)} %refs_6_.1) | copy-start | bytes 122884
  29.3 128.7 %copy-start = (f32[3000,128]{1,0:T(8,128)S(1)}, f32[3000,128]{1,0:T(8,128)}, u32[]{:S(2)}) copy-start(f32[3000,128]{1,0:T(8,128)} %proto_ref.1) | copy-start | bytes 4608004
  29.3 128.7 %copy-start.1 = (bf16[2,960,128]{2,1,0:T(8,128)(2,1)S(1)}, bf16[2,960,128]{2,1,0:T(8,128)(2,1)}, u32[]{:S(2)}) copy-start(bf16[2,960,128]{2,1,0:T(8,128)(2,1)} %queue_ref.3) | copy-start | bytes 1474564
  197.1 51.2 %copy-start.52 = (f32[1,512]{1,0:T(1,128)}, f32[1,512]{1,0:T(1,128)S(1)}, u32[]{:S(2)}) copy-start(f32[1,512]{1,0:T(1,128)S(1)} %get-tuple-element.153) | copy-start | bytes 6148
  197.1 51.2 %copy-start.53 = (f32[1,512]{1,0:T(1,128)}, f32[1,512]{1,0:T(1,128)S(1)}, u32[]{:S(2)}) copy-start(f32[1,512]{1,0:T(1,128)S(1)} %get-tuple-element.154) | copy-start | bytes 6148
  198.6 12.8 %copy-start.48 = (f32[512]{0:T(512)}, f32[512]{0:T(512)S(1)}, u32[]{:S(2)}) copy-start(f32[512]{0:T(512)S(1)} %get-tuple-element.84) | copy-start | bytes 6148
  198.6 12.8 %copy-start.50 = (f32[512]{0:T(512)}, f32[512]{0:T(512)S(1)}, u32[]{:S(2)}) copy-start(f32[512]{0:T(512)S(1)} %get-tuple-element.85) | copy-start | bytes 6148
  238.9 9.4 %copy-start.36 = (f32[1,2048]{1,0:T(1,128)}, f32[1,2048]{1,0:T(1,128)S(1)}, u32[]{:S(2)}) copy-start(f32[1,2048]{1,0:T(1,128)S(1)} %get-tuple-element.158) | copy-start | bytes 24580
  238.9 9.4 %copy-start.38 = (f32[1,2048]{1,0:T(1,128)}, f32[1,2048]{1,0:T(1,128)S(1)}, u32[]{:S(2)}) copy-start(f32[1,2048]{1,0:T(1,128)S(1)} %get-tuple-element.159) | copy-start | bytes 24580
  239.1 9.3 %copy-start.19 = (f32[1216,512]{1,0:T(8,128)S(1)}, f32[1216,512]{1,0:T(8,128)}, u32[]{:S(2)}) copy-start(f32[1216,512]{1,0:T(8,128)} %get-tuple-element.59) | copy-start | bytes 7471108
  239.1 9.3 %copy-start.60 = (bf16[4,2,256,512]{3,2,1,0:T(8,128)(2,1)S(1)}, bf16[4,2,256,512]{3,2,1,0:T(8,128)(2,1)}, u32[]{:S(2)}) copy-start(bf16[4,2,256,512]{3,2,1,0:T(8,128)(2,1)} %get-tuple-element.58) | copy-start | bytes 6291460
  267.1 8.7 %copy-start.10 = (f32[2,256,512]{2,1,0:T(8,128)S(1)}, f32[2,256,512]{2,1,0:T(8,128)}, u32[]{:S(2)}) copy-start(f32[2,256,512]{2,1,0:T(8,128)} %param.27) | copy-start | bytes 3145732
  267.1 9.4 %copy-start.5 = (f32[256,2048]{1,0:T(8,128)S(1)}, f32[256,2048]{1,0:T(8,128)}, u32[]{:S(2)}) copy-start(f32[256,2048]{1,0:T(8,128)} %param.29) | copy-start | bytes 6291460
  287.9 6.8 %copy-start.59 = (f32[1216,512]{1,0:T(8,128)S(1)}, f32[1216,512]{1,0:T(8,128)}, u32[]{:S(2)}) copy-start(f32[1216,512]{1,0:T(8,128)} %get-tuple-element.61) | copy-start | bytes 7471108
  311.2 17.3 %copy-start.45 = (f32[1,512]{1,0:T(1,128)S(1)}, f32[1,512]{1,0:T(1,128)}, u32[]{:S(2)}) copy-start(f32[1,512]{1,0:T(1,128)} %copy-done.44) | copy-start | bytes 6148
  311.3 17.3 %copy-start.47 = (f32[1,512]{1,0:T(1,128)S(1)}, f32[1,512]{1,0:T(1,128)}, u32[]{:S(2)}) copy-start(f32[1,512]{1,0:T(1,128)} %copy-done.46) | copy-start | bytes 6148
  311.3 17.3 %copy-start.54 = (f32[1,512]{1,0:T(1,128)S(1)}, f32[1,512]{1,0:T(1,128)}, u32[]{:S(2)}) copy-start(f32[1,512]{1,0:T(1,128)} %get-tuple-element.139) | copy-start | bytes 6148
  328.6 8.5 %copy-start.37 = (f32[1,2048]{1,0:T(1,128)S(1)}, f32[1,2048]{1,0:T(1,128)}, u32[]{:S(2)}) copy-start(f32[1,2048]{1,0:T(1,128)} %copy-done.36) | copy-start | bytes 24580
  328.6 8.5 %copy-start.39 = (f32[1,2048]{1,0:T(1,128)S(1)}, f32[1,2048]{1,0:T(1,128)}, u32[]{:S(2)}) copy-start(f32[1,2048]{1,0:T(1,128)} %copy-done.38) | copy-start | bytes 24580
  337.8 113.4 %copy-start.63 = (f32[5]{0:T(128)S(1)}, f32[5]{0:T(128)}, u32[]{:S(2)}) copy-start(f32[5]{0:T(128)} %constant.63) | copy-start | bytes 64
  337.8 121.5 %copy-start.27 = (f32[2,256,512]{2,1,0:T(8,128)S(1)}, f32[2,256,512]{2,1,0:T(8,128)}, u32[]{:S(2)}) copy-start(f32[2,256,512]{2,1,0:T(8,128)} %param.33) | copy-start | bytes 3145732
  450.3 8.9 %copy-start.11 = (f32[2,256,512]{2,1,0:T(8,128)S(1)}, f32[2,256,512]{2,1,0:T(8,128)}, u32[]{:S(2)}) copy-start(f32[2,256,512]{2,1,0:T(8,128)} %param.27) | copy-start | bytes 3145732
  (45 other events, 176.3 us)
Sparse Core Ops, SparseCore 0:
  195.9 135.2 all-reduce.4

commit v5 on v4

--- a/solution.py
+++ b/solution.py
@@ -90,57 +90,6 @@
     own.wait()
     for copy in copies:
         copy.wait()
-
-
-def relay_kernel(scatter, x_ref, o_ref, *rest):
-    sub = lax.axis_index("sub")
-    row, core = sub // 2, sub % 2
-    row_sub, core_sub = 2 * (1 - row) + core, 2 * row + (1 - core)
-    barrier = pltpu.get_barrier_semaphore()
-    for peer in (row_sub, core_sub):
-        pl.semaphore_signal(barrier, inc=1, device_id={"sub": peer}, device_id_type=MESH)
-    pl.semaphore_wait(barrier, 2)
-    links = Links(*rest[-2:])
-    if scatter:
-        landed, summed, arrived = rest[:3]
-        pair = [
-            links(x_ref.at[2 * line + (1 - core)], landed.at[line], {"sub": core_sub})
-            for line in (1 - row, row)
-        ]
-        pair[0].wait()
-        summed[...] = plus(x_ref[2 * (1 - row) + core], landed[1 - row]).astype(summed.dtype)
-        over = links(summed, arrived, {"sub": row_sub})
-        pair[1].wait()
-        value = plus(x_ref[sub], landed[row])
-        over.wait()
-        o_ref[...] = value + arrived[...].astype(jnp.float32)
-    else:
-        over = links(x_ref, o_ref.at[sub], {"sub": row_sub})
-        pair = links(x_ref, o_ref.at[sub], {"sub": core_sub})
-        o_ref[sub] = x_ref[...]
-        over.wait()
-        last = links(o_ref.at[row_sub], o_ref.at[row_sub], {"sub": core_sub})
-        pair.wait()
-        last.wait()
-
-
-def relay(collective_id, values, scatter, name):
-    block = values.shape[1:] if scatter else values.shape
-    held = [pltpu.VMEM((2,) + block, values.dtype)] + [pltpu.VMEM(block, values.dtype)] * 2
-    return pl.pallas_call(
-        functools.partial(relay_kernel, scatter),
-        out_shape=jax.ShapeDtypeStruct(
-            block if scatter else (4,) + block, jnp.float32 if scatter else values.dtype
-        ),
-        in_specs=[pl.BlockSpec(memory_space=pltpu.VMEM)],
-        out_specs=pl.BlockSpec(memory_space=pltpu.VMEM),
-        scratch_shapes=(held if scatter else [])
-        + [pltpu.SemaphoreType.DMA((3,)), pltpu.SemaphoreType.DMA((3,))],
-        compiler_params=pltpu.CompilerParams(
-            collective_id=collective_id, has_side_effects=True, vmem_limit_bytes=32 * MIB
-        ),
-        name=name,
-    )(values)
 
 
 class Exchanger:
@@ -316,10 +265,10 @@
 def forward_kernel(n_dp, images, *refs):
     w_first, w_mid, w_last, w_hid, w_out, x_ref, norm_ref, live_ref = refs[:8]
     (
-        o_mid, o_last, o_hid, o_out, o_columns, o_one, o_two, o_act, o_stat, o_pooled, o_live,
+        o_mid, o_last, o_hid, o_out, o_one, o_two, o_act, o_stat, o_pooled, o_live, o_slope,
     ) = refs[8:19]
     (
-        first_w, mid_w, last_w, columns, act_one, act_two, one, two, three, total, pool,
+        first_w, mid_w, last_w, out_w, columns, act_one, act_two, one, two, three, total, pool,
         sums_a, land_a, sums_b, land_b, sums_c, land_c, pooled, send_sem, recv_sem, own_sem,
     ) = refs[19:]
     at = Place(n_dp)
@@ -334,30 +283,37 @@
     mask = live_ref[...][:, :1]
     half = middle // 2
 
-    def flat(source, target, split):
+    def flat(source, target, part, parts, split):
+        height = source.shape[0] // parts
+        some = pl.ds(part * height, height)
         return (
-            lambda cols: source.at[:, cols],
-            lambda near, far, cols: target.at[near, far, :, cols],
+            lambda cols: source.at[some, cols],
+            lambda near, far, cols: target.at[near, far, some, cols],
             split,
         )
 
-    def taps(start, split):
-        some = pl.ds(start, 3)
+    def taps(start, size):
+        some = pl.ds(start, size)
         return (
             lambda cols: w_mid.at[some, :, cols],
             lambda near, far, cols: mid_w.at[some, near, far, :, cols],
-            split,
+            4,
         )
 
-    pieces = [
-        flat(w_first, first_w, 4),
-        taps(0, 4),
-        taps(3, 2),
-        taps(6, 4),
-        flat(w_last, last_w, 2),
-        flat(w_hid, o_hid, 1),
-        flat(w_out, o_out, 1),
-    ]
+    quarter = w_out.shape[0] // 4
+    out_rows = pl.ds(at.sub * quarter, quarter)
+    pieces = [flat(w_first, first_w, part, 2, 4) for part in range(2)]
+    pieces += [taps(0, 1), taps(1, 2), taps(3, 1), taps(4, 2), taps(6, 1), taps(7, 2)]
+    pieces += [flat(w_last, last_w, part, 4, 2) for part in range(4)]
+    trunk_pieces = len(pieces)
+    pieces += [flat(w_hid, o_hid, part, 4, 1) for part in range(4)]
+    pieces.append(
+        (
+            lambda cols: w_out.at[out_rows],
+            lambda near, far, cols: out_w.at[near, far],
+            1,
+        )
+    )
     count = len(pieces)
     mine = {4: lanes_of(at.sub), 2: lanes_of(at.core, half), 1: ALL}
     own, first, second, third, fourth = [], [], [], [], []
@@ -366,38 +322,44 @@
         copy = pltpu.make_async_copy(source(cols), target(at.near, at.far, cols), own_sem.at[index])
         copy.start()
         own.append(copy)
-    for source, target, split in pieces:
-        cols = mine[split]
-        first.append(
-            [
-                links(source(cols), target(at.near, at.far, cols), at.near_peer(hop))
-                for hop in range(1, at.span)
-            ]
-        )
+
+    def begin(index):
+        if index < count:
+            source, target, split = pieces[index]
+            cols = mine[split]
+            first.append(
+                [
+                    links(source(cols), target(at.near, at.far, cols), at.near_peer(hop))
+                    for hop in range(1, at.span)
+                ]
+            )
+
+    for index in range(3):
+        begin(index)
+    lag = 2
+    ticks = count + 2 * lag
 
     def tick(now):
         if now < count:
             source, target, split = pieces[now]
             own[now].wait()
             wait_all(first[now])
+            begin(now + 3)
             slab = target(ALL, at.far, mine[split])
             second.append(links(slab, slab, at.far_peer))
-        if 0 <= now - 1 < count:
-            source, target, split = pieces[now - 1]
-            second[now - 1].wait()
+        past = now - lag
+        if 0 <= past < count:
+            source, target, split = pieces[past]
+            second[past].wait()
             slab = target(ALL, ALL, mine[split])
             third.append(links(slab, slab, at.row_peer) if split == 4 else None)
-            if split == 2:
-                fourth.append([links(slab, slab, at.core_peer)])
-            elif split == 1:
-                fourth.append([])
-            else:
-                fourth.append(None)
-        if 0 <= now - 2 < count and pieces[now - 2][2] == 4:
-            source, target, split = pieces[now - 2]
-            third[now - 2].wait()
+            fourth.append([links(slab, slab, at.core_peer)] if split == 2 else [])
+        past = now - 2 * lag
+        if 0 <= past < count and pieces[past][2] == 4:
+            source, target, split = pieces[past]
+            third[past].wait()
             slabs = [target(ALL, ALL, cols) for cols in (mine[4], lanes_of(at.row_sub))]
-            fourth[now - 2] = [links(slab, slab, at.core_peer) for slab in slabs]
+            fourth[past] = [links(slab, slab, at.core_peer) for slab in slabs]
 
     def arrived(index):
         wait_all(fourth[index])
@@ -417,10 +379,10 @@
         scale = norm_ref[pl.ds(0, 1), pl.ds(start, wide)] * inverse
         return scale, norm_ref[pl.ds(1, 1), pl.ds(start, wide)] - scale * mean
 
-    for now in range(4):
+    for now in range(6):
         tick(now)
     arrived(0)
-    tick(4)
+    arrived(1)
 
     total[...] = jnp.zeros_like(total)
 
@@ -440,7 +402,7 @@
     live = jnp.sum(mask, 0, keepdims=True)
     sums_a[pl.ds(2, 1), :] = jnp.broadcast_to(live, (1, middle))
     sums.start(sums_a, land_a)
-    tick(5)
+    tick(6)
     value = sums.finish()
     per_image = rows // images
     lives = value[2:3, :1]
@@ -462,16 +424,15 @@
     step_act(one, act_one)
     save = [pltpu.make_async_copy(one, o_one, own_sem.at[count])]
     save[-1].start()
-    tick(6)
+    tick(7)
     fill_columns(columns, act_one, images, False)
-    save.append(pltpu.make_async_copy(columns, o_columns, own_sem.at[count + 1]))
-    save[-1].start()
 
     total[...] = jnp.zeros_like(total)
     for part in range(3):
-        arrived(1 + part)
-        if part == 0:
-            tick(7)
+        for now in range(2):
+            tick(8 + 2 * part + now)
+        for index in range(2):
+            arrived(2 + 2 * part + index)
 
         def step_two(index, carry):
             span = rows_at(index * tile, tile)
@@ -492,7 +453,6 @@
     save[-1].start()
     pack(sums_b, middle)
     sums.start(sums_b, land_b)
-    tick(8)
     scale, shift = settle(sums.finish(), count_all, middle, middle)
     step_act(two, act_two)
     save.append(pltpu.make_async_copy(two, o_two, own_sem.at[count + 3]))
@@ -500,7 +460,10 @@
     save.append(pltpu.make_async_copy(act_two, o_act, own_sem.at[count + 4]))
     save[-1].start()
 
-    arrived(4)
+    for now in range(14, trunk_pieces + 2 * lag):
+        tick(now)
+    for index in range(trunk_pieces - 4, trunk_pieces):
+        arrived(index)
     save.append(pltpu.make_async_copy(last_w, o_last, own_sem.at[count + 5]))
     save[-1].start()
     total[...] = jnp.zeros_like(total)
@@ -519,9 +482,22 @@
     lax.fori_loop(0, 4, step_three, 0)
     pack(sums_c, channels)
     sums.start(sums_c, land_c)
+    for now in range(trunk_pieces + 2 * lag, ticks):
+        tick(now)
+    some = at.span // 4
+    out_own = out_w.at[pl.ds(at.sub * some, some)]
+    into = o_out.at[:, :, out_rows]
+    own.append(pltpu.make_async_copy(out_own, into, own_sem.at[count - 1]))
+    own[-1].start()
+    out_copies = [
+        links(out_w.at[pl.ds(peer["sub"] * some, some)], into, peer) for peer in at.sub_peers()
+    ]
     scale, shift = settle(sums.finish(), count_all, 2 * middle, channels)
 
     pool[...] = jnp.zeros_like(pool)
+    o_slope[...] = jnp.zeros_like(o_slope)
+    wide = pl.ds(2 * middle, channels)
+    center = o_stat[pl.ds(0, 1), wide] * o_stat[pl.ds(1, 1), wide]
     base = 0
     for extent, crops in ((BIG, NBIG), (SMALL, NSMALL)):
         lines = crops * images
@@ -533,8 +509,15 @@
                 cols = pl.ds(start, 512)
                 pre = three[span, cols] * scale[:, start : start + 512]
                 pre = pre + shift[:, start : start + 512] + x_ref[span, cols].astype(jnp.float32)
-                value = pre * sigmoid_of(pre)
+                sigma = sigmoid_of(pre)
+                value = pre * sigma
+                slope = sigma + value * (1.0 - sigma)
+                normal = three[span, cols] * o_stat[1:2, 2 * middle + start : 2 * middle + start + 512]
+                normal = normal - center[:, start : start + 512]
                 pool[into, cols] += jnp.sum(value.reshape(extent, lines, 512), 0)
+                o_slope[0, into, cols] += jnp.sum(slope.reshape(extent, lines, 512), 0)
+                slope = slope * normal
+                o_slope[1, into, cols] += jnp.sum(slope.reshape(extent, lines, 512), 0)
             return carry
 
         lax.fori_loop(0, extent, step_out, 0)
@@ -548,6 +531,8 @@
     last = links(o_pooled.at[at.row_sub], o_pooled.at[at.row_sub], at.core_peer)
     pair.wait()
     last.wait()
+    own[-1].wait()
+    wait_all(out_copies)
     for copy in save:
         copy.wait()
 
@@ -558,7 +543,7 @@
     rows, channels = inputs.shape
     some = jax.ShapeDtypeStruct
     low, full = jnp.bfloat16, jnp.float32
-    copies = 7 * (span + 4) + 12
+    copies = 17 * (span + 4) + 16
     vmem, anywhere = pl.BlockSpec(memory_space=pltpu.VMEM), pl.BlockSpec(memory_space=pl.ANY)
     return pl.pallas_call(
         functools.partial(forward_kernel, n_dp, images),
@@ -566,21 +551,22 @@
             some((TAPS, span, 2, mid.shape[1], middle), low),
             some((span, 2, height, middle), low),
             some((span, 2, height, hid.shape[1]), low),
-            some((span, 2, height, out.shape[1]), low),
-            some((rows, TAPS * middle), low),
+            some((span // 4, 2, height, out.shape[1]), low),
             some((rows, middle), full),
             some((rows, middle), full),
             some((rows, middle), low),
             some((2, 2 * middle + channels), full),
             some((4, CROPS * images, channels), low),
             some((4, 8, LANES), full),
+            some((2, CROPS * images, channels), full),
         ),
         in_specs=[vmem] * 8,
-        out_specs=(anywhere,) * 8 + (vmem,) * 3,
+        out_specs=(anywhere,) * 7 + (vmem,) * 4,
         scratch_shapes=[
             pltpu.VMEM((span, 2, height, middle), low),
             pltpu.VMEM((TAPS, span, 2, mid.shape[1], middle), low),
             pltpu.VMEM((span, 2, height, middle), low),
+            pltpu.VMEM((span, 2, height // 4, out.shape[1]), low),
             pltpu.VMEM((rows, TAPS * middle), low),
             pltpu.VMEM((rows, middle), low),
             pltpu.VMEM((rows, middle), low),
@@ -598,7 +584,7 @@
             pltpu.VMEM((CROPS * images, channels), low),
             pltpu.SemaphoreType.DMA((copies,)),
             pltpu.SemaphoreType.DMA((copies,)),
-            pltpu.SemaphoreType.DMA((7 + 6,)),
+            pltpu.SemaphoreType.DMA((17 + 6,)),
         ],
         compiler_params=pltpu.CompilerParams(
             collective_id=collective_id, has_side_effects=True, vmem_limit_bytes=60 * MIB
@@ -611,136 +597,81 @@
     return left.astype(jnp.float32) + right.astype(jnp.float32)
 
 
-def reduce_kernel(n_dp, *refs):
-    g_first, g_mid, g_last, g_hid, g_some, g_vec = refs[:6]
-    o_first, o_mid, o_last, o_hid, o_out, o_vec, o_sq = refs[6:13]
-    bufs = refs[13:-13]
+def piece_list(n_dp, height, mid_height, refs):
+    first, mid, last = refs
+    half, quarter = height // 2, height // 4
+    pieces = [last + (0, 1, part * half, half, 2) for part in range(2)]
+    for start, taps in ((0, 1), (1, 1), (2, 1), (3, 1), (4, 1), (5, 1), (6, 1), (7, 2)):
+        pieces.append(mid + (start, taps, 0, mid_height, 1))
+    return pieces + [first + (0, 1, part * quarter, quarter, 0) for part in range(4)]
+
+
+def backward_kernel(n_dp, images, *refs):
+    p_pool, slope_ref, stat_ref, norm_ref, live_ref, lives_ref, extra_ref, g_hid, g_some = refs[:9]
+    h_x, h_one, h_two, h_act, h_last, h_mid = refs[9:15]
+    o_first, o_mid, o_last, o_hid, o_out, o_vec, o_sq = refs[15:22]
     (
-        hid_in, hid_sum, hid_land, g_out, out_in, out_sum, out_land, vec_land, sq_mine, sq_land,
-        send_sem, recv_sem, own_sem,
-    ) = refs[-13:]
+        x_ref, one, two, act_two, last_w, mid_w, act_one, wide_low, work, thin_low, g_first, g_mid,
+        g_last, total, pair_land, pair_sum, row_land, grad_pool, sums_a, land_a, sums_b, land_b,
+        sums_c, land_c, hid_in, hid_sum, hid_land, g_out, out_in, out_sum, out_land, vec, vec_land,
+        sq_mine, sq_land, send_sem, recv_sem, own_sem,
+    ) = refs[22:60]
+    bufs = refs[60:]
     at = Place(n_dp)
     links = Links(send_sem, recv_sem)
     span = at.span
     at.greet(at.dp_peers() + at.sub_peers())
     low = jnp.bfloat16
-    wide = g_vec.shape[1] // 4
-    vec_cols = lanes_of(at.sub, wide)
-    vec_copies = [
-        links(g_vec.at[:, vec_cols], vec_land.at[hop], peer)
-        for hop, peer in enumerate(at.dp_peers())
+    rows, channels = x_ref.shape
+    middle = one.shape[1]
+    height = g_last.shape[3]
+    mask = live_ref[...][:, :1]
+    tile = rows // 4
+
+    loads = {}
+    for index, (name, source, target) in enumerate(
+        (
+            ("act", h_act, act_two), ("last", h_last, last_w), ("x", h_x, x_ref), ("two", h_two, two),
+            ("one", h_one, one), ("mid", h_mid, mid_w),
+        )
+    ):
+        loads[name] = pltpu.make_async_copy(source, target, own_sem.at[index])
+        loads[name].start()
+
+    pair = [
+        links(p_pool.at[2 * line + (1 - at.core)], pair_land.at[line], at.core_peer)
+        for line in (1 - at.row, at.row)
     ]
-    pieces = [(g_last, o_last, 0, 1), (g_mid, o_mid, 0, 3), (g_mid, o_mid, 3, 3), (g_mid, o_mid, 6, 3), (g_first, o_first, 0, 1)]
-    count = len(pieces)
-    mine, beside = lanes_of(at.sub), lanes_of(at.row_sub)
-
+    far_copies = [links(g_hid.at[:, 1 - at.far], hid_in, at.far_peer)]
     some = g_some.shape[0]
     block = g_out.at[pl.ds(at.sub * some, some)]
-    own_out = pltpu.make_async_copy(g_some, block, own_sem)
+    own_out = pltpu.make_async_copy(g_some, block, own_sem.at[6])
     own_out.start()
     out_copies = [links(g_some, block, peer) for peer in at.sub_peers()]
-
-    pair = []
-    for index, (source, target, start, taps) in enumerate(pieces):
-        land = bufs[4 * index]
-        sent = []
-        for row in range(2):
-            cols = lanes_of(2 * row + (1 - at.core))
-            sent.append(
-                links(source.at[pl.ds(start, taps), :, :, :, cols], land.at[row], at.core_peer)
-            )
-        pair.append(sent)
+    pair[0].wait()
+    pair_sum[...] = plus(p_pool[2 * (1 - at.row) + at.core], pair_land[1 - at.row]).astype(low)
+    over = links(pair_sum, row_land, at.row_peer)
+    pair[1].wait()
 
     wholes = [(g_hid, hid_in, hid_sum, hid_land), (g_out, out_in, out_sum, out_land)]
-    far_copies = [links(g_hid.at[:, 1 - at.far], hid_in, at.far_peer)]
 
     def whole_far(which):
-        source, landed, total, land = wholes[which]
+        source, landed, summed, land = wholes[which]
         far_copies[which].wait()
         for near in range(span):
-            total[near] = plus(source[near, at.far], landed[near]).astype(low)
+            summed[near] = plus(source[near, at.far], landed[near]).astype(low)
         return [
-            links(total.at[at.near_index(hop)], land.at[hop - 1], at.near_peer(hop))
+            links(summed.at[at.near_index(hop)], land.at[hop - 1], at.near_peer(hop))
             for hop in range(1, span)
         ]
 
     def whole_near(which, copies):
-        source, landed, total, land = wholes[which]
+        source, landed, summed, land = wholes[which]
         wait_all(copies)
-        value = total[at.near].astype(jnp.float32)
+        value = summed[at.near].astype(jnp.float32)
         for hop in range(1, span):
             value = value + land[hop - 1].astype(jnp.float32)
         return value.astype(low)
-
-    def blocks(taps, body):
-        def step(index, carry):
-            rest = index // 2
-            body(rest // span, rest % span, index % 2)
-            return carry
-
-        lax.fori_loop(0, taps * span * 2, step, 0)
-
-    def lines(taps, body):
-        def step(index, carry):
-            body(index // span, index % span)
-            return carry
-
-        lax.fori_loop(0, taps * span, step, 0)
-
-    def stage_pair(index):
-        source, target, start, taps = pieces[index]
-        land = bufs[4 * index]
-        wait_all(pair[index])
-        for row in range(2):
-            cols = lanes_of(2 * row + at.core)
-
-            def body(tap, near, far):
-                land[row, tap, near, far] = plus(
-                    source[start + tap, near, far, :, cols], land[row, tap, near, far]
-                ).astype(low)
-
-            blocks(taps, body)
-        if index % 2 == 0:
-            return links(land.at[1 - at.row], bufs[4 * index + 1], at.row_peer)
-        return links(land.at[:, :, :, 1 - at.far], bufs[4 * index + 1], at.far_peer)
-
-    def stage_second(index, copy):
-        source, target, start, taps = pieces[index]
-        held, land, total = bufs[4 * index], bufs[4 * index + 1], bufs[4 * index + 2]
-        copy.wait()
-        if index % 2 == 0:
-
-            def body(tap, near, far):
-                land[tap, near, far] = plus(
-                    held[at.row, tap, near, far], land[tap, near, far]
-                ).astype(low)
-
-            blocks(taps, body)
-            return links(land.at[:, :, 1 - at.far], total, at.far_peer)
-        for row in range(2):
-
-            def body(tap, near):
-                land[row, tap, near] = plus(
-                    held[row, tap, near, at.far], land[row, tap, near]
-                ).astype(low)
-
-            lines(taps, body)
-        return links(land.at[1 - at.row], total, at.row_peer)
-
-    def stage_third(index, copy):
-        source, target, start, taps = pieces[index]
-        held, total, land = bufs[4 * index + 1], bufs[4 * index + 2], bufs[4 * index + 3]
-        copy.wait()
-
-        def body(tap, near):
-            part = held[tap, near, at.far] if index % 2 == 0 else held[at.row, tap, near]
-            total[tap, near] = plus(part, total[tap, near]).astype(low)
-
-        lines(taps, body)
-        return [
-            links(total.at[:, at.near_index(hop)], land.at[hop - 1], at.near_peer(hop))
-            for hop in range(1, span)
-        ]
 
     sq_mine[0] = jnp.zeros_like(sq_mine[0])
 
@@ -750,58 +681,325 @@
         for lane in range(0, line.shape[1], LANES):
             sq_mine[0, pl.ds(matrix, 1), :] += line[:, lane : lane + LANES]
 
-    def stage_near(index, copies):
-        source, target, start, taps = pieces[index]
-        total, land = bufs[4 * index + 2], bufs[4 * index + 3]
-        wait_all(copies)
-        for tap in range(taps):
-            value = total[tap, at.near].astype(jnp.float32)
-            for hop in range(1, span):
-                value = value + land[hop - 1, tap].astype(jnp.float32)
-            value = value.astype(low)
-            squares_of({0: 2, count - 1: 0}.get(index, 1), value)
-            target[start + tap, :, mine] = value
-        slab = target.at[pl.ds(start, taps), :, mine]
-        return links(slab, slab, at.row_peer)
-
-    def stage_row(index, copy):
-        source, target, start, taps = pieces[index]
-        copy.wait()
-        sent = []
-        for cols in (mine, beside):
-            slab = target.at[pl.ds(start, taps), :, cols]
-            sent.append(links(slab, slab, at.core_peer))
-        return sent
-
-    hold = {}
-    final = []
-    for tick in range(count + 4):
-        if tick < count:
-            hold[0, tick] = stage_pair(tick)
-        if tick == 0:
-            near_hid = whole_far(0)
-            own_out.wait()
-            wait_all(out_copies)
-            far_copies.append(links(g_out.at[:, 1 - at.far], out_in, at.far_peer))
-        if tick == 1:
-            near_out = whole_far(1)
-        if 0 <= tick - 1 < count:
-            hold[1, tick - 1] = stage_second(tick - 1, hold[0, tick - 1])
-        if 0 <= tick - 2 < count:
-            hold[2, tick - 2] = stage_third(tick - 2, hold[1, tick - 2])
-        if tick == 2:
-            hid_slabs = [
-                o_hid.at[:, lanes_of(which, g_hid.shape[3])] for which in (at.sub, at.row_sub)
+    pieces = piece_list(
+        n_dp, height, g_mid.shape[3], ((g_first, o_first), (g_mid, o_mid), (g_last, o_last))
+    )
+    mine, beside = lanes_of(at.sub), lanes_of(at.row_sub)
+    state = [0] * len(pieces)
+    flight = [None] * len(pieces)
+
+    def loop(count, body):
+        def step(index, carry):
+            body(index)
+            return carry
+
+        lax.fori_loop(0, count, step, 0)
+
+    def go(index):
+        source, target, start, taps, line, size, matrix = pieces[index]
+        held, second, third, nears = bufs[4 * index : 4 * index + 4]
+        stage = state[index]
+        state[index] += 1
+        row_first = index % 2 == 0
+        lines, some = pl.ds(line, size), pl.ds(start, taps)
+        if stage == 0:
+            flight[index] = [
+                links(
+                    source.at[some, :, :, lines, lanes_of(2 * row + (1 - at.core))],
+                    held.at[row],
+                    at.core_peer,
+                )
+                for row in range(2)
             ]
+            return
+        wait_all(flight[index])
+        if stage == 1:
+            for row in range(2):
+                cols = lanes_of(2 * row + at.core)
+
+                def body(at_block):
+                    tap, near, far = at_block // (2 * span), at_block // 2 % span, at_block % 2
+                    held[row, tap, near, far] = plus(
+                        source[start + tap, near, far, lines, cols], held[row, tap, near, far]
+                    ).astype(low)
+
+                loop(taps * span * 2, body)
+            if row_first:
+                flight[index] = [links(held.at[1 - at.row], second, at.row_peer)]
+            else:
+                flight[index] = [links(held.at[:, :, :, 1 - at.far], second, at.far_peer)]
+        elif stage == 2:
+            if row_first:
+
+                def body(at_block):
+                    tap, near, far = at_block // (2 * span), at_block // 2 % span, at_block % 2
+                    second[tap, near, far] = plus(
+                        held[at.row, tap, near, far], second[tap, near, far]
+                    ).astype(low)
+
+                loop(taps * span * 2, body)
+                flight[index] = [links(second.at[:, :, 1 - at.far], third, at.far_peer)]
+            else:
+
+                def body(at_block):
+                    row, tap, near = at_block // (taps * span), at_block // span % taps, at_block % span
+                    second[row, tap, near] = plus(
+                        held[row, tap, near, at.far], second[row, tap, near]
+                    ).astype(low)
+
+                loop(taps * span * 2, body)
+                flight[index] = [links(second.at[1 - at.row], third, at.row_peer)]
+        elif stage == 3:
+
+            def body(at_block):
+                tap, near = at_block // span, at_block % span
+                part = second[tap, near, at.far] if row_first else second[at.row, tap, near]
+                third[tap, near] = plus(part, third[tap, near]).astype(low)
+
+            loop(taps * span, body)
+            flight[index] = [
+                links(third.at[:, at.near_index(hop)], nears.at[hop - 1], at.near_peer(hop))
+                for hop in range(1, span)
+            ]
+        elif stage == 4:
+            for tap in range(taps):
+                value = third[tap, at.near].astype(jnp.float32)
+                for hop in range(1, span):
+                    value = value + nears[hop - 1, tap].astype(jnp.float32)
+                value = value.astype(low)
+                squares_of(matrix, value)
+                target[start + tap, lines, mine] = value
+            slab = target.at[some, lines, mine]
+            flight[index] = [links(slab, slab, at.row_peer)]
+        elif stage == 5:
+            slabs = [target.at[some, lines, cols] for cols in (mine, beside)]
+            flight[index] = [links(slab, slab, at.core_peer) for slab in slabs]
+
+    def go_pair(number):
+        go(2 * number)
+        go(2 * number + 1)
+
+    count_all = jnp.sum(lives_ref[...][:, :1, :1], 0) * float(rows // images)
+    sums = GroupSums(at, links)
+
+    def terms(start, wide):
+        cols = pl.ds(start, wide)
+        mean, inverse = stat_ref[pl.ds(0, 1), cols], stat_ref[pl.ds(1, 1), cols]
+        scale = norm_ref[pl.ds(0, 1), cols] * inverse
+        return mean * inverse, inverse, scale, norm_ref[pl.ds(1, 1), cols] - scale * mean
+
+    def slope_of(pre):
+        sigma = sigmoid_of(pre)
+        return sigma + pre * sigma * (1.0 - sigma)
+
+    def pack(target, wide):
+        target[pl.ds(0, 1), :] = jnp.sum(total[0, :, :wide], 0, keepdims=True)
+        target[pl.ds(1, 1), :] = jnp.sum(total[1, :, :wide], 0, keepdims=True)
+
+    center_one, inverse_one, scale_one, shift_one = terms(0, middle)
+    center_two, inverse_two, scale_two, shift_two = terms(middle, middle)
+    center_three, inverse_three, scale_three, shift_three = terms(2 * middle, channels)
+    loads["one"].wait()
+
+    def step_act(index):
+        span_rows = rows_at(index * tile, tile)
+        pre = one[span_rows, :] * scale_one + shift_one
+        act_one[span_rows, :] = (pre * sigmoid_of(pre)).astype(low)
+
+    loop(4, step_act)
+    own_out.wait()
+    wait_all(out_copies)
+    far_copies.append(links(g_out.at[:, 1 - at.far], out_in, at.far_peer))
+    value = plus(p_pool[at.sub], pair_land[at.row])
+    over.wait()
+    value = value + row_land[...].astype(jnp.float32)
+    big = NBIG * images
+    grad_pool[pl.ds(0, big), :] = value[:big] * (1.0 / (BIG * BIG))
+    grad_pool[pl.ds(big, NSMALL * images), :] = value[big:] * (1.0 / (SMALL * SMALL))
+    for which in range(2):
+        sums_c[pl.ds(which, 1), :] = jnp.sum(grad_pool[...] * slope_ref[which], 0, keepdims=True)
+    sums.start(sums_c, land_c)
+    loads["act"].wait()
+    loads["last"].wait()
+    loads["x"].wait()
+    both_three = sums.finish()
+    vec[...] = extra_ref[...]
+    vec[pl.ds(1, 1), :] = both_three[1:2]
+    vec[pl.ds(3, 1), :] = both_three[0:1]
+    both_three = both_three / count_all
+
+    chunk = channels // 4
+    for quarter in range(4):
+        cols = pl.ds(quarter * chunk, chunk)
+        here = slice(quarter * chunk, (quarter + 1) * chunk)
+        weights = last_w[pl.ds(quarter * (span // 4), span // 4)].reshape(chunk, middle)
+
+        def step_three(index):
+            span_rows = rows_at(index * tile, tile)
+            work[span_rows, :] = against(act_two[span_rows, :], weights)
+
+        loop(4, step_three)
+        base = 0
+        for extent, crops in ((BIG, NBIG), (SMALL, NSMALL)):
+            lines = crops * images
+            into = pl.ds(0, lines) if extent == BIG else pl.ds(big, lines)
+
+            def step_grad(index):
+                span_rows = rows_at(base + index * extent * lines, extent * lines)
+                hidden = work[span_rows, :]
+                pre = hidden * scale_three[:, here] + shift_three[:, here]
+                pre = pre + x_ref[span_rows, cols].astype(jnp.float32)
+                grad = slope_of(pre).reshape(extent, lines, chunk) * grad_pool[into, cols]
+                normal = hidden * inverse_three[:, here] - center_three[:, here]
+                back = both_three[0:1, here] + normal * both_three[1:2, here]
+                back = back.reshape(extent * crops, images, chunk) * mask
+                grad = grad.reshape(extent * crops, images, chunk) - back
+                grad = grad.reshape(extent * lines, chunk) * scale_three[:, here]
+                wide_low[span_rows, cols] = grad.astype(low)
+
+            loop(extent, step_grad)
+            base += extent * extent * lines
+
+    near_hid, near_out = whole_far(0), whole_far(1)
+
+    def norm_sums(grad, normal):
+        total[0, :, :middle] += jnp.sum(grad.reshape(tile // 8, 8, middle), 0)
+        total[1, :, :middle] += jnp.sum((grad * normal).reshape(tile // 8, 8, middle), 0)
+
+    loads["two"].wait()
+    total[...] = jnp.zeros_like(total)
+
+    def step_two(index):
+        span_rows = rows_at(index * tile, tile)
+        grad = jnp.dot(
+            wide_low[span_rows, :],
+            last_w[...].reshape(channels, middle),
+            preferred_element_type=jnp.float32,
+        )
+        grad = grad * slope_of(two[span_rows, :] * scale_two + shift_two)
+        work[span_rows, :] = grad
+        norm_sums(grad, two[span_rows, :] * inverse_two - center_two)
+
+    loop(4, step_two)
+    pack(sums_a, middle)
+    sums.start(sums_a, land_a)
+
+    def weight_rows(target, left, right):
+        part = 256
+        shards = max(1, part // height)
+        for index in range(channels // part):
+            value = cross_rows(left[:, pl.ds(index * part, part)], right[...]).astype(low)
+            if shards == 1:
+                target[0, index // 2, index % 2] = value
+            else:
+                some = pl.ds(index * (shards // 2), shards // 2)
+                target[0, some] = value.reshape(shards // 2, 2, height, middle)
+
+    weight_rows(g_last, wide_low, act_two)
+    go_pair(0)
+
+    def settle_grad(source, center, inverse, scale, both):
+        def step(index):
+            span_rows = rows_at(index * tile, tile)
+            normal = source[span_rows, :] * inverse - center
+            back = both[0:1] + normal * both[1:2]
+            back = (back.reshape(tile // 8, 8, middle) * mask).reshape(tile, middle)
+            thin_low[span_rows, :] = ((work[span_rows, :] - back) * scale).astype(low)
+
+        loop(4, step)
+
+    both_two = sums.finish()
+    settle_grad(two, center_two, inverse_two, scale_two, both_two / count_all)
+    vec[pl.ds(0, 1), pl.ds(middle, middle)] = both_two[1:2]
+    vec[pl.ds(0, 1), pl.ds(3 * middle, middle)] = both_two[0:1]
+    go_pair(0)
+
+    loads["mid"].wait()
+    moves, zeros = tap_blocks(images, True)
+    total[...] = jnp.zeros_like(total)
+    for part in range(3):
+        for slot in range(3):
+            cols = pl.ds(slot * middle, middle)
+            for target, start, size in moves[3 * part + slot]:
+                wide_low[pl.ds(target, size), cols] = thin_low[pl.ds(start, size), :]
+            for target, size in zeros[3 * part + slot]:
+                wide_low[pl.ds(target, size), cols] = jnp.zeros((size, middle), low)
+
+        def step_one(index):
+            span_rows = rows_at(index * tile, tile)
+            grad = against(
+                wide_low[span_rows, pl.ds(0, middle)], mid_w[3 * part].reshape(middle, middle)
+            )
+            for slot in range(1, 3):
+                grad = grad + against(
+                    wide_low[span_rows, pl.ds(slot * middle, middle)],
+                    mid_w[3 * part + slot].reshape(middle, middle),
+                )
+            if part:
+                grad = grad + work[span_rows, :]
+            if part == 2:
+                grad = grad * slope_of(one[span_rows, :] * scale_one + shift_one)
+                norm_sums(grad, one[span_rows, :] * inverse_one - center_one)
+            work[span_rows, :] = grad
+
+        loop(4, step_one)
+        if part == 2:
+            pack(sums_b, middle)
+            sums.start(sums_b, land_b)
+        for slot in range(3):
+            value = cross_rows(act_one[...], wide_low[:, pl.ds(slot * middle, middle)]).astype(low)
+            g_mid[3 * part + slot] = value.reshape(g_mid.shape[1:])
+        if part == 0:
+            go_pair(1)
+            go_pair(0)
+        elif part == 1:
+            go_pair(2)
+            go_pair(1)
+            go_pair(0)
+        else:
+            go_pair(3)
+            go_pair(4)
+            go_pair(2)
+            go_pair(1)
+            go_pair(0)
             value = whole_near(0, near_hid)
+            wide = g_hid.shape[3]
             squares_of(3, value)
-            o_hid[:, lanes_of(at.sub, g_hid.shape[3])] = value
-            hid_row = links(hid_slabs[0], hid_slabs[0], at.row_peer)
+            slabs = [o_hid.at[:, lanes_of(which, wide)] for which in (at.sub, at.row_sub)]
+            o_hid[:, lanes_of(at.sub, wide)] = value
+            hid_row = links(slabs[0], slabs[0], at.row_peer)
             value = whole_near(1, near_out)
             squares_of(4, value)
             o_out[...] = value
+
+    both_one = sums.finish()
+    settle_grad(one, center_one, inverse_one, scale_one, both_one / count_all)
+    vec[pl.ds(0, 1), pl.ds(0, middle)] = both_one[1:2]
+    vec[pl.ds(0, 1), pl.ds(2 * middle, middle)] = both_one[0:1]
+    wide = vec.shape[1] // 4
+    vec_cols = lanes_of(at.sub, wide)
+    vec_copies = [
+        links(vec.at[:, vec_cols], vec_land.at[hop], peer)
+        for hop, peer in enumerate(at.dp_peers())
+    ]
+    go_pair(3)
+    hid_row.wait()
+    final = [links(slab, slab, at.core_peer) for slab in slabs]
+
+    weight_rows(g_first, x_ref, thin_low)
+    go_pair(5)
+    go_pair(6)
+
+    numbers = range(len(pieces) // 2)
+    tick = 0
+    sent = False
+    while min(state) < 6:
+        for number in numbers:
+            if state[2 * number] < 6 and tick >= max(0, number - 4):
+                go_pair(number)
+        if tick == 1:
             wait_all(vec_copies)
-            value = g_vec[:, vec_cols]
+            value = vec[:, vec_cols]
             for hop in range(n_dp - 1):
                 value = value + vec_land[hop]
             o_vec[:, vec_cols] = value
@@ -809,47 +1007,47 @@
                 links(o_vec.at[:, vec_cols], o_vec.at[:, vec_cols], peer)
                 for peer in at.sub_peers()
             ]
-        if 0 <= tick - 3 < count:
-            hold[3, tick - 3] = stage_near(tick - 3, hold[2, tick - 3])
-        if tick == 3:
-            hid_row.wait()
-            for slab in hid_slabs:
-                final.append(links(slab, slab, at.core_peer))
-        if 0 <= tick - 4 < count:
-            final += stage_row(tick - 4, hold[3, tick - 4])
-        if tick == count + 2:
+        if not sent and min(state) >= 5:
+            sent = True
             sq_copies = [
                 links(sq_mine.at[0], sq_land.at[hop], peer)
                 for hop, peer in enumerate(at.dp_peers())
             ]
+        tick += 1
     wait_all(sq_copies)
-    total = sq_mine[0]
+    value = sq_mine[0]
     for hop in range(n_dp - 1):
-        total = total + sq_land[hop]
-    sq_mine[1] = total
+        value = value + sq_land[hop]
+    sq_mine[1] = value
     sq_copies = [
         links(sq_mine.at[1], sq_land.at[n_dp - 1 + hop], peer)
         for hop, peer in enumerate(at.sub_peers())
     ]
     wait_all(sq_copies)
     for hop in range(3):
-        total = total + sq_land[n_dp - 1 + hop]
-    o_sq[...] = total
+        value = value + sq_land[n_dp - 1 + hop]
+    o_sq[...] = value
+    for copies in flight:
+        wait_all(copies)
     wait_all(final)
     wait_all(vec_final)
 
 
-def reduce_gradients(n_dp, collective_id, first, mid, last, hid, out, vec):
+def backward_trunk(
+    n_dp, collective_id, images, pooled, slopes, stat, norms, live, lives, extra, hid, out, inputs,
+    one, two, act, last, mid,
+):
     span = n_dp // 2
-    low = jnp.bfloat16
-    rows = first.shape[0] // n_dp
-    mid_rows = mid.shape[1] // n_dp
-    wide, narrow = first.shape[1], out.shape[1]
+    low, full = jnp.bfloat16, jnp.float32
+    rows, channels = inputs.shape
+    middle = one.shape[1]
+    height, mid_height = last.shape[2], mid.shape[3]
+    narrow = out.shape[1]
+    crops = CROPS * images
     some = jax.ShapeDtypeStruct
     bufs = []
-    for index in range(5):
-        taps, height = (3, mid_rows) if 1 <= index <= 3 else (1, rows)
-        block = (height, LANES)
+    for index, piece in enumerate(piece_list(n_dp, height, mid_height, ((0, 0),) * 3)):
+        taps, block = piece[3], (piece[5], LANES)
         bufs.append(pltpu.VMEM((2, taps, span, 2) + block, low))
         if index % 2 == 0:
             bufs.append(pltpu.VMEM((taps, span, 2) + block, low))
@@ -857,49 +1055,83 @@
             bufs.append(pltpu.VMEM((2, taps, span) + block, low))
         bufs.append(pltpu.VMEM((taps, span) + block, low))
         bufs.append(pltpu.VMEM((span - 1, taps) + block, low))
-    copies = 5 * (span + 8) + 2 * (span + 2) + 2 * n_dp + 16
-    results = pl.pallas_call(
-        functools.partial(reduce_kernel, n_dp),
+    copies = 14 * (span + 6) + 2 * (span + 4) + 2 * n_dp + 40
+    vmem, anywhere = pl.BlockSpec(memory_space=pltpu.VMEM), pl.BlockSpec(memory_space=pl.ANY)
+    return pl.pallas_call(
+        functools.partial(backward_kernel, n_dp, images),
         out_shape=(
-            some((1, rows, wide), low),
-            some((TAPS, mid_rows, wide), low),
-            some((1, rows, wide), low),
-            some((rows, 4 * hid.shape[1]), low),
-            some((rows, narrow), low),
-            some(vec.shape, vec.dtype),
-            some((8, LANES), jnp.float32),
+            some((1, height, middle), low),
+            some((TAPS, mid_height, middle), low),
+            some((1, height, middle), low),
+            some((height, 4 * hid.shape[1]), low),
+            some((height, narrow), low),
+            some(extra.shape, full),
+            some((8, LANES), full),
         ),
-        in_specs=[pl.BlockSpec(memory_space=pltpu.VMEM)] * 6,
-        out_specs=(pl.BlockSpec(memory_space=pltpu.VMEM),) * 7,
-        scratch_shapes=bufs
-        + [
-            pltpu.VMEM((span, rows, hid.shape[1]), low),
-            pltpu.VMEM((span, rows, hid.shape[1]), low),
-            pltpu.VMEM((span - 1, rows, hid.shape[1]), low),
-            pltpu.VMEM((span, 2, rows, narrow), low),
-            pltpu.VMEM((span, rows, narrow), low),
-            pltpu.VMEM((span, rows, narrow), low),
-            pltpu.VMEM((span - 1, rows, narrow), low),
-            pltpu.VMEM((n_dp - 1, vec.shape[0], vec.shape[1] // 4), jnp.float32),
-            pltpu.VMEM((2, 8, LANES), jnp.float32),
-            pltpu.VMEM((n_dp + 2, 8, LANES), jnp.float32),
+        in_specs=[vmem] * 9 + [anywhere] * 6,
+        out_specs=(vmem,) * 7,
+        scratch_shapes=[
+            pltpu.VMEM((rows, channels), low),
+            pltpu.VMEM((rows, middle), full),
+            pltpu.VMEM((rows, middle), full),
+            pltpu.VMEM((rows, middle), low),
+            pltpu.VMEM((span, 2, height, middle), low),
+            pltpu.VMEM((TAPS, span, 2, mid_height, middle), low),
+            pltpu.VMEM((rows, middle), low),
+            pltpu.VMEM((rows, channels), low),
+            pltpu.VMEM((rows, middle), full),
+            pltpu.VMEM((rows, middle), low),
+            pltpu.VMEM((1, span, 2, height, middle), low),
+            pltpu.VMEM((TAPS, span, 2, mid_height, middle), low),
+            pltpu.VMEM((1, span, 2, height, middle), low),
+            pltpu.VMEM((2, 8, middle), full),
+            pltpu.VMEM((2, crops, channels), low),
+            pltpu.VMEM((crops, channels), low),
+            pltpu.VMEM((crops, channels), low),
+            pltpu.VMEM((crops, channels), full),
+            pltpu.VMEM((2, middle), full),
+            pltpu.VMEM((3, 2, middle), full),
+            pltpu.VMEM((2, middle), full),
+            pltpu.VMEM((3, 2, middle), full),
+            pltpu.VMEM((2, channels), full),
+            pltpu.VMEM((3, 2, channels), full),
+            pltpu.VMEM((span, height, hid.shape[1]), low),
+            pltpu.VMEM((span, height, hid.shape[1]), low),
+            pltpu.VMEM((span - 1, height, hid.shape[1]), low),
+            pltpu.VMEM((span, 2, height, narrow), low),
+            pltpu.VMEM((span, height, narrow), low),
+            pltpu.VMEM((span, height, narrow), low),
+            pltpu.VMEM((span - 1, height, narrow), low),
+            pltpu.VMEM(extra.shape, full),
+            pltpu.VMEM((n_dp - 1, extra.shape[0], extra.shape[1] // 4), full),
+            pltpu.VMEM((2, 8, LANES), full),
+            pltpu.VMEM((n_dp + 2, 8, LANES), full),
             pltpu.SemaphoreType.DMA((copies,)),
             pltpu.SemaphoreType.DMA((copies,)),
-            pltpu.SemaphoreType.DMA,
-        ],
+            pltpu.SemaphoreType.DMA((7,)),
+        ]
+        + bufs,
         compiler_params=pltpu.CompilerParams(
-            collective_id=collective_id, has_side_effects=True, vmem_limit_bytes=56 * MIB
+            collective_id=collective_id, has_side_effects=True, vmem_limit_bytes=62 * MIB
         ),
-        name="reduce_gradients",
+        name="backward_trunk",
     )(
-        first.reshape(1, span, 2, rows, wide),
-        mid.reshape(TAPS, span, 2, mid_rows, wide),
-        last.reshape(1, span, 2, rows, wide),
-        hid.reshape(span, 2, rows, hid.shape[1]),
-        out.reshape(span // 4, 2, rows, narrow),
-        vec,
-    )
-    return results
+        pooled,
+        slopes,
+        stat,
+        norms,
+        live,
+        lives,
+        extra,
+        hid.reshape(span, 2, height, hid.shape[1]),
+        out.reshape(span // 4, 2, height, narrow),
+        inputs,
+        one,
+        two,
+        act,
+        last,
+        mid,
+    )
 
 
 def row_tile(rows):
@@ -1163,47 +1395,6 @@
         ),
         name="sinkhorn",
     )(queue, centers, turned, partial, live, first)
-
-
-def split_rows(values, images):
-    big = BIG * BIG * NBIG * images
-    wide = values.shape[1]
-    return (
-        values[:big].reshape(BIG, BIG, NBIG * images, wide),
-        values[big:].reshape(SMALL, SMALL, NSMALL * images, wide),
-    )
-
-
-def patches(values, images, flip):
-    parts = []
-    for spatial in split_rows(values, images):
-        extent = spatial.shape[0]
-        padded = jnp.pad(spatial, ((1, 1), (1, 1), (0, 0), (0, 0)))
-        pieces = [
-            padded[row : row + extent, col : col + extent]
-            for row in range(3)
-            for col in range(3)
-        ]
-        if flip:
-            pieces = pieces[::-1]
-        parts.append(jnp.concatenate(pieces, -1).reshape(-1, TAPS * values.shape[1]))
-    return jnp.concatenate(parts, 0)
-
-
-def spread_crops(values, images):
-    wide = values.shape[1]
-    big = jnp.broadcast_to(
-        values[: NBIG * images] / (BIG * BIG), (BIG * BIG, NBIG * images, wide)
-    ).reshape(-1, wide)
-    small = jnp.broadcast_to(
-        values[NBIG * images :] / (SMALL * SMALL), (SMALL * SMALL, NSMALL * images, wide)
-    ).reshape(-1, wide)
-    return jnp.concatenate([big, small], 0)
-
-
-def pool_crops(values, images):
-    big, small = split_rows(values, images)
-    return jnp.concatenate([jnp.mean(big, (0, 1)), jnp.mean(small, (0, 1))], 0)
 
 
 def advance(weight, gradient, moment, average, trust):
@@ -1276,9 +1467,10 @@
         0,
     )
 
+    live_tile = jnp.broadcast_to(image_mask, (images, LANES))
     (
-        inner_low, last_w, hidden_low, out_low, columns, hidden_one, hidden_two, act_two,
-        trunk_stat, pooled_all, lives,
+        inner_low, last_w, hidden_low, out_low, hidden_one, hidden_two, act_two, trunk_stat,
+        pooled_all, lives_tile, slopes,
     ) = forward_trunk(
         n_dp,
         exchange.next_id(),
@@ -1290,24 +1482,11 @@
         proj_out.astype(low),
         inputs,
         norm_params,
-        jnp.broadcast_to(image_mask, (images, LANES)),
-    )
-    last_w = last_w.reshape(channels, middle)
+        live_tile,
+    )
     hidden_low = hidden_low.reshape(channels, share)
-    out_low = lax.dynamic_slice_in_dim(out_low.reshape(hidden_width, out_width), here * share, share, 0)
-    inner_low = inner_low.reshape(TAPS, middle, middle)
-    middle_t = jnp.transpose(inner_low, (0, 2, 1)).reshape(TAPS * middle, middle)
-    lives = lives[:, 0, 0]
-    count_all = jnp.sum(lives) * per_image
-    mean_one, mean_two, mean_three = [trunk_stat[0, bounds[k] : bounds[k + 1]] for k in range(3)]
-    inv_one, inv_two, inv_three = [trunk_stat[1, bounds[k] : bounds[k + 1]] for k in range(3)]
-    normal_one = (hidden_one - mean_one) * inv_one
-    pre_one = gains[0] * normal_one + biases[0]
-    normal_two = (hidden_two - mean_two) * inv_two
-    pre_two = gains[1] * normal_two + biases[1]
-    hidden_three = against(act_two, last_w)
-    normal_three = (hidden_three - mean_three) * inv_three
-    summed = gains[2] * normal_three + biases[2] + inputs.astype(jnp.float32)
+    out_low = out_low.reshape(share, out_width)
+    lives = lives_tile[:, 0, 0]
 
     def stats(total, squares, count):
         mean = total / count
@@ -1351,7 +1530,6 @@
     ).astype(jnp.bfloat16)
     d_hidden = cross_rows(pooled_all, proj_low)
     partial = against(proj_low, hidden_low).astype(jnp.bfloat16).reshape(n_sub, crops, channels)
-    grad_pooled = relay(exchange.next_id(), partial, True, "pooled_grad")
 
     four = exchange(
         jnp.stack([gain_four, bias_four, jnp.broadcast_to(loss_tile[0, 0], (share,))]),
@@ -1361,30 +1539,6 @@
     gain_four, bias_four = four[:, 0].reshape(-1), four[:, 1].reshape(-1)
     loss_group = jnp.sum(four[:, 2, 0])
     centers_sum = lax.psum(grad_centers, ("dp", "sub"))[:proto_count]
-
-    def norm_back(grad_out, normal, inv_std, gain_vec, name):
-        both = jnp.stack([jnp.sum(grad_out, 0), jnp.sum(grad_out * normal, 0)])
-        both = jnp.sum(exchange(both, "sub", name=name), 0)
-        grad_in = (
-            gain_vec * inv_std * (grad_out - row_mask * (both[0] + normal * both[1]) / count_all)
-        )
-        return grad_in.astype(jnp.bfloat16), both[1], both[0]
-
-    grad_summed = spread_crops(grad_pooled, images) * silu_slope(summed)
-    three_low, gain_three, bias_three = norm_back(
-        grad_summed, normal_three, inv_three, gains[2], "back_three"
-    )
-    d_last = cross_rows(three_low, act_two)
-    grad_act_two = forward_dot(three_low, last_w) * silu_slope(pre_two)
-    two_low, gain_two, bias_two = norm_back(
-        grad_act_two, normal_two, inv_two, gains[1], "back_two"
-    )
-    d_middle = cross_rows(columns, two_low)
-    grad_act_one = forward_dot(patches(two_low, images, True), middle_t) * silu_slope(pre_one)
-    one_low, gain_one, bias_one = norm_back(
-        grad_act_one, normal_one, inv_one, gains[0], "back_one"
-    )
-    d_first = cross_rows(inputs, one_low)
 
     scalars = jnp.stack(
         [
@@ -1398,27 +1552,39 @@
         ]
     )
     width = 4 * middle
-    vector = jnp.concatenate(
+    zero = jnp.zeros((1, width), jnp.float32)
+    extra = jnp.concatenate(
         [
-            jnp.concatenate([gain_one, gain_two, bias_one, bias_two]).reshape(1, width),
-            gain_three.reshape(-1, width),
+            zero,
+            zero,
             gain_four.reshape(-1, width),
-            bias_three.reshape(-1, width),
+            zero,
             bias_four.reshape(-1, width),
             jnp.pad(scalars, (0, width - 7))[None],
-            jnp.zeros((2, width), jnp.float32),
+            zero,
+            zero,
         ],
         0,
     )
-    shard_first, shard_inner, shard_last, shard_hidden, shard_out, vector, grad_all = reduce_gradients(
+    shard_first, shard_inner, shard_last, shard_hidden, shard_out, vector, grad_all = backward_trunk(
         n_dp,
         exchange.next_id(),
-        d_first.astype(low),
-        d_middle.astype(low).reshape(TAPS, middle, middle),
-        d_last.astype(low),
+        images,
+        partial,
+        slopes,
+        trunk_stat,
+        norm_params,
+        live_tile,
+        lives_tile,
+        extra,
         d_hidden.astype(low),
         d_out.astype(low),
-        vector,
+        inputs,
+        hidden_one,
+        hidden_two,
+        act_two,
+        last_w,
+        inner_low,
     )
     shard_outer = jnp.concatenate([shard_first, shard_last], 0).astype(jnp.float32)
     shard_inner = shard_inner.astype(jnp.float32)

time: 499 us -> 378 us (0.76)
  matrix products: 67.6 us -> 8.07 us
  local copies, waits for them, and re-layouts: 49.4 us -> 25.1 us
  Pallas kernels: 301 us -> 280 us
  other arithmetic: 58.9 us -> 43.7 us
    dot_general x5 -> x2, matrix products: 28.3 us -> 2.99 us  [cross_rows(): lax.dot_general(left, right, (((0,), (0,)), ((), ())), preferred_element_...]
    pallas_call x1, Pallas kernels: 126 us -> 105 us  [forward_trunk(): pl.pallas_call(functools.partial(forward_kernel, n_dp, images), out_shape...]
    dot_general x3 -> x2, matrix products: 19.3 us -> 2.09 us  [against(): lax.dot_general(left, right, (((1,), (1,)), ((), ())), preferred_element_...]
    dot_general x4 -> x2, matrix products: 20 us -> 2.99 us  [forward_dot(): return jnp.dot(left, right, preferred_element_type=jnp.float32)]
    convert_element_type x2 -> x0, other arithmetic: 12.6 us -> none  [norm_back(): return (grad_in.astype(jnp.bfloat16), both[1], both[0])]
    pallas_call x4 -> x1, Pallas kernels: 15.1 us -> 3.73 us  [__call__(): pl.pallas_call(functools.partial(exchange_kernel, axis, count, scatter),...]
    pallas_call x2 -> x1, Pallas kernels: 124 us -> 136 us  [backward_trunk(): pl.pallas_call(functools.partial(backward_kernel, n_dp, images), out_shap...]
    unnamed x148 -> x70, local copies, waits for them, and re-layouts: 12.3 us -> 4.55 us
  transfers between devices with their start and end apart: 1 -> 1, of which waited for: 0 -> 0; matrix products, arithmetic and copies ran while one was open for 26% -> 11% of each run, Pallas kernels for 28% -> 37%
where the time goes in v5:
time: 378 us; the launch traced here: 374 us
  Pallas kernels  280 us (74%)
  other arithmetic  43.7 us (12%)
  local copies, waits for them, and re-layouts  25.1 us (7%)
  between operations  17.4 us (5%)
  matrix products  8.07 us (2%)
    pallas_call x1, Pallas kernels, backward_trunk(): pl.pallas_call(functools.partial(backward_kernel, n_dp, images), out_shap...  136 us
    pallas_call x1, Pallas kernels, forward_trunk(): pl.pallas_call(functools.partial(forward_kernel, n_dp, images), out_shape...  105 us
    pallas_call x1, Pallas kernels, sinkhorn(): pl.pallas_call(functools.partial(sinkhorn_kernel, 'sub', count, protos),...  29.8 us
    add x6, other arithmetic, advance(): average_new = average_rate * average + (1.0 - average_rate) * weight_new  10.4 us
    convert_element_type x4, other arithmetic, per_device(): new[0].astype(jnp.bfloat16)  10.3 us
  transfers between devices with their start and end apart: 1, of which 0 were waited for; matrix products, arithmetic and copies ran while one was open for 11% of the time, Pallas kernels for 37%

profile of v5, /device:TPU:0, one launch (start us, length us, event | category | flops | bytes accessed | tf_op | source)
XLA Modules:
  0.0 374.2 jit_solution(3807593487619853444)
XLA Ops:
  7.9 5.1 %copy.49 = bf16[7,7,2,8,2048]{4,3,2,1,0:T(8,128)(2,1)} copy(bf16[7,7,2,8,2048]{4,2,1,0,3:T(2,128)(2,1)} %bitcast.76) | data formatting | bytes 6422528 | tf_op jit(solution)/shard_map/transpose | solution.py:1464
  14.3 1.6 multiply_reduce_fusion.5
  18.9 1.8 dynamic-slice_convert_fusion.refs_3_
  20.7 5.1 %pad_maximum_fusion.refs_5_.refs_9_ = bf16[1216,2048]{1,0:T(8,128)(2,1)} fusion(bf16[432,2048]{1,0:T(8,128)(2,1)S(1)} %bitcast.72, bf16[784,2048]{1,0:T(8,128)(2,1)} %bitcast.71), kind=kLoop, calls=%fused_computation | loop fusion | flops 9961472 | bytes 9961472 | tf_op jit(solution)/shard_map/concatenate | solution.py:1462
  26.4 105.4 %forward_trunk.1 = (bf16[9,4,2,64,512]{4,3,2,1,0:T(8,128)(2,1)}, bf16[4,2,256,512]{3,2,1,0:T(8,128)(2,1)}, bf16[4,2,256,512]{3,2,1,0:T(8,128)(2,1)}, bf16[1,2,25...) custom-call(bf16[256,512]{1,0:T(8,128)(2,1)} %get-tuple-element.105., ...), custom_call_target="tpu_custom_call" | custom-call | tf_op jit(solution)/shard_map/forward_trunk/pallas_call | solution.py:548
  131.8 1.4 slice_reduce_fusion.2
  134.1 2.8 multiply_reduce_fusion.6
  137.3 5.4 %column_sums.1 = (bf16[3072,128]{1,0:T(8,128)(2,1)S(1)}, bf16[128,3072]{1,0:T(8,128)(2,1)S(1)}, f32[2,3072]{1,0:T(2,128)S(1)}) custom-call(bf16[2,960,128]{2,1,0:T(8,128)(2,1)S(1)} %copy-done.1, f32[3000,128]{1,0:T(8,128)S(1)} %copy-done), custom_call_target="tpu_custom_call" | custom-call | flops 1509949440 | bytes 491520 | tf_op jit(solution)/shard_map/column_sums/pallas_call | solution.py:1175
  142.8 29.8 %sinkhorn.1 = (bf16[4,64,128]{2,1,0:T(8,128)(2,1)S(1)}, f32[3072,128]{1,0:T(8,128)}, f32[8,128]{1,0:T(8,128)S(1)}) custom-call(bf16[2,960,128]{2,1,0:T(8,128)(2,1)S(1)} %copy-done.1, bf16[3072,128]{1,0:T(8,128)(2,1)S(1)} %get-tuple-element.51.centers_ref, bf16[128,3072]{1,0:T(8,128)(2,1)S(1)} %get-tuple-element.52.turned_ref, ...), custom_call_target="tpu_custom_call" | custom-call | tf_op jit(solution)/shard_map/sinkhorn/pallas_call | solution.py:1372
  173.3 2.8 multiply_reduce_fusion
  178.7 3.7 sums_four.1
  183.3 2.1 convolution_convert_fusion
  185.4 1.7 convolution_convert_fusion.1
  187.1 4.6 %stack.50 = f32[7]{0:T(128)S(1)} concatenate(f32[1]{0:T(128)} %bitcast.23, f32[1]{0:T(128)} %bitcast.24, f32[1]{0:T(128)} %bitcast.25, f32[1]{0:T(128)} %bitcast.26, f32[1]{0:T(128)} %bitcast.27, f32[1]{0:T(128)} %bitcast.28, f32[1]{0:T(128)} %bitcast.29), dimensions={0} | concatenate | bytes 56 | tf_op jit(solution)/shard_map/stack | solution.py:1543
  192.5 135.6 %backward_trunk.1 = (bf16[1,256,512]{2,1,0:T(8,128)(2,1)}, bf16[9,64,512]{2,1,0:T(8,128)(2,1)}, bf16[1,256,512]{2,1,0:T(8,128)(2,1)}, bf16[256,2048]{1,0:T(8,128...) custom-call(bf16[4,64,2048]{2,1,0:T(8,128)(2,1)} %bitcast.73, ...), custom_call_target="tpu_custom_call" | custom-call | tf_op jit(solution)/shard_map/backward_trunk/pallas_call | solution.py:1060
  333.4 2.7 fusion.5
  337.0 2.2 fusion.7
  339.9 3.4 fusion.9
  345.8 1.5 fusion.10
  350.1 3.2 fusion.8
  354.6 1.7 add_multiply_fusion
  356.4 2.4 multiply_reduce_fusion.2
  358.8 2.2 multiply_reduce_fusion.1
  362.4 4.8 %add_multiply_fusion.1 = (f32[3000,128]{1,0:T(8,128)}, f32[3000,128]{1,0:T(8,128)}, f32[3000,128]{1,0:T(8,128)}) fusion(f32[3000,128]{1,0:T(8,128)} %param.43, f32[3000,128]{1,0:T(8,128)S(1)} %copy-done, f32[3000]{0:T(1024)S(1)} %multiply_reduce_fusion.2, f32[3072,128]{1,0:T(8,128)S(1)} %copy-done.2, f32[3000]{0:T(1024)S(1)} %add_rsqrt_fusion, f32[]{:T(128)S(6)} %div.69, ...), kind=kLoop, calls=%fused_computation.8 | loop fusion | flops 4608000 | bytes 10776004 | tf_op jit(solution)/shard_map/add | solution.py:1404
  (120 shorter events, 23.8 us)
Async XLA Ops:
  7.2 349.2 %all-reduce.3.cloned.1.call-start = ((), (), s32[]{:S(2)}) async-start(), calls=%async_computation | async-start | bytes 3145728 | tf_op jit(solution)/shard_map/psum | solution.py:1541
  7.9 5.1 %copy-start.16 = (bf16[8,6,3,3,2048]{4,0,3,2,1:T(8,128)(2,1)S(1)}, bf16[8,6,3,3,2048]{4,0,3,2,1:T(8,128)(2,1)}, u32[]{:S(2)}) copy-start(bf16[8,6,3,3,2048]{4,0,3,2,1:T(8,128)(2,1)} %param.24) | copy-start | bytes 5308420
  14.3 2.5 copy-start.24
  134.0 3.0 copy-start.30
  134.1 3.3 copy-start
  134.1 3.3 copy-start.1
  142.7 29.9 %copy-start.6 = (f32[2,256,512]{2,1,0:T(8,128)S(1)}, f32[2,256,512]{2,1,0:T(8,128)}, u32[]{:S(2)}) copy-start(f32[2,256,512]{2,1,0:T(8,128)} %param.27) | copy-start | bytes 3145732
  173.3 3.7 copy-start.31
  177.4 5.9 %copy-start.12 = (bf16[4,64,2048]{2,1,0:T(8,128)(2,1)S(1)}, bf16[4,64,2048]{2,1,0:T(8,128)(2,1)}, u32[]{:S(2)}) copy-start(bf16[4,64,2048]{2,1,0:T(8,128)(2,1)} %get-tuple-element.48) | copy-start | bytes 3145732
  192.4 137.6 %copy-start.22 = (f32[2,5120]{1,0:T(2,128)S(1)}, f32[2,5120]{1,0:T(2,128)}, u32[]{:S(2)}) copy-start(f32[2,5120]{1,0:T(2,128)} %refs_3_.1) | copy-start | bytes 122884
  192.4 139.0 %copy-start.34 = (f32[5]{0:T(128)S(1)}, f32[5]{0:T(128)}, u32[]{:S(2)}) copy-start(f32[5]{0:T(128)} %constant.22) | copy-start | bytes 64
  192.4 144.5 %copy-start.25 = (f32[256,128]{1,0:T(8,128)S(1)}, f32[256,128]{1,0:T(8,128)}, u32[]{:S(2)}) copy-start(f32[256,128]{1,0:T(8,128)} %param.30) | copy-start | bytes 393220
  192.4 144.5 %copy-start.29 = (f32[256,128]{1,0:T(8,128)S(1)}, f32[256,128]{1,0:T(8,128)}, u32[]{:S(2)}) copy-start(f32[256,128]{1,0:T(8,128)} %param.36) | copy-start | bytes 393220
  328.1 11.1 %copy-start.28 = (f32[256,128]{1,0:T(8,128)S(1)}, f32[256,128]{1,0:T(8,128)}, u32[]{:S(2)}) copy-start(f32[256,128]{1,0:T(8,128)} %param.42) | copy-start | bytes 393220
  328.1 11.8 %copy-start.10 = (f32[9,64,512]{2,1,0:T(8,128)S(1)}, f32[9,64,512]{2,1,0:T(8,128)}, u32[]{:S(2)}) copy-start(f32[9,64,512]{2,1,0:T(8,128)} %param.28) | copy-start | bytes 3538948
  328.1 11.8 %copy-start.18 = (f32[9,64,512]{2,1,0:T(8,128)S(1)}, f32[9,64,512]{2,1,0:T(8,128)}, u32[]{:S(2)}) copy-start(f32[9,64,512]{2,1,0:T(8,128)} %param.34) | copy-start | bytes 3538948
  339.2 4.1 %copy-start.23 = (f32[256,128]{1,0:T(8,128)}, f32[256,128]{1,0:T(8,128)S(1)}, u32[]{:S(2)}) copy-start(f32[256,128]{1,0:T(8,128)S(1)} %get-tuple-element.83) | copy-start | bytes 393220
  339.9 3.4 copy-start.17
  345.8 2.8 copy-start.32
  345.8 2.8 copy-start.33
  345.8 3.6 copy-start.15
  347.3 2.5 copy-start.3
  347.3 2.8 copy-start.21
  350.1 4.5 %copy-start.13 = (f32[256,2048]{1,0:T(8,128)S(1)}, f32[256,2048]{1,0:T(8,128)}, u32[]{:S(2)}) copy-start(f32[256,2048]{1,0:T(8,128)} %param.41) | copy-start | bytes 6291460
  (12 other events, 22.3 us)
Sparse Core Ops, SparseCore 0:
  172.7 145.4 all-reduce.2
